TPU v7x, 32 devices: a whole 2x2x4 slice. The times are simulated.
32 devices in a mesh: dp: 8 (over z, y), tensor: 4 (over x, core).
Axes of the slice: x: 2, y: 2, z: 4, core: 2. Of those that a mesh axis runs over, the one named last changes fastest.
Arguments:
- tokens: bfloat16 [16, 1024, 768], P('dp', 'tensor'), may hold values from -6 to 6
- lengths: int32 [16], P('dp'), may hold values from 256 to 1024, as said below
- times: int32 [16], P('dp'), may hold values from 0 to 999
- cotangent: bfloat16 [16, 1024, 768], P('dp', 'tensor'), may hold values from -6 to 6
- w_qkv: bfloat16 [3, 768, 768], P(None, 'dp', 'tensor'), may hold values from -0.21875 to 0.21875
- w_out: bfloat16 [768, 768], P('tensor', 'dp'), may hold values from -2 to 2
- w_up: bfloat16 [768, 3072], P('dp', 'tensor'), may hold values from -0.21875 to 0.21875
- up_bias: bfloat16 [3072], P('dp'), may hold values from -3 to 3
- w_down: bfloat16 [3072, 768], P('tensor', 'dp'), may hold values from -0.109375 to 0.109375
- down_bias: bfloat16 [768], P('dp'), may hold values from -3 to 3
- norm1_gain: bfloat16 [768], P('dp'), may hold values from 0.5 to 1.5
- norm2_gain: bfloat16 [768], P('dp'), may hold values from 0.5 to 1.5
- ada_weight: bfloat16 [128, 4608], P(None, 'dp'), may hold values from -0.5 to 0.5
- ada_bias: bfloat16 [4608], P('dp'), may hold values from -3 to 3
Outputs:
- out: bfloat16 [16, 1024, 768], P('dp', 'tensor')
- grad_tokens: bfloat16 [16, 1024, 768], P('dp', 'tensor')
- grad_w_qkv: float32 [3, 768, 768], P(None, 'dp', 'tensor')
- grad_w_out: float32 [768, 768], P('tensor', 'dp')
- grad_w_up: float32 [768, 3072], P('dp', 'tensor')
- grad_up_bias: float32 [3072], P('dp')
- grad_w_down: float32 [3072, 768], P('tensor', 'dp')
- grad_down_bias: float32 [768], P('dp')
- grad_norm1_gain: float32 [768], P('dp')
- grad_norm2_gain: float32 [768], P('dp')
- grad_ada_weight: float32 [128, 4608], P(None, 'dp')
- grad_ada_bias: float32 [4608], P('dp')
Inputs may be any that keep to these rules, and one draw needn't show every extreme that they name: A sequence's real tokens fill its first lengths slots; at least one sequence has exactly 1024.
All inputs are finite; a program needn't handle non-finite values.
Results may differ from a plain program's by a relative error of at most 0.015.
The roundings to bfloat16 on the way count: a program that leaves them out, or rounds other values in their place, can miss the bound.
Values may be sent and summed in bfloat16 or wider, within the bound.
No kernel may reach another device: no remote copies, remote signals or barrier semaphores. Data moves between devices by JAX's collectives and lax.ppermute only.
A program may use at most 128 MiB of HBM per device.

v0:
```python
import math

import jax
import jax.numpy as jnp
from jax import lax
from jax.sharding import PartitionSpec as P

HEAD = 64


norm_epsilon = 1e-05
masked_score = -1e30


def time_embedding(time_steps, width_total):
    half_width = width_total // 2
    frequency = jnp.exp(-math.log(10000.0) * jnp.arange(half_width, dtype=jnp.float32) / half_width)
    angles = time_steps.astype(jnp.float32)[:, None] * frequency[None, :]
    return jnp.concatenate([jnp.cos(angles), jnp.sin(angles)], axis=-1)


def rotary_tables(length_total, head_width):
    half_width = head_width // 2
    inverse = jnp.exp(
        -math.log(10000.0) * 2.0 * jnp.arange(half_width, dtype=jnp.float32) / head_width
    )
    angles = jnp.arange(length_total, dtype=jnp.float32)[:, None] * inverse[None, :]
    cosine = jnp.concatenate([jnp.cos(angles), jnp.cos(angles)], axis=-1)
    sine = jnp.concatenate([jnp.sin(angles), jnp.sin(angles)], axis=-1)
    return (cosine, sine)


def rotate(vectors, cosine, sine):
    half_width = vectors.shape[-1] // 2
    turned = jnp.concatenate([-vectors[..., half_width:], vectors[..., :half_width]], axis=-1)
    return vectors * cosine[:, None, :] + turned * sine[:, None, :]


def modulate(token_rows, gain_vec, scale_vec, shift_vec):
    centered = token_rows - jnp.mean(token_rows, axis=-1, keepdims=True)
    variance = jnp.mean(centered * centered, axis=-1, keepdims=True)
    return centered * lax.rsqrt(variance + norm_epsilon) * gain_vec * (1.0 + scale_vec) + shift_vec


def gelu_tanh(values_in):
    return (
        0.5
        * values_in
        * (
            1.0
            + jnp.tanh(
                math.sqrt(2.0 / math.pi)
                * (values_in + 0.044715 * values_in * values_in * values_in)
            )
        )
    )


def block_scores(query_block, key_rows, live_keys, scale_score):
    scores = (
        jnp.einsum("qhd,khd->hqk", query_block, key_rows, preferred_element_type=jnp.float32)
        * scale_score
    )
    return jnp.where(live_keys[None, None, :], scores, masked_score)


def attend_forward(query_rows, key_rows, value_rows, seq_length, block_rows):
    length_total, heads_here, head_width = query_rows.shape
    scale_score = head_width ** (-0.5)
    live_keys = jnp.arange(length_total) < seq_length
    query_blocks = query_rows.reshape(
        length_total // block_rows, block_rows, heads_here, head_width
    )

    def one_block(query_block):
        scores = block_scores(query_block, key_rows, live_keys, scale_score)
        largest = jnp.max(scores, axis=-1, keepdims=True)
        weights_exp = jnp.exp(scores - largest)
        weight_total = jnp.sum(weights_exp, axis=-1, keepdims=True)
        weights_low = (weights_exp / weight_total).astype(jnp.bfloat16)
        mixed_block = jnp.einsum(
            "hqk,khd->qhd", weights_low, value_rows, preferred_element_type=jnp.float32
        )
        return (mixed_block, (largest + jnp.log(weight_total))[:, :, 0])

    mixed_blocks, log_totals = lax.map(one_block, query_blocks)
    return (mixed_blocks.reshape(length_total, heads_here, head_width), log_totals)


def attend_backward(
    query_rows, key_rows, value_rows, grad_mixed, log_totals, seq_length, block_rows
):
    length_total, heads_here, head_width = query_rows.shape
    scale_score = head_width ** (-0.5)
    live_keys = jnp.arange(length_total) < seq_length
    count_blocks = length_total // block_rows
    query_blocks = query_rows.reshape(count_blocks, block_rows, heads_here, head_width)
    grad_blocks = grad_mixed.reshape(count_blocks, block_rows, heads_here, head_width)

    def one_block(carried, block_item):
        grad_keys, grad_values = carried
        query_block, grad_block, log_block = block_item
        scores = block_scores(query_block, key_rows, live_keys, scale_score)
        weights_soft = jnp.exp(scores - log_block[:, :, None])
        weights_low = weights_soft.astype(jnp.bfloat16)
        grad_values = grad_values + jnp.einsum(
            "hqk,qhd->khd", weights_low, grad_block, preferred_element_type=jnp.float32
        )
        grad_weights = jnp.einsum(
            "qhd,khd->hqk", grad_block, value_rows, preferred_element_type=jnp.float32
        )
        inner_sum = jnp.sum(weights_soft * grad_weights, axis=-1, keepdims=True)
        grad_scores = (weights_soft * (grad_weights - inner_sum)).astype(jnp.bfloat16)
        grad_query = scale_score * jnp.einsum(
            "hqk,khd->qhd", grad_scores, key_rows, preferred_element_type=jnp.float32
        )
        grad_keys = grad_keys + scale_score * jnp.einsum(
            "hqk,qhd->khd", grad_scores, query_block, preferred_element_type=jnp.float32
        )
        return ((grad_keys, grad_values), grad_query)

    zeros_start = jnp.zeros((length_total, heads_here, head_width), jnp.float32)
    (grad_keys, grad_values), grad_query = lax.scan(
        one_block, (zeros_start, zeros_start), (query_blocks, grad_blocks, log_totals)
    )
    return (grad_query.reshape(length_total, heads_here, head_width), grad_keys, grad_values)


def shards(
    tokens,
    lengths,
    times,
    cotangent,
    w_qkv,
    w_out,
    w_up,
    up_bias,
    w_down,
    down_bias,
    norm1_gain,
    norm2_gain,
    ada_weight,
    ada_bias,
):
    groups, piece_rows, width_model = tokens.shape
    seq_len = piece_rows * lax.axis_size("tensor")
    tensor_pos = lax.axis_index("tensor")
    gathered = (
        lax.all_gather(w_qkv, "dp", axis=1, tiled=True),
        lax.all_gather(w_out, "dp", axis=1, tiled=True),
        lax.all_gather(w_up, "dp", axis=0, tiled=True),
        lax.all_gather(up_bias, "dp", axis=0, tiled=True),
        lax.all_gather(w_down, "dp", axis=1, tiled=True),
        lax.all_gather(down_bias, "dp", axis=0, tiled=True),
        lax.all_gather(norm1_gain, "dp", axis=0, tiled=True),
        lax.all_gather(norm2_gain, "dp", axis=0, tiled=True),
        lax.all_gather(ada_weight, "dp", axis=1, tiled=True),
        lax.all_gather(ada_bias, "dp", axis=0, tiled=True),
    )
    (
        qkv_all,
        out_all,
        up_all,
        upb_all,
        down_all,
        downb_all,
        gain_first,
        gain_second,
        adaw_all,
        adab_all,
    ) = gathered
    hidden_here = up_all.shape[1]
    width_here = qkv_all.shape[2]
    heads_here = width_here // HEAD
    up_bias_here = lax.dynamic_slice_in_dim(upb_all, tensor_pos * hidden_here, hidden_here).astype(
        jnp.float32
    )
    condition = time_embedding(times, adaw_all.shape[0])
    modulation = jnp.dot(
        condition, adaw_all.astype(jnp.float32), precision=lax.Precision.HIGHEST
    ) + adab_all.astype(jnp.float32)
    shift_one, scale_one, gate_one, shift_two, scale_two, gate_two = [
        modulation[:, None, index * width_model : (index + 1) * width_model] for index in range(6)
    ]
    gain_one = gain_first.astype(jnp.float32)
    gain_two = gain_second.astype(jnp.float32)
    token_rows = tokens.astype(jnp.float32)
    first_in = modulate(token_rows, gain_one, scale_one, shift_one).astype(jnp.bfloat16)
    first_all = lax.all_gather(first_in, "tensor", axis=1, tiled=True)
    projected = jnp.einsum("gld,jde->jgle", first_all, qkv_all, preferred_element_type=jnp.float32)
    cosine, sine = rotary_tables(seq_len, HEAD)
    shape_heads = (groups, seq_len, heads_here, HEAD)
    query_pre = projected[0].reshape(shape_heads)
    query_rows = rotate(query_pre, cosine, sine).astype(jnp.bfloat16)
    key_rows = rotate(projected[1].reshape(shape_heads), cosine, sine).astype(jnp.bfloat16)
    value_rows = projected[2].reshape(shape_heads).astype(jnp.bfloat16)
    block_rows = min(512, seq_len)
    mixed_heads, log_totals = lax.map(
        lambda seq_item: attend_forward(
            seq_item[0], seq_item[1], seq_item[2], seq_item[3], block_rows
        ),
        (query_rows, key_rows, value_rows, lengths),
    )
    mixed_rows = mixed_heads.reshape(groups, seq_len, width_here).astype(jnp.bfloat16)
    attn_terms = jnp.einsum("gle,ed->gld", mixed_rows, out_all, preferred_element_type=jnp.float32)
    attended = lax.psum_scatter(attn_terms, "tensor", scatter_dimension=1, tiled=True)
    after_attn = token_rows + gate_one * attended
    second_in = modulate(after_attn, gain_two, scale_two, shift_two).astype(jnp.bfloat16)
    second_all = lax.all_gather(second_in, "tensor", axis=1, tiled=True)
    hidden_pre = (
        jnp.einsum("gld,df->glf", second_all, up_all, preferred_element_type=jnp.float32)
        + up_bias_here
    )
    active_rows = gelu_tanh(hidden_pre).astype(jnp.bfloat16)
    mlp_terms = jnp.einsum("glf,fd->gld", active_rows, down_all, preferred_element_type=jnp.float32)
    branch_out = lax.psum_scatter(
        mlp_terms.astype(jnp.bfloat16), "tensor", scatter_dimension=1, tiled=True
    ).astype(jnp.float32) + downb_all.astype(jnp.float32)
    result = after_attn + gate_two * branch_out
    positions = tensor_pos * piece_rows + jnp.arange(piece_rows)
    live_rows = (positions[None, :] < lengths[:, None]).astype(jnp.float32)
    grad_y = cotangent.astype(jnp.float32) * live_rows[:, :, None]
    grad_branch = (gate_two * grad_y).astype(jnp.bfloat16)
    grad_gate_two = jnp.sum(grad_y * branch_out, axis=1)
    grad_downb = jnp.sum(grad_branch.astype(jnp.float32), axis=(0, 1))
    qkv_back, out_back, up_back, down_back = (
        lax.all_gather(w_qkv, "dp", axis=1, tiled=True),
        lax.all_gather(w_out, "dp", axis=1, tiled=True),
        lax.all_gather(w_up, "dp", axis=0, tiled=True),
        lax.all_gather(w_down, "dp", axis=1, tiled=True),
    )
    branch_all = lax.all_gather(grad_branch, "tensor", axis=1, tiled=True)
    grad_down_w = jnp.einsum(
        "glf,gld->fd", active_rows, branch_all, preferred_element_type=jnp.float32
    )
    grad_active = jnp.einsum(
        "gld,fd->glf", branch_all, down_back, preferred_element_type=jnp.float32
    )
    _, gelu_pull = jax.vjp(gelu_tanh, hidden_pre)
    grad_hidden = gelu_pull(grad_active)[0].astype(jnp.bfloat16)
    grad_upb_here = jnp.sum(grad_hidden.astype(jnp.float32), axis=(0, 1))
    grad_up_w = jnp.einsum(
        "gld,glf->df", second_all, grad_hidden, preferred_element_type=jnp.float32
    )
    second_terms = jnp.einsum(
        "glf,df->gld", grad_hidden, up_back, preferred_element_type=jnp.float32
    )
    grad_second = lax.psum_scatter(second_terms, "tensor", scatter_dimension=1, tiled=True)
    _, second_pull = jax.vjp(modulate, after_attn, gain_two, scale_two, shift_two)
    grad_after, grad_gain_two, grad_scale_two, grad_shift_two = second_pull(grad_second)
    grad_after = grad_after + grad_y
    grad_attended = (gate_one * grad_after).astype(jnp.bfloat16)
    grad_gate_one = jnp.sum(grad_after * attended, axis=1)
    attended_all = lax.all_gather(grad_attended, "tensor", axis=1, tiled=True)
    grad_out_w = jnp.einsum(
        "gle,gld->ed", mixed_rows, attended_all, preferred_element_type=jnp.float32
    )
    grad_mixed = jnp.einsum(
        "gld,ed->gle", attended_all, out_back, preferred_element_type=jnp.float32
    ).astype(jnp.bfloat16)
    grad_mixed = grad_mixed.reshape(shape_heads)
    grad_query, grad_keys, grad_values = lax.map(
        lambda seq_item: attend_backward(
            seq_item[0], seq_item[1], seq_item[2], seq_item[3], seq_item[4], seq_item[5], block_rows
        ),
        (query_rows, key_rows, value_rows, grad_mixed, log_totals, lengths),
    )
    _, turn_pull = jax.vjp(lambda vectors: rotate(vectors, cosine, sine), query_pre)
    grad_projected = jnp.stack(
        [
            turn_pull(grad_query)[0].reshape(groups, seq_len, width_here),
            turn_pull(grad_keys)[0].reshape(groups, seq_len, width_here),
            grad_values.reshape(groups, seq_len, width_here),
        ]
    ).astype(jnp.bfloat16)
    grad_qkv_w = jnp.einsum(
        "gld,jgle->jde", first_all, grad_projected, preferred_element_type=jnp.float32
    )
    first_terms = jnp.einsum(
        "jgle,jde->gld", grad_projected, qkv_back, preferred_element_type=jnp.float32
    )
    grad_first = lax.psum_scatter(first_terms, "tensor", scatter_dimension=1, tiled=True)
    _, first_pull = jax.vjp(modulate, token_rows, gain_one, scale_one, shift_one)
    grad_input, grad_gain_one, grad_scale_one, grad_shift_one = first_pull(grad_first)
    grad_input = grad_input + grad_after
    grad_modulation = jnp.concatenate(
        [
            grad_shift_one[:, 0],
            grad_scale_one[:, 0],
            grad_gate_one,
            grad_shift_two[:, 0],
            grad_scale_two[:, 0],
            grad_gate_two,
        ],
        axis=-1,
    )
    grad_adaw = jnp.dot(condition.T, grad_modulation, precision=lax.Precision.HIGHEST)
    grad_adab = jnp.sum(grad_modulation, axis=0)
    grad_upb = lax.dynamic_update_slice_in_dim(
        jnp.zeros((upb_all.shape[0],), jnp.float32), grad_upb_here, tensor_pos * hidden_here, 0
    )
    grad_upb, grad_downb, grad_gain_one, grad_gain_two, grad_adaw, grad_adab = lax.psum(
        (grad_upb, grad_downb, grad_gain_one, grad_gain_two, grad_adaw, grad_adab), "tensor"
    )
    summed = (
        lax.psum_scatter(grad_qkv_w, "dp", scatter_dimension=1, tiled=True),
        lax.psum_scatter(grad_out_w, "dp", scatter_dimension=1, tiled=True),
        lax.psum_scatter(grad_up_w, "dp", scatter_dimension=0, tiled=True),
        lax.psum_scatter(grad_upb, "dp", scatter_dimension=0, tiled=True),
        lax.psum_scatter(grad_down_w, "dp", scatter_dimension=1, tiled=True),
        lax.psum_scatter(grad_downb, "dp", scatter_dimension=0, tiled=True),
        lax.psum_scatter(grad_gain_one, "dp", scatter_dimension=0, tiled=True),
        lax.psum_scatter(grad_gain_two, "dp", scatter_dimension=0, tiled=True),
        lax.psum_scatter(grad_adaw, "dp", scatter_dimension=1, tiled=True),
        lax.psum_scatter(grad_adab, "dp", scatter_dimension=0, tiled=True),
    )
    (
        sum_qkv,
        sum_out,
        sum_up,
        sum_upb,
        sum_down,
        sum_downb,
        sum_gain_one,
        sum_gain_two,
        sum_adaw,
        sum_adab,
    ) = summed
    return (
        result.astype(jnp.bfloat16),
        grad_input.astype(jnp.bfloat16),
        sum_qkv,
        sum_out,
        sum_up,
        sum_upb,
        sum_down,
        sum_downb,
        sum_gain_one,
        sum_gain_two,
        sum_adaw,
        sum_adab,
    )


def solution(mesh):
    in_specs = (
        P("dp", "tensor", None),
        P("dp"),
        P("dp"),
        P("dp", "tensor", None),
        P(None, "dp", "tensor"),
        P("tensor", "dp"),
        P("dp", "tensor"),
        P("dp"),
        P("tensor", "dp"),
        P("dp"),
        P("dp"),
        P("dp"),
        P(None, "dp"),
        P("dp"),
    )
    out_specs = (
        P("dp", "tensor", None),
        P("dp", "tensor", None),
        P(None, "dp", "tensor"),
        P("tensor", "dp"),
        P("dp", "tensor"),
        P("dp"),
        P("tensor", "dp"),
        P("dp"),
        P("dp"),
        P("dp"),
        P(None, "dp"),
        P("dp"),
    )
    return jax.shard_map(shards, mesh=mesh, in_specs=in_specs, out_specs=out_specs, check_vma=False)
```

profile of v0, /device:TPU:0, one launch (start us, length us, event | category | flops | bytes accessed | tf_op | source)
XLA Modules:
  0.0 1072.2 jit_solution(3928920567224456242)
XLA Ops:
  14.6 39.8 %all-reduce.15 = (bf16[4608]{0:T(1024)(128)(2,1)S(1)}, bf16[768]{0:T(1024)(128)(2,1)S(1)}, bf16[768]{0:T(1024)(128)(2,1)}, bf16[768]{0:T(1024)(128)(2,1)}) all-reduce(bf16[4608]{0:T(1024)(128)(2,1)S(1)} %dynamic-update-slice, bf16[768]{0:T(1024)(128)(2,1)S(1)} %dynamic-update-slice.1, ...), channel_id=1, replica_groups=mesh['dp'=8,'tensor'=4] {'dp'}, use_global_device_ids=true, to_apply=%add.4 | all-reduce | flops 6912 | bytes 27648
  56.9 2.3 convolution_add_fusion
  64.0 34.5 %all_gather.50 = bf16[3,768,192]{2,0,1:T(4,128)(2,1)S(1)} all-gather(bf16[3,96,192]{2,0,1:T(4,128)(2,1)S(1)} %copy.83), channel_id=1, replica_groups=mesh['dp'=8,'tensor'=4] {'dp'}, dimensions={1}, use_global_device_ids=true | all-gather | bytes 995328 | tf_op jit(solution)/shard_map/all_gather | solution.py:149
  100.7 33.5 %all_gather.51 = bf16[192,768]{0,1:T(8,128)(2,1)} all-gather(bf16[192,96]{0,1:T(8,128)(2,1)S(1)} %copy.86), channel_id=1, replica_groups=mesh['dp'=8,'tensor'=4] {'dp'}, dimensions={1}, use_global_device_ids=true | all-gather | bytes 331776 | tf_op jit(solution)/shard_map/all_gather | solution.py:150
  134.2 3.9 fusion.59
  141.2 31.1 %while.61 = (s32[]{:T(128)}, bf16[2,1024,3,64]{1,3,2,0:T(8,128)(2,1)}, f32[2,2,3,512]{3,2,1,0:T(4,128)}, bf16[2,1024,3,64]{1,3,2,0:T(8,128)(2,1)S(1)}, bf16[2,10...) while((s32[]{:T(128)}, ...), condition=%wide.region_7.8_spmd.clone, body=%wide.region_2.7_spmd.sunk.clone | while | flops 421527040 | bytes 26634548 | solution.py:198
  143.2 10.8 %while.60 = (s32[]{:T(128)}, bf16[2,512,3,64]{1,3,2,0:T(8,128)(2,1)S(1)}, f32[2,3,512]{2,1,0:T(4,128)S(1)}, bf16[2,512,3,64]{1,3,2,0:T(8,128)(2,1)S(1)}, bf16[10...) while((s32[]{:T(128)}, ...), condition=%wide.region_6.6_spmd.clone, body=%wide.region_3.5_spmd.clone.sunk | while | flops 421527040 | bytes 20314220 | solution.py:86
  158.7 10.8 %while.60 = (s32[]{:T(128)}, bf16[2,512,3,64]{1,3,2,0:T(8,128)(2,1)S(1)}, f32[2,3,512]{2,1,0:T(4,128)S(1)}, bf16[2,512,3,64]{1,3,2,0:T(8,128)(2,1)S(1)}, bf16[10...) while((s32[]{:T(128)}, ...), condition=%wide.region_6.6_spmd.clone, body=%wide.region_3.5_spmd.clone.sunk | while | flops 421527040 | bytes 20314220 | solution.py:86
  172.2 5.3 fusion.90
  178.2 56.9 %reduce-scatter.14.cloned.1.call-done = f32[2,256,768]{2,1,0:T(8,128)} async-done(((f32[2,1024,768]{2,1,0:T(8,128)}), f32[2,256,768]{2,1,0:T(8,128)}) %reduce-scatter.14.cloned.1.call-update) | async-done | bytes 1572880 | tf_op jit(solution)/shard_map/reduce_scatter | solution.py:206
  241.4 26.4 %all-gather = bf16[8,1,384]{2,1,0:T(2,128)(2,1)S(1)} all-gather(bf16[1,1,384]{2,1,0:T(2,128)(2,1)S(1)} %reshape.200), channel_id=1, replica_groups=mesh['dp'=8,'tensor'=4] {'dp'}, dimensions={0}, use_global_device_ids=true | all-gather | bytes 6912 | tf_op jit(solution)/shard_map/all_gather | solution.py:152
  267.9 10.6 all-gather.15.cloned.1.call-done
  278.5 28.8 %all-gather.13.cloned.1.call-done = bf16[2,1024,768]{2,1,0:T(8,128)(2,1)} async-done(((bf16[2,256,768]{2,1,0:T(8,128)(2,1)}), bf16[2,1024,768]{2,1,0:T(8,128)(2,1)}) %all-gather.13.cloned.1.call-update) | async-done | bytes 3145744 | tf_op jit(solution)/shard_map/all_gather | solution.py:209
  307.3 7.5 fusion.84
  314.9 35.8 %all-gather.17.cloned.1.call-done = bf16[768,768]{0,1:T(8,128)(2,1)} async-done(((bf16[768,96]{0,1:T(8,128)(2,1)}), bf16[768,768]{0,1:T(8,128)(2,1)}) %all-gather.17.cloned.1.call-update) | async-done | bytes 1179664 | tf_op jit(solution)/shard_map/all_gather | solution.py:153
  350.7 29.5 %all-gather.19.cloned.1.call-done = bf16[2,1024,768]{2,1,0:T(8,128)(2,1)} async-done(((bf16[2,256,768]{2,1,0:T(8,128)(2,1)}), bf16[2,1024,768]{2,1,0:T(8,128)(2,1)}) %all-gather.19.cloned.1.call-update) | async-done | bytes 3145744 | tf_op jit(solution)/shard_map/all_gather | solution.py:232
  380.3 10.4 convert_reduce_fusion
  392.4 4.6 fusion.82
  397.1 9.1 convolution_convert_fusion
  406.8 48.7 %reduce-scatter.18.cloned.1.call-done = f32[2,256,768]{2,1,0:T(8,128)} async-done(((f32[2,1024,768]{2,1,0:T(8,128)}), f32[2,256,768]{2,1,0:T(8,128)}) %reduce-scatter.18.cloned.1.call-update) | async-done | bytes 1572880 | tf_op jit(solution)/shard_map/reduce_scatter | solution.py:248
  455.5 2.9 multiply_reduce_fusion.4
  458.4 37.7 %reduce-scatter.16.cloned.1.call-done = bf16[2,256,768]{2,1,0:T(8,128)(2,1)} async-done(((bf16[2,1024,768]{2,1,0:T(8,128)(2,1)}), bf16[2,256,768]{2,1,0:T(8,128)(2,1)}) %reduce-scatter.16.cloned.1.call-update) | async-done | bytes 786448 | tf_op jit(solution)/shard_map/reduce_scatter | solution.py:216
  496.0 3.3 fusion.99
  502.0 28.4 %all-gather.21.cloned.1.call-done = bf16[2,1024,768]{2,1,0:T(8,128)(2,1)} async-done(((bf16[2,256,768]{2,1,0:T(8,128)(2,1)}), bf16[2,1024,768]{2,1,0:T(8,128)(2,1)}) %all-gather.21.cloned.1.call-update) | async-done | bytes 3145744 | tf_op jit(solution)/shard_map/all_gather | solution.py:254
  530.4 4.0 convolution_convert_fusion.1
  535.8 66.1 %while.63 = (s32[]{:T(128)}, f32[2,1024,3,64]{1,3,2,0:T(8,128)}, f32[2,1024,3,64]{1,3,2,0:T(8,128)}, bf16[2,1024,3,64]{1,3,2,0:T(8,128)(2,1)}, bf16[2,1024,3,64]...) while((s32[]{:T(128)}, f32[2,1024,3,64]{1,3,2,0:T(8,128)}, ...), condition=%wide.region_19.20_spmd.clone, body=%wide.region_15.19_spmd.sunk.clone | while | flops 1031306752 | bytes 85797472 | solution.py:262
  541.0 19.4 %while.62 = (s32[]{:T(128)}, f32[1024,3,64]{0,2,1:T(8,128)S(1)}, f32[1024,3,64]{0,2,1:T(8,128)S(1)}, f32[2,512,3,64]{1,3,2,0:T(8,128)}, bf16[2,512,3,64]{1,3,2,0...) while((s32[]{:T(128)}, f32[1024,3,64]{0,2,1:T(8,128)S(1)}, ...), condition=%wide.region_18.18_spmd.clone, body=%wide.region_16.17_spmd.clone.sunk | while | flops 1031306752 | bytes 52742304 | solution.py:123
  564.6 2.2 constant_dynamic-update-slice_fusion.13
  574.1 19.4 %while.62 = (s32[]{:T(128)}, f32[1024,3,64]{0,2,1:T(8,128)S(1)}, f32[1024,3,64]{0,2,1:T(8,128)S(1)}, f32[2,512,3,64]{1,3,2,0:T(8,128)}, bf16[2,512,3,64]{1,3,2,0...) while((s32[]{:T(128)}, f32[1024,3,64]{0,2,1:T(8,128)S(1)}, ...), condition=%wide.region_18.18_spmd.clone, body=%wide.region_16.17_spmd.clone.sunk | while | flops 1031306752 | bytes 52742304 | solution.py:123
  597.7 2.3 constant_dynamic-update-slice_fusion.13
  601.9 2.2 broadcast_multiply_fusion.1
  608.2 4.7 convolution_bitcast_fusion
  613.4 58.0 %reduce-scatter.20.cloned.1.call-done = f32[2,256,768]{2,1,0:T(8,128)} async-done(((f32[2,1024,768]{2,1,0:T(8,128)}), f32[2,256,768]{2,1,0:T(8,128)}) %reduce-scatter.20.cloned.1.call-update) | async-done | bytes 1572880 | tf_op jit(solution)/shard_map/reduce_scatter | solution.py:282
  677.3 5.3 fusion.98
  683.8 4.1 convolution_bitcast_fusion.3
  688.0 5.1 fusion.76
  693.1 3.0 copy.105
  696.0 2.9 reshape.222
  699.6 8.7 convolution_bitcast_fusion.1
  708.4 6.0 convolution_bitcast_fusion.2
  714.5 37.6 %reduce-scatter.26.cloned.1.call-done = f32[128,576]{0,1:T(8,128)} async-done(((f32[128,4608]{0,1:T(8,128)}), f32[128,576]{0,1:T(8,128)}) %reduce-scatter.26.cloned.1.call-update) | async-done | bytes 294928 | tf_op jit(solution)/shard_map/reduce_scatter | solution.py:314
  754.3 62.5 %reduce-scatter.30.cloned.1.call-done = f32[96,192]{1,0:T(8,128)} async-done(((f32[768,192]{1,0:T(8,128)}), f32[96,192]{1,0:T(8,128)}) %reduce-scatter.30.cloned.1.call-update) | async-done | bytes 73744
  818.5 67.9 %reduce-scatter.28.cloned.1.call-done = f32[96,576]{1,0:T(8,128)} async-done(((f32[768,576]{1,0:T(8,128)}), f32[96,576]{1,0:T(8,128)}) %reduce-scatter.28.cloned.1.call-update) | async-done | bytes 221200
  888.4 35.6 %all-reduce.13 = (f32[3072]{0:T(1024)S(1)}, f32[768]{0:T(1024)S(1)}, f32[768]{0:T(1024)S(1)}, f32[768]{0:T(1024)S(1)}, f32[4608]{0:T(1024)S(1)}) all-reduce(f32[3072]{0:T(1024)S(1)} %dynamic_update_slice.31, f32[768]{0:T(1024)S(1)} %copy-done.57, f32[768]{0:T(1024)S(1)} %get-tuple-element.403, ...), channel_id=9, replica_groups=mesh['dp'=8,'tensor'=4] {'dp'}, use_global_device_ids=true, to_apply=%region_28.29.clone | all-reduce | flops 9984 | bytes 79872
  924.4 6.3 all-reduce.14
  930.7 27.7 %reduce-scatter.24.cloned.1.call-done = f32[768,96]{0,1:T(8,128)} async-done(((f32[768,768]{0,1:T(8,128)}), f32[768,96]{0,1:T(8,128)}) %reduce-scatter.24.cloned.1.call-update) | async-done | bytes 294928 | tf_op jit(solution)/shard_map/reduce_scatter | solution.py:310
  958.4 72.0 %reduce-scatter.22.cloned.1.call-done = f32[96,768]{1,0:T(8,128)} async-done(((f32[768,768]{1,0:T(8,128)}), f32[96,768]{1,0:T(8,128)}) %reduce-scatter.22.cloned.1.call-update) | async-done | bytes 294928 | tf_op jit(solution)/shard_map/reduce_scatter | solution.py:308
  1030.4 33.4 %all-reduce.18.cloned.1.call-done = f32[128,576]{0,1:T(8,128)} async-done(((f32[128,576]{0,1:T(8,128)}), f32[128,576]{0,1:T(8,128)}) %all-reduce.18.cloned.1.call-update) | async-done | bytes 294928 | tf_op jit(solution)/shard_map/psum | solution.py:302
  (378 shorter events, 141.9 us)
Async XLA Ops:
  7.2 48.6 %copy-start = (bf16[2,256,768]{2,1,0:T(8,128)(2,1)S(1)}, bf16[2,256,768]{2,1,0:T(8,128)(2,1)}, u32[]{:S(2)}) copy-start(bf16[2,256,768]{2,1,0:T(8,128)(2,1)} %param.22) | copy-start | bytes 2359300
  7.2 49.2 %all-gather.9.cloned.1.call-start = ((), (), s32[]{:S(2)}) async-start(), calls=%async_computation.9 | async-start | bytes 1327104 | tf_op jit(solution)/shard_map/all_gather | solution.py:157
  7.9 126.3 %all-gather.11.cloned.1.call-start = ((), (), s32[]{:S(2)}) async-start(), calls=%async_computation.10 | async-start | bytes 3932160 | tf_op jit(solution)/shard_map/all_gather | solution.py:189
  54.5 7.3 copy-start.36
  55.8 5.9 copy-start.39
  56.4 5.4 copy-start.48
  56.9 5.0 copy-start.43
  61.8 173.3 %reduce-scatter.14.cloned.1.call-start = ((), (), s32[]{:S(2)}) async-start(), calls=%async_computation.11 | async-start | bytes 7864320 | tf_op jit(solution)/shard_map/reduce_scatter | solution.py:206
  100.7 39.1 %copy-start.25 = (f32[1024,64]{0,1:T(8,128)}, f32[1024,64]{0,1:T(8,128)S(1)}, u32[]{:S(2)}) copy-start(f32[1024,64]{0,1:T(8,128)S(1)} %get-tuple-element.540) | copy-start | bytes 786436
  172.2 5.3 copy-start.5
  177.5 57.6 %copy-start.1 = (bf16[2,256,768]{2,1,0:T(8,128)(2,1)S(1)}, bf16[2,256,768]{2,1,0:T(8,128)(2,1)}, u32[]{:S(2)}) copy-start(bf16[2,256,768]{2,1,0:T(8,128)(2,1)} %param.22) | copy-start | bytes 2359300
  177.5 57.6 %copy-start.42 = (f32[2,768]{1,0:T(2,128)S(1)}, f32[2,768]{1,0:T(2,128)}, u32[]{:S(2)}) copy-start(f32[2,768]{1,0:T(2,128)} %get-tuple-element.531) | copy-start | bytes 18436
  177.5 101.0 %all-gather.15.cloned.1.call-start = ((), (), s32[]{:S(2)}) async-start(), calls=%async_computation.13 | async-start | bytes 1327104 | tf_op jit(solution)/shard_map/all_gather | solution.py:151
  178.1 129.2 %all-gather.13.cloned.1.call-start = ((), (), s32[]{:S(2)}) async-start(), calls=%async_computation.12 | async-start | bytes 3932160 | tf_op jit(solution)/shard_map/all_gather | solution.py:209
  238.8 111.9 %all-gather.17.cloned.1.call-start = ((), (), s32[]{:S(2)}) async-start(), calls=%async_computation.14 | async-start | bytes 1327104 | tf_op jit(solution)/shard_map/all_gather | solution.py:153
  239.4 140.8 %all-gather.19.cloned.1.call-start = ((), (), s32[]{:S(2)}) async-start(), calls=%async_computation.16 | async-start | bytes 3932160 | tf_op jit(solution)/shard_map/all_gather | solution.py:232
  239.5 259.8 %copy-start.46 = (f32[2,256]{1,0:T(2,128)}, f32[2,256]{1,0:T(2,128)S(1)}, u32[]{:S(2)}) copy-start(f32[2,256]{1,0:T(2,128)S(1)} %compare_convert_fusion) | copy-start | bytes 6148
  241.3 214.2 %reduce-scatter.18.cloned.1.call-start = ((), (), s32[]{:S(2)}) async-start(), calls=%async_computation.17 | async-start | bytes 7864320 | tf_op jit(solution)/shard_map/reduce_scatter | solution.py:248
  267.9 129.1 %copy-start.64 = (f32[768]{0:T(1024)}, f32[768]{0:T(1024)S(1)}, u32[]{:S(2)}) copy-start(f32[768]{0:T(1024)S(1)} %dynamic-slice_convert_fusion) | copy-start | bytes 9220
  380.3 12.1 %copy-start.71 = (bf16[768,768]{1,0:T(8,128)(2,1)S(1)}, bf16[768,768]{1,0:T(8,128)(2,1)}, u32[]{:S(2)}) copy-start(bf16[768,768]{1,0:T(8,128)(2,1)} %all-gather.15.cloned.1.call-done) | copy-start | bytes 3538948
  397.0 99.0 %reduce-scatter.16.cloned.1.call-start = ((), (), s32[]{:S(2)}) async-start(), calls=%async_computation.15 | async-start | bytes 3932160 | tf_op jit(solution)/shard_map/reduce_scatter | solution.py:216
  406.2 124.3 %all-gather.21.cloned.1.call-start = ((), (), s32[]{:S(2)}) async-start(), calls=%async_computation.18 | async-start | bytes 3932160 | tf_op jit(solution)/shard_map/all_gather | solution.py:254
  406.8 89.3 %copy-start.44 = (f32[768]{0:T(1024)}, f32[768]{0:T(1024)S(1)}, u32[]{:S(2)}) copy-start(f32[768]{0:T(1024)S(1)} %convert_element_type.113) | copy-start | bytes 9220
  500.5 30.0 %copy-start.19 = (bf16[192,768]{0,1:T(8,128)(2,1)S(1)}, bf16[192,768]{0,1:T(8,128)(2,1)}, u32[]{:S(2)}) copy-start(bf16[192,768]{0,1:T(8,128)(2,1)} %all_gather.51) | copy-start | bytes 884740
  501.7 169.7 %reduce-scatter.20.cloned.1.call-start = ((), (), s32[]{:S(2)}) async-start(), calls=%async_computation.19 | async-start | bytes 7864320 | tf_op jit(solution)/shard_map/reduce_scatter | solution.py:282
  535.8 66.1 %copy-start.28 = (f32[1024,64]{0,1:T(8,128)S(1)}, f32[1024,64]{0,1:T(8,128)}, u32[]{:S(2)}) copy-start(f32[1024,64]{0,1:T(8,128)} %get-tuple-element.541) | copy-start | bytes 786436
  535.8 3.7 copy-start.3
  568.8 3.8 copy-start.3
  612.9 58.5 %copy-start.2 = (bf16[2,256,768]{2,1,0:T(8,128)(2,1)S(1)}, bf16[2,256,768]{2,1,0:T(8,128)(2,1)}, u32[]{:S(2)}) copy-start(bf16[2,256,768]{2,1,0:T(8,128)(2,1)} %param.22) | copy-start | bytes 2359300
  612.9 58.5 %copy-start.34 = (f32[2,768]{1,0:T(2,128)S(1)}, f32[2,768]{1,0:T(2,128)}, u32[]{:S(2)}) copy-start(f32[2,768]{1,0:T(2,128)} %copy-done.33) | copy-start | bytes 18436
  612.9 58.6 %copy-start.37 = (f32[768]{0:T(1024)S(1)}, f32[768]{0:T(1024)}, u32[]{:S(2)}) copy-start(f32[768]{0:T(1024)} %copy-done.36) | copy-start | bytes 9220
  612.9 58.6 %copy-start.40 = (f32[2,256]{1,0:T(2,128)S(1)}, f32[2,256]{1,0:T(2,128)}, u32[]{:S(2)}) copy-start(f32[2,256]{1,0:T(2,128)} %copy-done.39) | copy-start | bytes 6148
  612.9 61.8 %copy-start.17 = (f32[2,256,768]{2,1,0:T(8,128)S(1)}, f32[2,256,768]{2,1,0:T(8,128)}, u32[]{:S(2)}) copy-start(f32[2,256,768]{2,1,0:T(8,128)} %reduce-scatter.14.cloned.1.call-done) | copy-start | bytes 4718596
  612.9 60.5 %copy-start.54 = (f32[2,256]{1,0:T(2,128)S(1)}, f32[2,256]{1,0:T(2,128)}, u32[]{:S(2)}) copy-start(f32[2,256]{1,0:T(2,128)} %copy-done.53) | copy-start | bytes 6148
  612.9 60.6 %copy-start.49 = (f32[2,256]{1,0:T(2,128)S(1)}, f32[2,256]{1,0:T(2,128)}, u32[]{:S(2)}) copy-start(f32[2,256]{1,0:T(2,128)} %copy-done.48) | copy-start | bytes 6148
  613.0 139.1 %reduce-scatter.26.cloned.1.call-start = ((), (), s32[]{:S(2)}) async-start(), calls=%async_computation.22 | async-start | bytes 2654208 | tf_op jit(solution)/shard_map/reduce_scatter | solution.py:314
  671.5 3.3 copy-start.24
  682.7 5.3 copy-start.30
  682.7 5.3 copy-start.32
  682.7 134.1 %reduce-scatter.30.cloned.1.call-start = ((), (), s32[]{:S(2)}) async-start(), calls=%async_computation.25 | async-start | bytes 884736
  687.9 198.5 %reduce-scatter.28.cloned.1.call-start = ((), (), s32[]{:S(2)}) async-start(), calls=%async_computation.24 | async-start | bytes 2211840
  698.9 259.5 %reduce-scatter.24.cloned.1.call-start = ((), (), s32[]{:S(2)}) async-start(), calls=%async_computation.21 | async-start | bytes 2654208 | tf_op jit(solution)/shard_map/reduce_scatter | solution.py:310
  699.6 8.8 copy-start.70
  708.3 322.1 %reduce-scatter.22.cloned.1.call-start = ((), (), s32[]{:S(2)}) async-start(), calls=%async_computation.20 | async-start | bytes 2654208 | tf_op jit(solution)/shard_map/reduce_scatter | solution.py:308
  714.4 39.6 %copy-start.63 = (f32[768]{0:T(1024)S(1)}, f32[768]{0:T(1024)}, u32[]{:S(2)}) copy-start(f32[768]{0:T(1024)} %get-tuple-element.538) | copy-start | bytes 9220
  714.4 174.0 %copy-start.57 = (f32[768]{0:T(1024)S(1)}, f32[768]{0:T(1024)}, u32[]{:S(2)}) copy-start(f32[768]{0:T(1024)} %get-tuple-element.492) | copy-start | bytes 9220
  714.4 174.0 %copy-start.58 = (f32[768]{0:T(1024)S(1)}, f32[768]{0:T(1024)}, u32[]{:S(2)}) copy-start(f32[768]{0:T(1024)} %get-tuple-element.400) | copy-start | bytes 9220
  714.4 349.4 %all-reduce.18.cloned.1.call-start = ((), (), s32[]{:S(2)}) async-start(), calls=%async_computation.23 | async-start | bytes 589824 | tf_op jit(solution)/shard_map/psum | solution.py:302
  (48 other events, 71.7 us)
Sparse Core Ops, SparseCore 0:
  10.2 43.9 all-gather.8
  61.9 25.8 all-gather.10
  177.6 57.4 reduce-scatter.13
  237.4 41.0 all-gather.14
  280.0 27.2 all-gather.12
  309.6 41.0 all-gather.16
  352.9 27.2 all-gather.18
  397.1 58.3 reduce-scatter.17
  458.0 37.9 reduce-scatter.15
  501.8 28.5 all-gather.20
  613.1 58.3 reduce-scatter.19
  682.8 69.1 reduce-scatter.25
  755.3 61.4 reduce-scatter.29
  820.6 65.7 reduce-scatter.27
  890.3 68.0 reduce-scatter.23
  962.3 67.9 reduce-scatter.21
  1032.5 31.1 all-reduce.17
where the time goes:
time: 1080 us; the launch traced here: 1070 us
  waiting for transfers between devices  638 us (59%)
  blocking collectives  176 us (16%)
  matrix products  123 us (11%)
  local copies, waits for them, and re-layouts  68.6 us (6%)
  other arithmetic  46.9 us (4%)
  between operations  18.1 us (2%)
    unnamed x19, waiting for transfers between devices  132 us
    unnamed x2, blocking collectives  75.5 us
    reduce_scatter x1, waiting for transfers between devices, shards(): lax.psum_scatter(grad_up_w, 'dp', scatter_dimension=0, tiled=True)  72 us
    reduce_scatter x1, waiting for transfers between devices, shards(): lax.psum_scatter(first_terms, 'tensor', scatter_dimension=1, tiled=True)  58 us
    reduce_scatter x1, waiting for transfers between devices, shards(): lax.psum_scatter(attn_terms, 'tensor', scatter_dimension=1, tiled=True)  56.9 us
    reduce_scatter x1, waiting for transfers between devices, shards(): lax.psum_scatter(second_terms, 'tensor', scatter_dimension=1, tiled=True)  48.7 us
    reduce_scatter x1, waiting for transfers between devices, shards(): lax.psum_scatter(mlp_terms.astype(jnp.bfloat16), 'tensor', scatter_dimens...  37.7 us
    reduce_scatter x1, waiting for transfers between devices, shards(): lax.psum_scatter(grad_adaw, 'dp', scatter_dimension=1, tiled=True)  37.6 us
  transfers between devices with their start and end apart: 17, of which 15 were waited for; matrix products, arithmetic and copies ran while one was open for 6% of the time, Pallas kernels for 0%

commit v1 on v0

v1 whole, which is shorter than its diff:
```python
import functools
import math

import jax
import jax.numpy as jnp
import numpy as np
from jax import lax
from jax.experimental import pallas as pl
from jax.experimental.pallas import tpu as pltpu
from jax.sharding import PartitionSpec as P

HEAD = 64
EPS = 1e-05
MASKED = -1e30
BF = jnp.bfloat16
F32 = jnp.float32
VMEM_MAX = 60 * 1024 * 1024
NBLK = 8
NT = (((1,), (1,)), ((), ()))


def spec(block, index_map):
    return pl.BlockSpec(block, index_map)


def whole(shape):
    return pl.BlockSpec(shape, lambda *_: (0,) * len(shape))


ANY = pl.BlockSpec(memory_space=pl.ANY)


def params():
    return pltpu.CompilerParams(vmem_limit_bytes=VMEM_MAX)


def cost(flops, moved, trans=0):
    return pl.CostEstimate(flops=flops, bytes_accessed=moved, transcendentals=trans)


def norm_rows(rows):
    centered = rows - jnp.mean(rows, axis=1, keepdims=True)
    variance = jnp.mean(centered * centered, axis=1, keepdims=True)
    inverse = lax.rsqrt(variance + EPS)
    return centered * inverse, inverse


def qkv_kernel(tab, tok, mod, gain, cos, sin, w0, w1, first, q, k, v, kt, vt, w, sem):
    heads, block = q.shape[1], q.shape[2]
    step = pl.program_id(0) * pl.num_programs(1) + pl.program_id(1)
    rows = w0.shape[2]

    @pl.when(step == 0)
    def _():
        copies = []
        for p, ref in enumerate((w0, w1)):
            for j in range(4):
                row = pl.multiple_of(tab[p * 4 + j] * rows, 16)
                copies.append(
                    pltpu.make_async_copy(
                        ref.at[j], w.at[:, pl.ds(row, rows), :], sem.at[p * 4 + j]
                    )
                )
        for copy in copies:
            copy.start()
        for copy in copies:
            copy.wait()

    normed, _ = norm_rows(tok[0].astype(F32))
    factor = gain[...] * (1.0 + mod[0, 1:2, :])
    x = (normed * factor + mod[0, 0:1, :]).astype(BF)
    first[0] = x
    wide = w.shape[2]
    low = lax.rem(lax.broadcasted_iota(jnp.int32, (block, wide), 1), HEAD) < HEAD // 2

    def rotate(vec):
        turned = jnp.where(
            low, pltpu.roll(vec, wide - HEAD // 2, 1), pltpu.roll(vec, HEAD // 2, 1)
        )
        return vec * cos[...] + turned * sin[...]

    def store_heads(ref, vec):
        for h in range(heads):
            shifted = vec if h == 0 else pltpu.roll(vec, wide - h * HEAD, 1)
            ref[0, h] = shifted[:, :HEAD].astype(BF)

    query = rotate(jnp.dot(x, w[0], preferred_element_type=F32))
    store_heads(q, query * (HEAD**-0.5))
    key = rotate(jnp.dot(x, w[1], preferred_element_type=F32))
    store_heads(k, key)
    kt[0] = key.T[: heads * HEAD].astype(BF)
    value = jnp.dot(x, w[2], preferred_element_type=F32)
    store_heads(v, value)
    vt[0] = value.T[: heads * HEAD].astype(BF)


def qkv_call(tab, tok_all, mod, gain, cos, sin, w0, w1):
    groups, seq, width = tok_all.shape
    block = seq // 4
    wide = w0.shape[3]
    heads = (wide // HEAD) * 3 // 4
    feats = heads * HEAD
    grid_spec = pltpu.PrefetchScalarGridSpec(
        num_scalar_prefetch=1,
        grid=(groups, 4),
        in_specs=[
            spec((1, block, width), lambda g, j, _: (g, j, 0)),
            spec((1, 6, width), lambda g, j, _: (g, 0, 0)),
            whole((1, width)),
            spec((block, wide), lambda g, j, _: (j, 0)),
            spec((block, wide), lambda g, j, _: (j, 0)),
            ANY,
            ANY,
        ],
        out_specs=[
            spec((1, block, width), lambda g, j, _: (g, j, 0)),
            spec((1, heads, block, HEAD), lambda g, j, _: (g, 0, j, 0)),
            spec((1, heads, block, HEAD), lambda g, j, _: (g, 0, j, 0)),
            spec((1, heads, block, HEAD), lambda g, j, _: (g, 0, j, 0)),
            spec((1, feats, block), lambda g, j, _: (g, 0, j)),
            spec((1, feats, block), lambda g, j, _: (g, 0, j)),
            whole((3, width, wide)),
        ],
        scratch_shapes=[pltpu.SemaphoreType.DMA((8,))],
    )
    head_shape = jax.ShapeDtypeStruct((groups, heads, seq, HEAD), BF)
    turned = jax.ShapeDtypeStruct((groups, feats, seq), BF)
    return pl.pallas_call(
        qkv_kernel,
        grid_spec=grid_spec,
        out_shape=[
            jax.ShapeDtypeStruct((groups, seq, width), BF),
            head_shape,
            head_shape,
            head_shape,
            turned,
            turned,
            jax.ShapeDtypeStruct((3, width, wide), BF),
        ],
        compiler_params=params(),
        cost_estimate=cost(2 * groups * seq * width * wide * 3, 16 * 2**20),
        name="qkv",
    )(tab, tok_all, mod, gain, cos, sin, w0, w1)


def attend_kernel(lens, q, k, vt, mixed, probs):
    heads, seq = k.shape[1], k.shape[2]
    block = q.shape[2]
    live = lax.broadcasted_iota(jnp.int32, (seq, block), 0) < lens[pl.program_id(0)]
    parts = []
    for h in range(heads):
        scores = lax.dot_general(k[0, h], q[0, h], NT, preferred_element_type=F32)
        scores = jnp.where(live, scores, MASKED)
        largest = jnp.max(scores, axis=0, keepdims=True)
        weights = jnp.exp(scores - largest)
        total = jnp.sum(weights, axis=0, keepdims=True)
        low = (weights * (1.0 / total)).astype(BF)
        probs[0, h] = low
        parts.append(
            jnp.dot(vt[0, h * HEAD : (h + 1) * HEAD, :], low, preferred_element_type=F32)
        )
    pad = (-heads * HEAD) % 128
    if pad:
        parts.append(jnp.zeros((pad, block), F32))
    mixed[0, 0] = jnp.concatenate(parts, axis=0).T[:, : heads * HEAD].astype(BF)


def attend_call(lens, q, k, vt):
    groups, heads, seq, _ = q.shape
    block = seq // 4
    feats = heads * HEAD
    grid_spec = pltpu.PrefetchScalarGridSpec(
        num_scalar_prefetch=1,
        grid=(groups, 4),
        in_specs=[
            spec((1, heads, block, HEAD), lambda g, j, _: (g, 0, j, 0)),
            spec((1, heads, seq, HEAD), lambda g, j, _: (g, 0, 0, 0)),
            spec((1, feats, seq), lambda g, j, _: (g, 0, 0)),
        ],
        out_specs=[
            spec((1, 1, block, feats), lambda g, j, _: (j, g, 0, 0)),
            spec((1, heads, seq, block), lambda g, j, _: (g, 0, 0, j)),
        ],
    )
    return pl.pallas_call(
        attend_kernel,
        grid_spec=grid_spec,
        out_shape=[
            jax.ShapeDtypeStruct((4, groups, block, feats), BF),
            jax.ShapeDtypeStruct((groups, heads, seq, seq), BF),
        ],
        compiler_params=params(),
        cost_estimate=cost(
            16 * groups * heads * seq * seq * HEAD, 20 * 2**20, groups * heads * seq * seq
        ),
        name="attend",
    )(lens, q, k, vt)


def attend_back_kernel(q, kt, v, probs, gm, cos, sin, out, dk, dv):
    heads, block = q.shape[1], q.shape[2]
    half = HEAD // 2
    j = pl.program_id(1)

    @pl.when(j == 0)
    def _():
        dk[...] = jnp.zeros_like(dk)
        dv[...] = jnp.zeros_like(dv)

    columns = pl.ds(pl.multiple_of(j * block, 128), block)
    cos_here, sin_here = cos[:, columns], sin[:, columns]

    def store_turned(plane, h, vec, c, s, where):
        low, high = vec[:half], vec[half:]
        base = h * HEAD
        out[0, plane, base : base + half, where] = (low * c + high * s).astype(BF)
        out[0, plane, base + half : base + HEAD, where] = (high * c - low * s).astype(BF)

    for h in range(heads):
        tile = h // 2 * 128
        stop = min(tile + 128, heads * HEAD)
        part = gm[0, 0, :, tile:stop].astype(F32)
        if h % 2:
            part = pltpu.roll(part, HEAD, 1)
        grad = part[:, :HEAD].astype(BF)
        low = probs[0, h]
        dp = lax.dot_general(v[0, h], grad, NT, preferred_element_type=F32)
        soft = low.astype(F32)
        prod = soft * dp
        inner = jnp.sum(prod, axis=0, keepdims=True)
        ds = (prod - soft * inner).astype(BF)
        dv[h] += jnp.dot(low, grad, preferred_element_type=F32)
        dk[h] += jnp.dot(ds, q[0, h], preferred_element_type=F32)
        dq = jnp.dot(kt[0, h * HEAD : (h + 1) * HEAD, :], ds, preferred_element_type=F32)
        store_turned(0, h, dq * (HEAD**-0.5), cos_here, sin_here, columns)

    @pl.when(j == pl.num_programs(1) - 1)
    def _():
        for h in range(heads):
            store_turned(1, h, dk[h].T, cos[...], sin[...], slice(None))
            out[0, 2, h * HEAD : (h + 1) * HEAD, :] = dv[h].T.astype(BF)


def attend_back_call(q, kt, v, probs, gm, cos, sin):
    groups, heads, seq, _ = q.shape
    block = seq // 4
    feats = heads * HEAD
    half = HEAD // 2
    return pl.pallas_call(
        attend_back_kernel,
        grid=(groups, 4),
        in_specs=[
            spec((1, heads, block, HEAD), lambda g, j: (g, 0, j, 0)),
            spec((1, feats, seq), lambda g, j: (g, 0, 0)),
            spec((1, heads, seq, HEAD), lambda g, j: (g, 0, 0, 0)),
            spec((1, heads, seq, block), lambda g, j: (g, 0, 0, j)),
            spec((1, 1, block, feats), lambda g, j: (j, g, 0, 0)),
            whole((half, seq)),
            whole((half, seq)),
        ],
        out_specs=spec((1, 3, feats, seq), lambda g, j: (g, 0, 0, 0)),
        out_shape=jax.ShapeDtypeStruct((groups, 3, feats, seq), BF),
        scratch_shapes=[
            pltpu.VMEM((heads, seq, HEAD), F32),
            pltpu.VMEM((heads, seq, HEAD), F32),
        ],
        compiler_params=params(),
        cost_estimate=cost(32 * groups * heads * seq * seq * HEAD, 20 * 2**20),
        name="attend_back",
    )(q, kt, v, probs, gm, cos, sin)


def qkv_back_kernel(tab, gt, first, tok, w, fts, ftk, sums, dw, acc):
    i = pl.program_id(0)
    feats, block = gt.shape[2], gt.shape[3]
    wide, width = w.shape[2], w.shape[1]
    rows = dw.shape[2]
    g = lax.rem(i, 2)

    @pl.when(i == 0)
    def _():
        acc[...] = jnp.zeros_like(acc)
        sums[...] = jnp.zeros_like(sums)

    total = None
    for j in range(3):
        part = gt[0, j]
        tall = part.astype(F32)
        if wide > feats:
            tall = jnp.concatenate([tall, jnp.zeros((wide - feats, block), F32)], axis=0)
        term = lax.dot_general(tall.T.astype(BF), w[j], NT, preferred_element_type=F32)
        total = term if total is None else total + term
        acc[j, :feats] += jnp.dot(part, first[0], preferred_element_type=F32)
    normed, _ = norm_rows(tok[0].astype(F32))
    sums[g, 0:1, :] += jnp.sum(total, axis=0, keepdims=True)
    sums[g, 1:2, :] += jnp.sum(total * normed, axis=0, keepdims=True)
    low = total.astype(BF)

    @pl.when(i < 4)
    def _():
        fts[0, 0] = low

    @pl.when(i >= 4)
    def _():
        ftk[0, 0] = low

    @pl.when(i == pl.num_programs(0) - 1)
    def _():
        for j in range(3):
            flat = acc[j].T.astype(BF)
            for b in range(NBLK):
                dw[tab[b], j] = flat[b * rows : (b + 1) * rows]


def qkv_back_call(tab, gt, first, tok_all, w):
    groups, _, feats, seq = gt.shape
    block = seq // 4
    width = first.shape[2]
    wide = w.shape[2]
    rows = width // NBLK

    def piece(i, tab):
        return lax.bitwise_xor(tab[NBLK], lax.rem(i, 4) // 2 * 2 + (1 - i // 4))

    grid_spec = pltpu.PrefetchScalarGridSpec(
        num_scalar_prefetch=1,
        grid=(8,),
        in_specs=[
            spec((1, 3, feats, block), lambda i, tab: (lax.rem(i, 2), 0, 0, piece(i, tab))),
            spec((1, block, width), lambda i, tab: (lax.rem(i, 2), piece(i, tab), 0)),
            spec((1, block, width), lambda i, tab: (lax.rem(i, 2), piece(i, tab), 0)),
            whole((3, width, wide)),
        ],
        out_specs=[
            spec(
                (1, 1, block, width),
                lambda i, tab: (jnp.minimum(i, 3) // 2, lax.rem(jnp.minimum(i, 3), 2), 0, 0),
            ),
            spec(
                (1, 1, block, width),
                lambda i, tab: (
                    jnp.maximum(i - 4, 0) // 2,
                    lax.rem(jnp.maximum(i - 4, 0), 2),
                    0,
                    0,
                ),
            ),
            whole((groups, 2, width)),
            whole((NBLK, 3, rows, wide)),
        ],
        scratch_shapes=[pltpu.VMEM((3, wide, width), F32)],
    )
    terms = jax.ShapeDtypeStruct((2, groups, block, width), BF)
    return pl.pallas_call(
        qkv_back_kernel,
        grid_spec=grid_spec,
        out_shape=[
            terms,
            terms,
            jax.ShapeDtypeStruct((groups, 2, width), F32),
            jax.ShapeDtypeStruct((NBLK, 3, rows, wide), BF),
        ],
        compiler_params=params(),
        cost_estimate=cost(4 * groups * seq * width * wide * 3, 16 * 2**20),
        name="qkv_back",
    )(tab, gt, first, tok_all, w)


def mlp_kernel(
    tab,
    tok,
    cot,
    mixed,
    mod,
    gain,
    upb,
    downb,
    *rest,
):
    pieces = rest[:8]
    (
        out,
        gafter,
        gmixed,
        sums,
        upsum,
        gu_s,
        gu_k,
        gd_s,
        gd_k,
        w,
        gu,
        gd,
        after,
        normed,
        inverse,
        second,
        second_t,
        gbr,
        gbr_t,
        att,
        branch,
        gsec,
        act,
        gh,
        sem_w,
        sem_g,
        sem_d,
    ) = rest[8:]
    groups, block, width = tok.shape
    feats = mixed.shape[3]
    rows = pieces[0].shape[1]
    fh = upb.shape[1]
    total_rows = groups * block
    t_part, t_row, t_slot, t_dst = 3, 7, 39, 47

    loads = []
    for p in range(8):
        for j in range(4):
            row = pl.multiple_of(tab[t_row + p * 4 + j] * rows, 16)
            loads.append(
                pltpu.make_async_copy(
                    pieces[p].at[j],
                    w.at[tab[t_slot + p], pl.ds(row, rows), :],
                    sem_w.at[p * 4 + j],
                )
            )
    for load in loads:
        load.start()
    for load in loads:
        load.wait()

    def span(g):
        return pl.ds(pl.multiple_of(g * block, block), block)

    def prepare(g, _):
        here = span(g)
        total = jnp.zeros((block, width), F32)
        for k in range(4):
            total += lax.dot_general(
                mixed[tab[t_part + k], g],
                w[k, :, 2 * fh : 2 * fh + feats],
                NT,
                preferred_element_type=F32,
            )
        att[here, :] = total
        rows_after = tok[g].astype(F32) + mod[g, 2:3, :] * total
        after[here, :] = rows_after
        n, inv = norm_rows(rows_after)
        normed[here, :] = n
        inverse[here, :] = jnp.broadcast_to(inv, (block, 128))
        x = n * (gain[...] * (1.0 + mod[g, 4:5, :])) + mod[g, 3:4, :]
        second[here, :] = x.astype(BF)
        position = tab[2] + lax.broadcasted_iota(jnp.int32, (block, width), 0)
        grad_y = jnp.where(position < tab[g], cot[g].astype(F32), 0.0)
        gb = (mod[g, 5:6, :] * grad_y).astype(BF)
        gbr[here, :] = gb
        sums[g, 4:5, :] = jnp.sum(gb.astype(F32), axis=0, keepdims=True)
        branch[here, :] = jnp.broadcast_to(downb[...], (block, width))
        gsec[here, :] = jnp.zeros((block, width), F32)
        return 0

    lax.fori_loop(0, groups, prepare, 0)
    second_t[...] = second[...].T
    gbr_t[...] = gbr[...].T

    c1, c3 = math.sqrt(2.0 / math.pi), 0.044715

    def store_grads(k, src, send, keep, sem):
        for b in range(NBLK):
            there = tab[t_dst + k * NBLK + b]
            piece = src.at[k, pl.ds(b * rows, rows), :]

            @pl.when(k < 2)
            def _():
                pltpu.make_async_copy(piece, keep.at[there], sem.at[k, b]).start()

            @pl.when(k >= 2)
            def _():
                pltpu.make_async_copy(piece, send.at[there], sem.at[k, b]).start()

    def slot(k, _):
        part = tab[t_part + k]
        bias = upb[pl.ds(part, 1), :]

        def half(g, total):
            here = span(g)
            hidden = jnp.dot(second[here, :], w[k, :, :fh], preferred_element_type=F32) + bias
            square = hidden * hidden
            th = jnp.tanh(c1 * hidden * (1.0 + c3 * square))
            up = 0.5 * (1.0 + th)
            active = (hidden * up).astype(BF)
            act[here, :] = active
            slope = up + (0.5 * c1) * hidden * (1.0 - th * th) * (1.0 + (3.0 * c3) * square)
            branch[here, :] += lax.dot_general(
                active, w[k, :, fh : 2 * fh], NT, preferred_element_type=F32
            )
            ga = jnp.dot(gbr[here, :], w[k, :, fh : 2 * fh], preferred_element_type=F32)
            grad = (ga * slope).astype(BF)
            gh[here, :] = grad
            gsec[here, :] += lax.dot_general(
                grad, w[k, :, :fh], NT, preferred_element_type=F32
            )
            return total + jnp.sum(grad.astype(F32), axis=0, keepdims=True)

        upsum[pl.ds(part, 1), :] = lax.fori_loop(0, groups, half, jnp.zeros((1, fh), F32))

        def grads(r, _):
            these = pl.ds(pl.multiple_of(r * 256, 256), 256)
            gu[k, these, :] = jnp.dot(
                second_t[these, :], gh[...], preferred_element_type=F32
            ).astype(BF)
            gd[k, these, :fh] = jnp.dot(
                gbr_t[these, :], act[...], preferred_element_type=F32
            ).astype(BF)
            return 0

        lax.fori_loop(0, width // 256, grads, 0)
        store_grads(k, gu, gu_s, gu_k, sem_g)
        return 0

    lax.fori_loop(0, 4, slot, 0)

    def finish(g, _):
        here = span(g)
        position = tab[2] + lax.broadcasted_iota(jnp.int32, (block, width), 0)
        grad_y = jnp.where(position < tab[g], cot[g].astype(F32), 0.0)
        out[g] = (after[here, :] + mod[g, 5:6, :] * branch[here, :]).astype(BF)
        sums[g, 2:3, :] = jnp.sum(grad_y * branch[here, :], axis=0, keepdims=True)
        n = normed[here, :]
        gs = gsec[here, :]
        sums[g, 0:1, :] = jnp.sum(gs, axis=0, keepdims=True)
        sums[g, 1:2, :] = jnp.sum(gs * n, axis=0, keepdims=True)
        scaled = gs * (gain[...] * (1.0 + mod[g, 4:5, :]))
        mean = jnp.mean(scaled, axis=1, keepdims=True)
        along = jnp.mean(scaled * n, axis=1, keepdims=True)
        grad = grad_y + inverse[here, 0:1] * (scaled - mean - n * along)
        gafter[g] = grad
        sums[g, 3:4, :] = jnp.sum(grad * att[here, :], axis=0, keepdims=True)
        low = (mod[g, 2:3, :] * grad).astype(BF)
        gbr[here, :] = low
        for k in range(4):
            gmixed[tab[t_part + k], g] = jnp.dot(
                low, w[k, :, 2 * fh : 2 * fh + feats], preferred_element_type=F32
            ).astype(BF)
        return 0

    lax.fori_loop(0, groups, finish, 0)
    gbr_t[...] = gbr[...].T

    def last(k, _):
        part = mixed[tab[t_part + k]].reshape(total_rows, feats)
        gd[k, :, fh : fh + feats] = jnp.dot(
            gbr_t[...], part, preferred_element_type=F32
        ).astype(BF)
        store_grads(k, gd, gd_s, gd_k, sem_d)
        return 0

    lax.fori_loop(0, 4, last, 0)
    for k in range(4):
        for b in range(NBLK):
            pltpu.make_async_copy(
                gu.at[k, pl.ds(b * rows, rows), :], gu_s.at[0], sem_g.at[k, b]
            ).wait()
            pltpu.make_async_copy(
                gd.at[k, pl.ds(b * rows, rows), :], gd_s.at[0], sem_d.at[k, b]
            ).wait()


def mlp_call(tab, tok, cot, mixed, mod, gain, upb, downb, pieces):
    groups, block, width = tok.shape
    feats = mixed.shape[3]
    fh = upb.shape[1]
    lanes = pieces[0].shape[2]
    rows = width // NBLK
    total = groups * block
    vm = pl.BlockSpec(memory_space=pltpu.VMEM)
    sm = pl.BlockSpec(memory_space=pltpu.SMEM)
    up = jax.ShapeDtypeStruct((16, rows, fh), BF)
    down = jax.ShapeDtypeStruct((16, rows, fh + feats), BF)
    return pl.pallas_call(
        mlp_kernel,
        in_specs=[sm] + [vm] * 7 + [ANY] * 8,
        out_specs=[vm] * 5 + [ANY] * 4,
        out_shape=[
            jax.ShapeDtypeStruct((groups, block, width), BF),
            jax.ShapeDtypeStruct((groups, block, width), F32),
            jax.ShapeDtypeStruct((4, groups, block, feats), BF),
            jax.ShapeDtypeStruct((groups, 8, width), F32),
            jax.ShapeDtypeStruct((4, fh), F32),
            up,
            up,
            down,
            down,
        ],
        scratch_shapes=[
            pltpu.VMEM((4, width, lanes), BF),
            pltpu.VMEM((4, width, fh), BF),
            pltpu.VMEM((4, width, fh + feats), BF),
            pltpu.VMEM((total, width), F32),
            pltpu.VMEM((total, width), F32),
            pltpu.VMEM((total, 128), F32),
            pltpu.VMEM((total, width), BF),
            pltpu.VMEM((width, total), BF),
            pltpu.VMEM((total, width), BF),
            pltpu.VMEM((width, total), BF),
            pltpu.VMEM((total, width), F32),
            pltpu.VMEM((total, width), F32),
            pltpu.VMEM((total, width), F32),
            pltpu.VMEM((total, fh), BF),
            pltpu.VMEM((total, fh), BF),
            pltpu.SemaphoreType.DMA((32,)),
            pltpu.SemaphoreType.DMA((4, NBLK)),
            pltpu.SemaphoreType.DMA((4, NBLK)),
        ],
        compiler_params=params(),
        cost_estimate=cost(12 * total * width * fh * 4, 28 * 2**20, total * fh * 4),
        name="mlp",
    )(tab, tok, cot, mixed, mod, gain, upb, downb, *pieces)


def time_embedding(time_steps, width_total):
    half_width = width_total // 2
    frequency = jnp.exp(-math.log(10000.0) * jnp.arange(half_width, dtype=F32) / half_width)
    angles = time_steps.astype(F32)[:, None] * frequency[None, :]
    return jnp.concatenate([jnp.cos(angles), jnp.sin(angles)], axis=-1)


def rotary_halves(length_total):
    half = HEAD // 2
    inverse = jnp.exp(-math.log(10000.0) * 2.0 * jnp.arange(half, dtype=F32) / HEAD)
    angles = jnp.arange(length_total, dtype=F32)[:, None] * inverse[None, :]
    return jnp.cos(angles), jnp.sin(angles)


def device_index(z, y, x, c):
    return ((z * 2 + y) * 2 + x) * 2 + c


def permutation(move):
    pairs = []
    for z in range(4):
        for y in range(2):
            for x in range(2):
                for c in range(2):
                    pairs.append((device_index(z, y, x, c), device_index(*move(z, y, x, c))))
    return pairs


CORE = permutation(lambda z, y, x, c: (z, y, x, 1 - c))
FLIP_X = permutation(lambda z, y, x, c: (z, y, 1 - x, c))
FLIP_Y = permutation(lambda z, y, x, c: (z, 1 - y, x, c))
FIRST = permutation(lambda z, y, x, c: (z, 1 - y, x, c) if c == 0 else (z, y, 1 - x, c))
SECOND = permutation(lambda z, y, x, c: (z, y, 1 - x, c) if c == 0 else (z, 1 - y, x, c))
ALONG_Z = [permutation(lambda z, y, x, c, s=s: ((z + s) % 4, y, x, c)) for s in range(4)]


def send(array, pairs):
    return lax.ppermute(array, ("dp", "tensor"), pairs)


def gather_z(shard):
    parts = [shard] + [send(shard, ALONG_Z[s]) for s in (1, 2, 3)]
    return jnp.stack(parts)


def reduce_chunk(sent, kept):
    shape = (2, 2, 4) + sent.shape[1:]
    kept = kept.reshape(shape)
    got = send(sent, CORE).reshape(shape)
    first_half = (kept[1].astype(F32) + got[1].astype(F32)).astype(BF)
    got_two = send(first_half, SECOND)
    second_half = (
        kept[0, 1].astype(F32) + got[0, 1].astype(F32) + got_two[1].astype(F32)
    ).astype(BF)
    got_three = send(second_half, FIRST)
    summed = (
        kept[0, 0].astype(F32)
        + got[0, 0].astype(F32)
        + got_two[0].astype(F32)
        + got_three.astype(F32)
    )
    result = summed[0]
    for s in (1, 2, 3):
        result = result + send(summed[s].astype(BF), ALONG_Z[s]).astype(F32)
    return result


def tables(z, y, x, c):
    far_core = np.array([0, 0, 0, 0, 1, 1, 1, 1])
    kind = np.array([0, 1, 2, 3] * 2)
    core = jnp.bitwise_xor(c, far_core)
    rel_x = jnp.where(kind == 0, 0, jnp.where(kind == 3, 1, jnp.where(kind == 1, core, 1 - core)))
    rel_y = jnp.where(kind == 0, 0, jnp.where(kind == 3, 1, jnp.where(kind == 1, 1 - core, core)))
    slots = far_core * 2 + rel_x
    back = np.arange(4)
    from_z = jnp.remainder(z - back, 4)
    weight_rows = (from_z[None, :] * 2 + jnp.bitwise_xor(y, rel_y)[:, None]).reshape(32)
    slot = np.arange(4)
    parts = jnp.bitwise_xor(x, slot % 2) * 2 + jnp.bitwise_xor(c, slot // 2)
    block = np.arange(NBLK)
    to_z = jnp.remainder(block // 2 - z, 4)
    to_y = jnp.bitwise_xor(block % 2, y)
    slot_core = jnp.bitwise_xor(c, slot // 2)[:, None]
    to_x = (slot % 2)[:, None]
    major = jnp.where(slot_core == 0, to_x, to_y[None, :])
    minor = jnp.where(slot_core == 0, to_y[None, :], to_x)
    targets = (major * 8 + minor * 4 + to_z[None, :]).reshape(4 * NBLK)
    qkv_rows = jnp.concatenate(
        [from_z * 2 + y, from_z * 2 + (1 - y)]
    )
    qkv_targets = to_y * 4 + to_z
    return parts, weight_rows, slots, targets, qkv_rows, qkv_targets


def shards(
    tokens,
    lengths,
    times,
    cotangent,
    w_qkv,
    w_out,
    w_up,
    up_bias,
    w_down,
    down_bias,
    norm1_gain,
    norm2_gain,
    ada_weight,
    ada_bias,
):
    groups, block, width = tokens.shape
    dp, tp = lax.axis_size("dp"), lax.axis_size("tensor")
    seq = block * tp
    t = lax.axis_index("tensor")
    d = lax.axis_index("dp")
    fast = dp == 8 and tp == 4
    feats = w_qkv.shape[2]
    fh = w_up.shape[1]
    rows = width // NBLK
    zero = jnp.zeros((), jnp.int32)
    z, y, x, c = (d // 2, d % 2, t // 2, t % 2) if fast else (zero, zero, zero, zero)
    here = t if fast else zero
    parts, weight_rows, slots, targets, qkv_rows, qkv_targets = tables(z, y, x, c)

    pad = (-feats) % 128
    qkv_shard = jnp.pad(w_qkv, ((0, 0), (0, 0), (0, pad)))
    mlp_shard = jnp.concatenate([w_up, w_down.T, w_out.T], axis=1)
    if fast:
        near = gather_z(qkv_shard)
        qkv_pieces = (near, send(near, FLIP_Y))
        base = gather_z(mlp_shard)
        one = send(base, FIRST)
        two = send(base, SECOND)
        both = send(one, SECOND)
        own = (base, one, two, both)
        pieces = own + tuple(send(piece, CORE) for piece in own)
    else:
        full = lax.all_gather(qkv_shard, "dp", axis=1, tiled=True)
        full = full.reshape(3, NBLK, rows, feats + pad).transpose(1, 0, 2, 3)
        order = [[(-j) % 4 * 2 + p for j in range(4)] for p in range(2)]
        qkv_pieces = tuple(jnp.stack([full[b] for b in order[p]]) for p in range(2))
        full = lax.all_gather(mlp_shard, "dp", axis=0, tiled=True)
        full = lax.all_gather(full, "tensor", axis=0, tiled=False)
        full = full.reshape(tp, NBLK, rows, full.shape[2])
        pieces = []
        for far in range(2):
            for rel_x, rel_y in ((0, 0), (far, 1 - far), (1 - far, far), (1, 1)):
                pieces.append(
                    jnp.stack([full[rel_x * 2 + far, b] for b in order[rel_y]])
                )
        pieces = tuple(pieces)
    tok_all = lax.all_gather(tokens, "tensor", axis=1, tiled=True)

    all_times = lax.all_to_all(
        jnp.broadcast_to(times[None, :], (dp, groups)), "dp", 0, 0, tiled=True
    ).reshape(-1)
    condition = time_embedding(all_times, ada_weight.shape[0])
    part = jnp.dot(
        condition, ada_weight.astype(F32), precision=lax.Precision.HIGHEST
    ) + ada_bias.astype(F32)
    cols = part.shape[1]
    vectors = jnp.concatenate([up_bias, down_bias, norm1_gain, norm2_gain]).astype(F32)
    payload = jnp.concatenate(
        [
            part.reshape(dp, groups * cols),
            jnp.broadcast_to(vectors[None, :], (dp, vectors.shape[0])),
        ],
        axis=1,
    )
    payload = lax.all_to_all(payload, "dp", 0, 0, tiled=True)
    mod = (
        payload[:, : groups * cols]
        .reshape(dp, groups, cols)
        .transpose(1, 0, 2)
        .reshape(groups, 6, width)
    )
    at = groups * cols
    small = []
    for count in (up_bias.shape[0], down_bias.shape[0], norm1_gain.shape[0], norm2_gain.shape[0]):
        small.append(payload[:, at : at + count].reshape(-1))
        at += count
    upb_all = small[0].reshape(tp, fh)
    downb_all, gain_one, gain_two = (v.reshape(1, width) for v in small[1:])

    cos, sin = rotary_halves(seq)
    heads_wide = (feats + pad) // HEAD
    cos_wide = jnp.tile(jnp.concatenate([cos, cos], axis=1), (1, heads_wide))
    sin_wide = jnp.tile(jnp.concatenate([-sin, sin], axis=1), (1, heads_wide))
    first_all, q, k, v, kt, vt, w_all = qkv_call(
        qkv_rows.astype(jnp.int32), tok_all, mod, gain_one, cos_wide, sin_wide, *qkv_pieces
    )
    mixed, probs = attend_call(lengths, q, k, vt)
    mixed = lax.all_to_all(mixed, "tensor", 0, 0, tiled=True)

    tab = jnp.concatenate(
        [
            lengths,
            (t * block).reshape(1),
            parts,
            weight_rows,
            slots,
            targets,
        ]
    ).astype(jnp.int32)
    out, grad_after, grad_mixed, sums, upsum, gu_s, gu_k, gd_s, gd_k = mlp_call(
        tab, tokens, cotangent, mixed, mod, gain_two, upb_all, downb_all, pieces
    )
    grad_mixed = lax.all_to_all(grad_mixed, "tensor", 0, 0, tiled=True)
    grad_t = attend_back_call(q, kt, v, probs, grad_mixed, cos.T, sin.T)
    fts, ftk, sums_one, dw = qkv_back_call(
        jnp.concatenate([qkv_targets, here.reshape(1)]).astype(jnp.int32),
        grad_t,
        first_all,
        tok_all,
        w_all,
    )

    if fast:
        sum_up = reduce_chunk(gu_s, gu_k)
        sum_down = reduce_chunk(gd_s, gd_k)
        near, far = dw[:4], dw[4:]
        near = near.astype(F32) + send(far, FLIP_Y).astype(F32)
        sum_qkv = near[0]
        for s in (1, 2, 3):
            sum_qkv = sum_qkv + send(near[s].astype(BF), ALONG_Z[s]).astype(F32)
        got = send(fts, CORE)
        far = (ftk[1].astype(F32) + got[1].astype(F32)).astype(BF)
        grad_first = ftk[0].astype(F32) + got[0].astype(F32) + send(far, FLIP_X).astype(F32)
    else:

        def absolute(sent, kept):
            lanes = sent.shape[2]
            near = kept.reshape(2, 2, 4, rows, lanes)
            far = sent.reshape(2, 2, 4, rows, lanes).transpose(1, 0, 2, 3, 4)
            both = jnp.stack([near, far], axis=1)
            return both.transpose(0, 1, 3, 2, 4, 5).reshape(tp, width, lanes).astype(F32)

        def reduce_all(sent, kept):
            terms = lax.psum_scatter(
                absolute(sent, kept), "tensor", scatter_dimension=0, tiled=True
            )[0]
            return lax.psum_scatter(terms, "dp", scatter_dimension=0, tiled=True)

        sum_up = reduce_all(gu_s, gu_k)
        sum_down = reduce_all(gd_s, gd_k)
        terms = dw.reshape(2, 4, 3, rows, feats + pad).transpose(2, 1, 0, 3, 4)
        terms = terms.reshape(3, width, feats + pad).astype(F32)
        sum_qkv = lax.psum_scatter(terms, "dp", scatter_dimension=1, tiled=True)
        terms = jnp.stack([ftk, fts], axis=1).reshape(tp, groups, block, width).astype(F32)
        grad_first = lax.psum_scatter(terms, "tensor", scatter_dimension=0, tiled=True)[0]

    p_one, q_one = sums_one[:, 0], sums_one[:, 1]
    p_two, q_two = sums[:, 0], sums[:, 1]
    grad_mod = jnp.stack(
        [p_one, gain_one * q_one, sums[:, 3], p_two, gain_two * q_two, sums[:, 2]], axis=1
    )
    grad_mod = grad_mod.reshape(groups, dp, cols).transpose(1, 0, 2).reshape(dp, groups * cols)
    payload = jnp.concatenate(
        [
            grad_mod,
            upsum.reshape(dp, -1),
            jnp.sum(sums[:, 4], axis=0).reshape(dp, -1),
            jnp.sum((1.0 + mod[:, 1]) * q_one, axis=0).reshape(dp, -1),
            jnp.sum((1.0 + mod[:, 4]) * q_two, axis=0).reshape(dp, -1),
        ],
        axis=1,
    )
    lanes = payload.shape[1]
    payload = jnp.broadcast_to(payload[:, None, :], (dp, tp, lanes)).reshape(dp * tp, lanes)
    payload = lax.all_to_all(payload, ("dp", "tensor"), 0, 0, tiled=True)
    payload = jnp.sum(payload.reshape(dp, tp, lanes), axis=1)
    mods = payload[:, : groups * cols].reshape(dp * groups, cols)
    grad_adaw = jnp.dot(condition.T, mods, precision=lax.Precision.HIGHEST)
    grad_adab = jnp.sum(mods, axis=0)
    vectors = jnp.sum(payload[:, groups * cols :], axis=0)
    at, small = 0, []
    for count in (up_bias.shape[0], down_bias.shape[0], norm1_gain.shape[0], norm2_gain.shape[0]):
        small.append(vectors[at : at + count])
        at += count

    normed, inverse = (
        a.reshape(groups, block, -1)
        for a in norm_rows(tokens.astype(F32).reshape(groups * block, width))
    )
    scaled = grad_first * (gain_one * (1.0 + mod[:, 1]))[:, None, :]
    mean = jnp.mean(scaled, axis=-1, keepdims=True)
    along = jnp.mean(scaled * normed, axis=-1, keepdims=True)
    grad_input = grad_after + inverse * (scaled - mean - normed * along)

    return (
        out,
        grad_input.astype(BF),
        sum_qkv[:, :, :feats],
        sum_down[:, fh:].T,
        sum_up,
        small[0],
        sum_down[:, :fh].T,
        small[1],
        small[2],
        small[3],
        grad_adaw,
        grad_adab,
    )


def solution(mesh):
    in_specs = (
        P("dp", "tensor", None),
        P("dp"),
        P("dp"),
        P("dp", "tensor", None),
        P(None, "dp", "tensor"),
        P("tensor", "dp"),
        P("dp", "tensor"),
        P("dp"),
        P("tensor", "dp"),
        P("dp"),
        P("dp"),
        P("dp"),
        P(None, "dp"),
        P("dp"),
    )
    out_specs = (
        P("dp", "tensor", None),
        P("dp", "tensor", None),
        P(None, "dp", "tensor"),
        P("tensor", "dp"),
        P("dp", "tensor"),
        P("dp"),
        P("tensor", "dp"),
        P("dp"),
        P("dp"),
        P("dp"),
        P(None, "dp"),
        P("dp"),
    )
    return jax.shard_map(shards, mesh=mesh, in_specs=in_specs, out_specs=out_specs, check_vma=False)
```

time: 1080 us -> 404 us (0.37)
  waiting for transfers between devices: 638 us -> 113 us
  blocking collectives: 176 us -> 0 us
  matrix products: 123 us -> 2.43 us
  Pallas kernels: 0 us -> 112 us
  starting transfers between devices: 1.49 us -> 97.8 us
  local copies, waits for them, and re-layouts: 68.6 us -> 30.1 us
  other arithmetic: 46.9 us -> 32.4 us
    reduce_scatter x7 -> x0, waiting for transfers between devices: 339 us -> none  [the longest x1 72 us: shards(): lax.psum_scatter(grad_up_w, 'dp', scatter_dimension=0, tiled=True)]
    all_gather x7 -> x1, waiting for transfers between devices: 133 us -> 0.01 us  [shards(): tok_all = lax.all_gather(tokens, 'tensor', axis=1, tiled=True)]
    unnamed x19 -> x1, waiting for transfers between devices: 132 us -> 0.68 us
    dot_general x42 -> x2, matrix products: 123 us -> 2.43 us  [the longest x1 2.16 us: shards(): grad_adaw = jnp.dot(condition.T, mods, precision=lax.Precision.HIGHEST)]
    pallas_call x0 -> x5, Pallas kernels: none -> 112 us  [the longest x1 37.2 us: mlp_call(): pl.pallas_call(mlp_kernel, in_specs=[sm] + [vm] * 7 + [ANY] * 8, out_spec...]
    all_gather x3 -> x0, blocking collectives: 94.3 us -> none  [the longest x1 34.5 us: shards(): lax.all_gather(w_qkv, 'dp', axis=1, tiled=True)]
    unnamed x2 -> x0, blocking collectives: 75.5 us -> none
    ppermute x0 -> x32, waiting for transfers between devices: none -> 74.8 us  [send(): return lax.ppermute(array, ('dp', 'tensor'), pairs)]
  transfers between devices with their start and end apart: 17 -> 38, of which waited for: 15 -> 14; matrix products, arithmetic and copies ran while one was open for 6% -> 14% of each run, Pallas kernels for 0% -> 19%
where the time goes in v1:
time: 404 us; the launch traced here: 402 us
  waiting for transfers between devices  113 us (28%)
  Pallas kernels  112 us (28%)
  starting transfers between devices  97.8 us (24%)
  other arithmetic  32.4 us (8%)
  local copies, waits for them, and re-layouts  30.1 us (7%)
  between operations  14.7 us (4%)
    ppermute x32, waiting for transfers between devices, send(): return lax.ppermute(array, ('dp', 'tensor'), pairs)  74.8 us
    ppermute x32, starting transfers between devices, send(): return lax.ppermute(array, ('dp', 'tensor'), pairs)  39.8 us
    pallas_call x1, Pallas kernels, mlp_call(): pl.pallas_call(mlp_kernel, in_specs=[sm] + [vm] * 7 + [ANY] * 8, out_spec...  37.2 us
    all_to_all x1, starting transfers between devices, shards(): payload = lax.all_to_all(payload, 'dp', 0, 0, tiled=True)  28.1 us
    pallas_call x1, Pallas kernels, attend_call(): pl.pallas_call(attend_kernel, grid_spec=grid_spec, out_shape=[jax.ShapeDt...  25.2 us
    pallas_call x1, Pallas kernels, attend_back_call(): pl.pallas_call(attend_back_kernel, grid=(groups, 4), in_specs=[spec((1, h...  22.8 us
    all_to_all x1, starting transfers between devices, shards(): payload = lax.all_to_all(payload, ('dp', 'tensor'), 0, 0, tiled=True)  16.8 us
    pallas_call x1, Pallas kernels, qkv_call(): pl.pallas_call(qkv_kernel, grid_spec=grid_spec, out_shape=[jax.ShapeDtype...  14.2 us
  transfers between devices with their start and end apart: 38, of which 14 were waited for; matrix products, arithmetic and copies ran while one was open for 14% of the time, Pallas kernels for 19%

profile of v1, /device:TPU:0, one launch (start us, length us, event | category | flops | bytes accessed | tf_op | source)
XLA Modules:
  0.0 402.5 jit_solution(13341434002060608716)
XLA Ops:
  9.9 3.1 collective-permute-start.4
  13.0 2.6 collective-permute-start.5
  19.2 5.6 %all-to-all-start = ((s32[8,1,2]{2,1,0:T(1,128)}), s32[8,1,2]{2,1,0:T(1,128)S(1)}, u32[]{:S(2)}, u32[]{:S(2)}) async-start(s32[8,1,2]{2,1,0:T(1,128)} %broadcast_in_dim.65), calls=%async_computation | async-start | bytes 8192 | tf_op jit(solution)/shard_map/all_to_all | solution.py:775
  24.8 3.8 collective-permute-start.2
  28.6 10.2 %collective-permute-done.5 = bf16[96,1728]{1,0:T(8,128)(2,1)S(1)} collective-permute-done((bf16[96,1728]{1,0:T(8,128)(2,1)S(1)}, bf16[96,1728]{1,0:T(8,128)(2,1)S(1)}, u32[]{:S(2)}, u32[]{:S(2)}) %collective-permute-start.5) | collective-permute-done | bytes 331808 | tf_op jit(solution)/shard_map/ppermute | solution.py:659
  40.0 1.8 collective-permute-start.7
  45.7 10.1 %all-to-all-done = s32[8,1,2]{2,1,0:T(1,128)S(1)} async-done(((s32[8,1,2]{2,1,0:T(1,128)}), s32[8,1,2]{2,1,0:T(1,128)S(1)}, u32[]{:S(2)}, u32[]{:S(2)}) %all-to-all-start) | async-done | bytes 96 | tf_op jit(solution)/shard_map/all_to_all | solution.py:775
  55.9 1.5 collective-permute-start.8
  58.7 2.0 collective-permute-start.9
  62.2 2.1 collective-permute-start.3
  65.0 28.1 %all-to-all-start.1 = ((f32[8,1,1824]{2,1,0:T(1,128)}), f32[8,1,1824]{2,1,0:T(1,128)S(1)}, u32[]{:S(2)}, u32[]{:S(2)}) async-start(f32[8,1,1824]{2,1,0:T(1,128)} %all_to_all.25), calls=%async_computation.1 | async-start | bytes 122880 | tf_op jit(solution)/shard_map/all_to_all | solution.py:791
  93.7 6.4 %all-to-all-done.1 = f32[8,1,1824]{2,1,0:T(1,128)S(1)} async-done(((f32[8,1,1824]{2,1,0:T(1,128)}), f32[8,1,1824]{2,1,0:T(1,128)S(1)}, u32[]{:S(2)}, u32[]{:S(2)}) %all-to-all-start.1) | async-done | bytes 58400 | tf_op jit(solution)/shard_map/all_to_all | solution.py:791
  104.0 14.2 %qkv.1 = (bf16[2,1024,768]{2,1,0:T(8,128)(2,1)}, bf16[2,3,1024,64]{3,2,1,0:T(8,128)(2,1)}, bf16[2,3,1024,64]{3,2,1,0:T(8,128)(2,1)}, bf16[2,3,1024,64]{3,2,1,0:T...) custom-call(s32[8]{0:T(128)} %pad_add_fusion.tab, ...), custom_call_target="tpu_custom_call" | custom-call | flops 2415919104 | bytes 16777216 | tf_op jit(solution)/shard_map/qkv/pallas_call | solution.py:128
  118.2 25.2 %attend.1 = (bf16[4,2,256,192]{3,2,1,0:T(8,128)(2,1)}, bf16[2,3,1024,1024]{3,2,1,0:T(8,128)(2,1)}) custom-call(s32[2]{0:T(128)} %lens.1, bf16[2,3,1024,64]{3,2,1,0:T(8,128)(2,1)} %get-tuple-element.34.q, bf16[2,3,1024,64]{3,2,1,0:T(8,128)(2,1)} %get-tuple-element.35.k, bf16[2,192,1024]{2,1,0:T(8,128)(2,1)} %get-tuple-element.36.vt), custom_call_target="tpu_custom_call" | custom-call | flops 6442450944 | bytes 20971520 | tf_op jit(solution)/shard_map/attend/pallas_call | solution.py:185
  143.4 2.2 copy.62
  145.6 3.7 all-to-all-start.2
  152.2 8.7 %all-to-all-done.2 = bf16[4,2,256,192]{2,3,1,0:T(8,128)(2,1)S(1)} async-done(((bf16[4,2,256,192]{2,3,1,0:T(8,128)(2,1)}), bf16[4,2,256,192]{2,3,1,0:T(8,128)(2,1)S(1)}, u32[]{:S(2)}, u32[]{:S(2)}) %all-to-all-start.2) | async-done | bytes 786464 | tf_op jit(solution)/shard_map/all_to_all | solution.py:814
  162.3 37.2 %mlp.1 = (bf16[2,256,768]{2,1,0:T(8,128)(2,1)}, f32[2,256,768]{2,1,0:T(8,128)}, bf16[4,2,256,192]{3,2,1,0:T(8,128)(2,1)}, f32[2,8,768]{2,1,0:T(8,128)}, f32[4,76...) custom-call(s32[79]{0:T(128)} %concatenate.34.tab, ...), custom_call_target="tpu_custom_call" | custom-call | flops 14495514624 | bytes 29360128 | tf_op jit(solution)/shard_map/mlp/pallas_call | solution.py:581
  199.5 2.3 copy.65
  201.8 3.8 all-to-all-start.3
  209.0 8.1 %all-to-all-done.3 = bf16[4,2,256,192]{2,3,1,0:T(8,128)(2,1)S(1)} async-done(((bf16[4,2,256,192]{2,3,1,0:T(8,128)(2,1)}), bf16[4,2,256,192]{2,3,1,0:T(8,128)(2,1)S(1)}, u32[]{:S(2)}, u32[]{:S(2)}) %all-to-all-start.3) | async-done | bytes 786464 | tf_op jit(solution)/shard_map/all_to_all | solution.py:829
  218.4 22.8 %attend_back.1.gt = bf16[2,3,192,1024]{3,2,1,0:T(8,128)(2,1)} custom-call(bf16[2,3,1024,64]{3,2,1,0:T(8,128)(2,1)} %get-tuple-element.34.q, bf16[2,192,1024]{2,1,0:T(8,128)(2,1)} %get-tuple-element.40.kt, bf16[2,3,1024,64]{3,2,1,0:T(8,128)(2,1)} %get-tuple-element.41.v, bf16[2,3,1024,1024]{3,2,1,0:T(8,128)(2,1)} %get-tuple-element.42.probs, ...), custom_call_target="tpu_custom_call" | custom-call | flops 12884901888 | bytes 20971520 | tf_op jit(solution)/shard_map/attend_back/pallas_call | solution.py:249
  241.1 13.0 %qkv_back.1 = (bf16[2,2,256,768]{3,2,1,0:T(8,128)(2,1)}, bf16[2,2,256,768]{3,2,1,0:T(8,128)(2,1)}, f32[2,2,768]{2,1,0:T(2,128)}, bf16[8,3,96,256]{3,2,1,0:T(8,128)(2,1)}) custom-call(s32[9]{0:T(128)} %pad_add_fusion.1.tab, bf16[2,3,192,1024]{3,2,1,0:T(8,128)(2,1)} %attend_back.1.gt, bf16[2,1024,768]{2,1,0:T(8,128)(2,1)} %get-tuple-element.44.first, ...), custom_call_target="tpu_custom_call" | custom-call | flops 4831838208 | bytes 16777216 | tf_op jit(solution)/shard_map/qkv_back/pallas_call | solution.py:354
  254.2 1.6 fusion.30
  257.3 16.8 %all-to-all-start.4 = ((f32[32,1,1824]{2,1,0:T(1,128)}), f32[32,1,1824]{2,1,0:T(1,128)}, u32[]{:S(2)}, u32[]{:S(2)}) async-start(f32[32,1,1824]{2,1,0:T(1,128)} %all_to_all.30), calls=%async_computation.4 | async-start | bytes 491520 | tf_op jit(solution)/shard_map/all_to_all | solution.py:891
  276.9 1.7 collective-permute-start.16
  280.4 4.0 all-to-all-done.4
  284.4 2.2 reduce.6
  286.6 1.7 reshape.318
  288.3 1.7 reduce_sum.97
  296.2 2.2 fusion.31
  301.7 1.9 collective-permute-start.19
  304.4 1.7 add_convert_fusion.1
  306.1 1.7 collective-permute-start.27
  307.8 2.1 add_convert_fusion
  310.5 3.4 collective-permute-done.18
  314.7 8.1 %collective-permute-done.15 = bf16[2,256,768]{2,1,0:T(8,128)(2,1)S(1)} collective-permute-done((bf16[2,256,768]{2,1,0:T(8,128)(2,1)S(1)}, bf16[2,256,768]{2,1,0:T(8,128)(2,1)S(1)}, u32[]{:S(2)}, u32[]{:S(2)}) %collective-permute-start.15) | collective-permute-done | bytes 786464 | tf_op jit(solution)/shard_map/ppermute | solution.py:659
  323.6 18.2 %collective-permute-done.27 = bf16[2,4,96,768]{3,2,1,0:T(8,128)(2,1)S(1)} collective-permute-done((bf16[2,4,96,768]{3,2,1,0:T(8,128)(2,1)S(1)}, bf16[2,4,96,768]{3,2,1,0:T(8,128)(2,1)S(1)}, u32[]{:S(2)}, u32[]{:S(2)}) %collective-permute-start.27) | collective-permute-done | bytes 1179680 | tf_op jit(solution)/shard_map/ppermute | solution.py:659
  343.4 23.7 %collective-permute-done.21 = bf16[2,4,96,960]{3,2,1,0:T(8,128)(2,1)S(1)} collective-permute-done((bf16[2,4,96,960]{3,2,1,0:T(8,128)(2,1)S(1)}, bf16[2,4,96,960]{3,2,1,0:T(8,128)(2,1)S(1)}, u32[]{:S(2)}, u32[]{:S(2)}) %collective-permute-start.21) | collective-permute-done | bytes 1474592 | tf_op jit(solution)/shard_map/ppermute | solution.py:659
  367.1 1.7 fusion.10
  369.0 1.7 fusion.8
  372.8 1.6 collective-permute-start.30
  374.3 2.5 collective-permute-start.31
  376.9 3.9 collective-permute-done.22
  380.8 1.8 fusion.48
  384.5 2.8 collective-permute-start.25
  388.2 2.2 collective-permute-done.23
  390.4 3.7 collective-permute-done.24
  (206 shorter events, 54.7 us)
Async XLA Ops:
  7.2 53.6 %copy-start = (bf16[128,576]{0,1:T(8,128)(2,1)S(1)}, bf16[128,576]{0,1:T(8,128)(2,1)}, u32[]{:S(2)}) copy-start(bf16[128,576]{0,1:T(8,128)(2,1)} %param.41) | copy-start | bytes 442372
  7.2 9.7 %copy-start.10 = (bf16[3,96,192]{2,1,0:T(8,128)(2,1)S(1)}, bf16[3,96,192]{2,1,0:T(8,128)(2,1)}, u32[]{:S(2)}) copy-start(bf16[3,96,192]{2,1,0:T(8,128)(2,1)} %param.33) | copy-start | bytes 331780
  7.2 11.4 %copy-start.20 = (s32[2]{0:T(128)S(1)}, s32[2]{0:T(128)}, u32[]{:S(2)}) copy-start(s32[2]{0:T(128)} %param.31) | copy-start | bytes 28
  7.2 95.9 %all-gather.2.cloned.1.call-start = ((), (), s32[]{:S(2)}) async-start(), calls=%async_computation.5 | async-start | bytes 3932160 | tf_op jit(solution)/shard_map/all_gather | solution.py:773
  9.9 14.9 %collective-permute-start.4 = (bf16[96,1728]{1,0:T(8,128)(2,1)S(1)}, bf16[96,1728]{1,0:T(8,128)(2,1)S(1)}, u32[]{:S(2)}, u32[]{:S(2)}) collective-permute-start(bf16[96,1728]{1,0:T(8,128)(2,1)S(1)} %get-tuple-element.127), channel_id=1, source_target_pairs={{0,8},{1,9},{2,10},{3,11},{4,12},{5,13},{6,14},{7,15},{8,16},{9,17... | collective-permute-start | bytes 995336 | tf_op jit(solution)/shard_map/ppermute | solution.py:659
  13.0 25.9 %collective-permute-start.5 = (bf16[96,1728]{1,0:T(8,128)(2,1)S(1)}, bf16[96,1728]{1,0:T(8,128)(2,1)S(1)}, u32[]{:S(2)}, u32[]{:S(2)}) collective-permute-start(bf16[96,1728]{1,0:T(8,128)(2,1)S(1)} %get-tuple-element.127), channel_id=1, source_target_pairs={{0,16},{1,17},{2,18},{3,19},{4,20},{5,21},{6,22},{7,23},{8,24},{9,... | collective-permute-start | bytes 995336 | tf_op jit(solution)/shard_map/ppermute | solution.py:659
  15.5 23.3 %collective-permute-start.6 = (bf16[96,1728]{1,0:T(8,128)(2,1)S(1)}, bf16[96,1728]{1,0:T(8,128)(2,1)}, u32[]{:S(2)}, u32[]{:S(2)}) collective-permute-start(bf16[96,1728]{1,0:T(8,128)(2,1)S(1)} %get-tuple-element.127), channel_id=1, source_target_pairs={{0,24},{1,25},{2,26},{3,27},{4,28},{5,29},{6,30},{7,31},{8,0},{9,1... | collective-permute-start | bytes 995336 | tf_op jit(solution)/shard_map/ppermute | solution.py:659
  17.6 43.6 %collective-permute-start = (bf16[3,96,256]{2,1,0:T(8,128)(2,1)}, bf16[3,96,256]{2,1,0:T(8,128)(2,1)S(1)}, u32[]{:S(2)}, u32[]{:S(2)}) collective-permute-start(bf16[3,96,256]{2,1,0:T(8,128)(2,1)} %get-tuple-element.129), channel_id=1, source_target_pairs={{0,8},{1,9},{2,10},{3,11},{4,12},{5,13},{6,14},{7,15},{8,16},{9,17... | collective-permute-start | bytes 442376 | tf_op jit(solution)/shard_map/ppermute | solution.py:659
  18.3 42.9 %collective-permute-start.1 = (bf16[3,96,256]{2,1,0:T(8,128)(2,1)}, bf16[3,96,256]{2,1,0:T(8,128)(2,1)}, u32[]{:S(2)}, u32[]{:S(2)}) collective-permute-start(bf16[3,96,256]{2,1,0:T(8,128)(2,1)} %get-tuple-element.129), channel_id=1, source_target_pairs={{0,16},{1,17},{2,18},{3,19},{4,20},{5,21},{6,22},{7,23},{8,24},{9,... | collective-permute-start | bytes 442376 | tf_op jit(solution)/shard_map/ppermute | solution.py:659
  19.2 36.6 %all-to-all-start = ((s32[8,1,2]{2,1,0:T(1,128)}), s32[8,1,2]{2,1,0:T(1,128)S(1)}, u32[]{:S(2)}, u32[]{:S(2)}) async-start(s32[8,1,2]{2,1,0:T(1,128)} %broadcast_in_dim.65), calls=%async_computation | async-start | bytes 8192 | tf_op jit(solution)/shard_map/all_to_all | solution.py:775
  24.8 36.4 %collective-permute-start.2 = (bf16[3,96,256]{2,1,0:T(8,128)(2,1)}, bf16[3,96,256]{2,1,0:T(8,128)(2,1)}, u32[]{:S(2)}, u32[]{:S(2)}) collective-permute-start(bf16[3,96,256]{2,1,0:T(8,128)(2,1)} %get-tuple-element.129), channel_id=1, source_target_pairs={{0,24},{1,25},{2,26},{3,27},{4,28},{5,29},{6,30},{7,31},{8,0},{9,1... | collective-permute-start | bytes 442376 | tf_op jit(solution)/shard_map/ppermute | solution.py:659
  40.0 61.7 %copy-start.7 = (bf16[4,96,1728]{2,1,0:T(8,128)(2,1)}, bf16[4,96,1728]{2,1,0:T(8,128)(2,1)S(1)}, u32[]{:S(2)}) copy-start(bf16[4,96,1728]{2,1,0:T(8,128)(2,1)S(1)} %pad_maximum_fusion.rest_0_) | copy-start | bytes 3981316
  40.0 18.7 %collective-permute-start.7 = (bf16[4,96,1728]{2,1,0:T(8,128)(2,1)S(1)}, bf16[4,96,1728]{2,1,0:T(8,128)(2,1)}, u32[]{:S(2)}, u32[]{:S(2)}) collective-permute-start(bf16[4,96,1728]{2,1,0:T(8,128)(2,1)S(1)} %pad_maximum_fusion.rest_0_), channel_id=1, source_target_pairs={{0,4},{1,3},{2,6},{3,1},{4,0},{5,7},{6,2},{7,5},{8,12},{9,11},{10,... | collective-permute-start | bytes 3981320 | tf_op jit(solution)/shard_map/ppermute | solution.py:659
  55.9 46.7 %collective-permute-start.8 = (bf16[4,96,1728]{2,1,0:T(8,128)(2,1)S(1)}, bf16[4,96,1728]{2,1,0:T(8,128)(2,1)}, u32[]{:S(2)}, u32[]{:S(2)}) collective-permute-start(bf16[4,96,1728]{2,1,0:T(8,128)(2,1)S(1)} %pad_maximum_fusion.rest_0_), channel_id=1, source_target_pairs={{0,2},{1,5},{2,0},{3,7},{4,6},{5,1},{6,4},{7,3},{8,10},{9,13},{10,... | collective-permute-start | bytes 3981320 | tf_op jit(solution)/shard_map/ppermute | solution.py:659
  58.7 44.4 %collective-permute-start.9 = (bf16[4,96,1728]{2,1,0:T(8,128)(2,1)}, bf16[4,96,1728]{2,1,0:T(8,128)(2,1)}, u32[]{:S(2)}, u32[]{:S(2)}) collective-permute-start(bf16[4,96,1728]{2,1,0:T(8,128)(2,1)} %collective-permute-done.7.rest_1_), channel_id=1, source_target_pairs={{0,2},{1,5},{2,0},{3,7},{4,6},{5,1},{6,4},{7,3},{8,10},{9,13},{10,... | collective-permute-start | bytes 3981320 | tf_op jit(solution)/shard_map/ppermute | solution.py:659
  62.2 40.9 %copy-start.9 = (bf16[4,3,96,256]{3,2,1,0:T(8,128)(2,1)}, bf16[4,3,96,256]{3,2,1,0:T(8,128)(2,1)S(1)}, u32[]{:S(2)}) copy-start(bf16[4,3,96,256]{3,2,1,0:T(8,128)(2,1)S(1)} %pad_maximum_fusion.1.w0) | copy-start | bytes 1769476
  62.2 40.9 %collective-permute-start.3 = (bf16[4,3,96,256]{3,2,1,0:T(8,128)(2,1)S(1)}, bf16[4,3,96,256]{3,2,1,0:T(8,128)(2,1)S(1)}, u32[]{:S(2)}, u32[]{:S(2)}) collective-permute-start(bf16[4,3,96,256]{3,2,1,0:T(8,128)(2,1)S(1)} %pad_maximum_fusion.1.w0), channel_id=1, source_target_pairs={{0,4},{1,5},{2,6},{3,7},{4,0},{5,1},{6,2},{7,3},{8,12},{9,13},{10,... | collective-permute-start | bytes 1769480 | tf_op jit(solution)/shard_map/ppermute | solution.py:659
  65.0 35.1 %all-to-all-start.1 = ((f32[8,1,1824]{2,1,0:T(1,128)}), f32[8,1,1824]{2,1,0:T(1,128)S(1)}, u32[]{:S(2)}, u32[]{:S(2)}) async-start(f32[8,1,1824]{2,1,0:T(1,128)} %all_to_all.25), calls=%async_computation.1 | async-start | bytes 122880 | tf_op jit(solution)/shard_map/all_to_all | solution.py:791
  101.7 60.6 %collective-permute-start.10 = (bf16[4,96,1728]{2,1,0:T(8,128)(2,1)S(1)}, bf16[4,96,1728]{2,1,0:T(8,128)(2,1)}, u32[]{:S(2)}, u32[]{:S(2)}) collective-permute-start(bf16[4,96,1728]{2,1,0:T(8,128)(2,1)S(1)} %pad_maximum_fusion.rest_0_), channel_id=1, source_target_pairs={{0,1},{1,0},{2,3},{3,2},{4,5},{5,4},{6,7},{7,6},{8,9},{9,8},{10,11... | collective-permute-start | bytes 3981320 | tf_op jit(solution)/shard_map/ppermute | solution.py:659
  102.6 59.7 %collective-permute-start.11 = (bf16[4,96,1728]{2,1,0:T(8,128)(2,1)}, bf16[4,96,1728]{2,1,0:T(8,128)(2,1)}, u32[]{:S(2)}, u32[]{:S(2)}) collective-permute-start(bf16[4,96,1728]{2,1,0:T(8,128)(2,1)} %collective-permute-done.7.rest_1_), channel_id=1, source_target_pairs={{0,1},{1,0},{2,3},{3,2},{4,5},{5,4},{6,7},{7,6},{8,9},{9,8},{10,11... | collective-permute-start | bytes 3981320 | tf_op jit(solution)/shard_map/ppermute | solution.py:659
  102.6 59.7 %collective-permute-start.12 = (bf16[4,96,1728]{2,1,0:T(8,128)(2,1)}, bf16[4,96,1728]{2,1,0:T(8,128)(2,1)}, u32[]{:S(2)}, u32[]{:S(2)}) collective-permute-start(bf16[4,96,1728]{2,1,0:T(8,128)(2,1)} %collective-permute-done.8.rest_2_), channel_id=1, source_target_pairs={{0,1},{1,0},{2,3},{3,2},{4,5},{5,4},{6,7},{7,6},{8,9},{9,8},{10,11... | collective-permute-start | bytes 3981320 | tf_op jit(solution)/shard_map/ppermute | solution.py:659
  103.1 59.2 %collective-permute-start.13 = (bf16[4,96,1728]{2,1,0:T(8,128)(2,1)}, bf16[4,96,1728]{2,1,0:T(8,128)(2,1)}, u32[]{:S(2)}, u32[]{:S(2)}) collective-permute-start(bf16[4,96,1728]{2,1,0:T(8,128)(2,1)} %collective-permute-done.9.rest_3_), channel_id=1, source_target_pairs={{0,1},{1,0},{2,3},{3,2},{4,5},{5,4},{6,7},{7,6},{8,9},{9,8},{10,11... | collective-permute-start | bytes 3981320 | tf_op jit(solution)/shard_map/ppermute | solution.py:659
  145.6 15.3 %all-to-all-start.2 = ((bf16[4,2,256,192]{2,3,1,0:T(8,128)(2,1)}), bf16[4,2,256,192]{2,3,1,0:T(8,128)(2,1)S(1)}, u32[]{:S(2)}, u32[]{:S(2)}) async-start(bf16[4,2,256,192]{2,3,1,0:T(8,128)(2,1)} %copy.62), calls=%async_computation.2 | async-start | bytes 1572864 | tf_op jit(solution)/shard_map/all_to_all | solution.py:814
  201.8 15.3 %all-to-all-start.3 = ((bf16[4,2,256,192]{2,3,1,0:T(8,128)(2,1)}), bf16[4,2,256,192]{2,3,1,0:T(8,128)(2,1)S(1)}, u32[]{:S(2)}, u32[]{:S(2)}) async-start(bf16[4,2,256,192]{2,3,1,0:T(8,128)(2,1)} %copy.65), calls=%async_computation.3 | async-start | bytes 1572864 | tf_op jit(solution)/shard_map/all_to_all | solution.py:829
  208.4 95.5 %collective-permute-start.26 = (bf16[16,96,768]{2,1,0:T(8,128)(2,1)}, bf16[16,96,768]{2,1,0:T(8,128)(2,1)}, u32[]{:S(2)}, u32[]{:S(2)}) collective-permute-start(bf16[16,96,768]{2,1,0:T(8,128)(2,1)} %get-tuple-element.52), channel_id=1, source_target_pairs={{0,1},{1,0},{2,3},{3,2},{4,5},{5,4},{6,7},{7,6},{8,9},{9,8},{10,11... | collective-permute-start | bytes 7077896 | tf_op jit(solution)/shard_map/ppermute | solution.py:659
  208.7 97.4 %collective-permute-start.20 = (bf16[16,96,960]{2,1,0:T(8,128)(2,1)}, bf16[16,96,960]{2,1,0:T(8,128)(2,1)}, u32[]{:S(2)}, u32[]{:S(2)}) collective-permute-start(bf16[16,96,960]{2,1,0:T(8,128)(2,1)} %get-tuple-element.50), channel_id=1, source_target_pairs={{0,1},{1,0},{2,3},{3,2},{4,5},{5,4},{6,7},{7,6},{8,9},{9,8},{10,11... | collective-permute-start | bytes 8847368 | tf_op jit(solution)/shard_map/ppermute | solution.py:659
  241.1 13.0 %copy-start.14 = (f32[2,8,768]{2,1,0:T(8,128)S(1)}, f32[2,8,768]{2,1,0:T(8,128)}, u32[]{:S(2)}) copy-start(f32[2,8,768]{2,1,0:T(8,128)} %get-tuple-element.54) | copy-start | bytes 147460
  254.1 21.9 %copy-start.8 = (bf16[8,3,96,256]{3,2,1,0:T(8,128)(2,1)S(1)}, bf16[8,3,96,256]{3,2,1,0:T(8,128)(2,1)}, u32[]{:S(2)}) copy-start(bf16[8,3,96,256]{3,2,1,0:T(8,128)(2,1)} %get-tuple-element.48) | copy-start | bytes 3538948
  257.3 27.1 %all-to-all-start.4 = ((f32[32,1,1824]{2,1,0:T(1,128)}), f32[32,1,1824]{2,1,0:T(1,128)}, u32[]{:S(2)}, u32[]{:S(2)}) async-start(f32[32,1,1824]{2,1,0:T(1,128)} %all_to_all.30), calls=%async_computation.4 | async-start | bytes 491520 | tf_op jit(solution)/shard_map/all_to_all | solution.py:891
  274.1 27.6 %collective-permute-start.14 = (bf16[2,2,256,768]{3,2,1,0:T(8,128)(2,1)}, bf16[2,2,256,768]{3,2,1,0:T(8,128)(2,1)S(1)}, u32[]{:S(2)}, u32[]{:S(2)}) collective-permute-start(bf16[2,2,256,768]{3,2,1,0:T(8,128)(2,1)} %get-tuple-element.47), channel_id=1, source_target_pairs={{0,1},{1,0},{2,3},{3,2},{4,5},{5,4},{6,7},{7,6},{8,9},{9,8},{10,11... | collective-permute-start | bytes 4718600 | tf_op jit(solution)/shard_map/ppermute | solution.py:659
  276.9 21.5 %collective-permute-start.16 = (bf16[4,3,96,256]{3,2,1,0:T(8,128)(2,1)}, bf16[4,3,96,256]{3,2,1,0:T(8,128)(2,1)}, u32[]{:S(2)}, u32[]{:S(2)}) collective-permute-start(bf16[4,3,96,256]{3,2,1,0:T(8,128)(2,1)} %slice.196), channel_id=1, source_target_pairs={{0,4},{1,5},{2,6},{3,7},{4,0},{5,1},{6,2},{7,3},{8,12},{9,13},{10,... | collective-permute-start | bytes 1769480 | tf_op jit(solution)/shard_map/ppermute | solution.py:659
  299.8 10.1 %collective-permute-start.17 = (bf16[3,96,256]{2,1,0:T(8,128)(2,1)S(1)}, bf16[3,96,256]{2,1,0:T(8,128)(2,1)S(1)}, u32[]{:S(2)}, u32[]{:S(2)}) collective-permute-start(bf16[3,96,256]{2,1,0:T(8,128)(2,1)S(1)} %get-tuple-element.123), channel_id=1, source_target_pairs={{0,8},{1,9},{2,10},{3,11},{4,12},{5,13},{6,14},{7,15},{8,16},{9,17... | collective-permute-start | bytes 442376 | tf_op jit(solution)/shard_map/ppermute | solution.py:659
  300.8 13.1 %collective-permute-start.18 = (bf16[3,96,256]{2,1,0:T(8,128)(2,1)S(1)}, bf16[3,96,256]{2,1,0:T(8,128)(2,1)S(1)}, u32[]{:S(2)}, u32[]{:S(2)}) collective-permute-start(bf16[3,96,256]{2,1,0:T(8,128)(2,1)S(1)} %get-tuple-element.125), channel_id=1, source_target_pairs={{0,16},{1,17},{2,18},{3,19},{4,20},{5,21},{6,22},{7,23},{8,24},{9,... | collective-permute-start | bytes 442376 | tf_op jit(solution)/shard_map/ppermute | solution.py:659
  301.7 12.1 %collective-permute-start.19 = (bf16[3,96,256]{2,1,0:T(8,128)(2,1)S(1)}, bf16[3,96,256]{2,1,0:T(8,128)(2,1)S(1)}, u32[]{:S(2)}, u32[]{:S(2)}) collective-permute-start(bf16[3,96,256]{2,1,0:T(8,128)(2,1)S(1)} %get-tuple-element.124), channel_id=1, source_target_pairs={{0,24},{1,25},{2,26},{3,27},{4,28},{5,29},{6,30},{7,31},{8,0},{9,1... | collective-permute-start | bytes 442376 | tf_op jit(solution)/shard_map/ppermute | solution.py:659
  303.9 18.9 %collective-permute-start.15 = (bf16[2,256,768]{2,1,0:T(8,128)(2,1)S(1)}, bf16[2,256,768]{2,1,0:T(8,128)(2,1)S(1)}, u32[]{:S(2)}, u32[]{:S(2)}) collective-permute-start(bf16[2,256,768]{2,1,0:T(8,128)(2,1)S(1)} %fusion.15), channel_id=1, source_target_pairs={{0,2},{1,3},{2,0},{3,1},{4,6},{5,7},{6,4},{7,5},{8,10},{9,11},{10,... | collective-permute-start | bytes 2359304 | tf_op jit(solution)/shard_map/ppermute | solution.py:659
  306.1 35.6 %collective-permute-start.27 = (bf16[2,4,96,768]{3,2,1,0:T(8,128)(2,1)S(1)}, bf16[2,4,96,768]{3,2,1,0:T(8,128)(2,1)S(1)}, u32[]{:S(2)}, u32[]{:S(2)}) collective-permute-start(bf16[2,4,96,768]{3,2,1,0:T(8,128)(2,1)S(1)} %bitcast.123), channel_id=1, source_target_pairs={{0,2},{1,5},{2,0},{3,7},{4,6},{5,1},{6,4},{7,3},{8,10},{9,13},{10,... | collective-permute-start | bytes 3538952 | tf_op jit(solution)/shard_map/ppermute | solution.py:659
  309.9 12.9 %copy-start.11 = (f32[2,1,768]{2,0,1:T(2,128)S(1)}, f32[2,1,768]{2,0,1:T(2,128)}, u32[]{:S(2)}) copy-start(f32[2,1,768]{2,0,1:T(2,128)} %copy.75) | copy-start | bytes 18436
  309.9 12.9 %copy-start.13 = (f32[2,256]{1,0:T(2,128)S(1)}, f32[2,256]{1,0:T(2,128)}, u32[]{:S(2)}) copy-start(f32[2,256]{1,0:T(2,128)} %copy-done.12) | copy-start | bytes 6148
  309.9 12.9 %copy-start.15 = (f32[2,256]{1,0:T(2,128)S(1)}, f32[2,256]{1,0:T(2,128)}, u32[]{:S(2)}) copy-start(f32[2,256]{1,0:T(2,128)} %add_rsqrt_fusion) | copy-start | bytes 6148
  309.9 57.1 %collective-permute-start.21 = (bf16[2,4,96,960]{3,2,1,0:T(8,128)(2,1)S(1)}, bf16[2,4,96,960]{3,2,1,0:T(8,128)(2,1)S(1)}, u32[]{:S(2)}, u32[]{:S(2)}) collective-permute-start(bf16[2,4,96,960]{3,2,1,0:T(8,128)(2,1)S(1)} %bitcast.122), channel_id=1, source_target_pairs={{0,2},{1,5},{2,0},{3,7},{4,6},{5,1},{6,4},{7,3},{8,10},{9,13},{10,... | collective-permute-start | bytes 4423688 | tf_op jit(solution)/shard_map/ppermute | solution.py:659
  343.1 27.6 %collective-permute-start.28 = (bf16[4,96,768]{2,1,0:T(8,128)(2,1)S(1)}, bf16[4,96,768]{2,1,0:T(8,128)(2,1)S(1)}, u32[]{:S(2)}, u32[]{:S(2)}) collective-permute-start(bf16[4,96,768]{2,1,0:T(8,128)(2,1)S(1)} %fusion.13), channel_id=1, source_target_pairs={{0,4},{1,3},{2,6},{3,1},{4,0},{5,7},{6,2},{7,5},{8,12},{9,11},{10,... | collective-permute-start | bytes 1769480 | tf_op jit(solution)/shard_map/ppermute | solution.py:659
  368.7 12.1 %collective-permute-start.22 = (bf16[4,96,960]{2,1,0:T(8,128)(2,1)S(1)}, bf16[4,96,960]{2,1,0:T(8,128)(2,1)S(1)}, u32[]{:S(2)}, u32[]{:S(2)}) collective-permute-start(bf16[4,96,960]{2,1,0:T(8,128)(2,1)S(1)} %fusion.10), channel_id=1, source_target_pairs={{0,4},{1,3},{2,6},{3,1},{4,0},{5,7},{6,2},{7,5},{8,12},{9,11},{10,... | collective-permute-start | bytes 2211848 | tf_op jit(solution)/shard_map/ppermute | solution.py:659
  372.2 12.4 %collective-permute-start.29 = (bf16[96,768]{1,0:T(8,128)(2,1)S(1)}, bf16[96,768]{1,0:T(8,128)(2,1)S(1)}, u32[]{:S(2)}, u32[]{:S(2)}) collective-permute-start(bf16[96,768]{1,0:T(8,128)(2,1)S(1)} %get-tuple-element.120), channel_id=1, source_target_pairs={{0,8},{1,9},{2,10},{3,11},{4,12},{5,13},{6,14},{7,15},{8,16},{9,17... | collective-permute-start | bytes 442376 | tf_op jit(solution)/shard_map/ppermute | solution.py:659
  372.8 14.6 %collective-permute-start.30 = (bf16[96,768]{1,0:T(8,128)(2,1)S(1)}, bf16[96,768]{1,0:T(8,128)(2,1)S(1)}, u32[]{:S(2)}, u32[]{:S(2)}) collective-permute-start(bf16[96,768]{1,0:T(8,128)(2,1)S(1)} %get-tuple-element.122), channel_id=1, source_target_pairs={{0,16},{1,17},{2,18},{3,19},{4,20},{5,21},{6,22},{7,23},{8,24},{9,... | collective-permute-start | bytes 442376 | tf_op jit(solution)/shard_map/ppermute | solution.py:659
  374.3 13.0 %collective-permute-start.31 = (bf16[96,768]{1,0:T(8,128)(2,1)S(1)}, bf16[96,768]{1,0:T(8,128)(2,1)S(1)}, u32[]{:S(2)}, u32[]{:S(2)}) collective-permute-start(bf16[96,768]{1,0:T(8,128)(2,1)S(1)} %get-tuple-element.121), channel_id=1, source_target_pairs={{0,24},{1,25},{2,26},{3,27},{4,28},{5,29},{6,30},{7,31},{8,0},{9,1... | collective-permute-start | bytes 442376 | tf_op jit(solution)/shard_map/ppermute | solution.py:659
  382.6 7.7 %collective-permute-start.23 = (bf16[96,960]{1,0:T(8,128)(2,1)S(1)}, bf16[96,960]{1,0:T(8,128)(2,1)S(1)}, u32[]{:S(2)}, u32[]{:S(2)}) collective-permute-start(bf16[96,960]{1,0:T(8,128)(2,1)S(1)} %get-tuple-element.117), channel_id=1, source_target_pairs={{0,8},{1,9},{2,10},{3,11},{4,12},{5,13},{6,14},{7,15},{8,16},{9,17... | collective-permute-start | bytes 552968 | tf_op jit(solution)/shard_map/ppermute | solution.py:659
  383.3 10.8 %collective-permute-start.24 = (bf16[96,960]{1,0:T(8,128)(2,1)S(1)}, bf16[96,960]{1,0:T(8,128)(2,1)S(1)}, u32[]{:S(2)}, u32[]{:S(2)}) collective-permute-start(bf16[96,960]{1,0:T(8,128)(2,1)S(1)} %get-tuple-element.119), channel_id=1, source_target_pairs={{0,16},{1,17},{2,18},{3,19},{4,20},{5,21},{6,22},{7,23},{8,24},{9,... | collective-permute-start | bytes 552968 | tf_op jit(solution)/shard_map/ppermute | solution.py:659
  384.5 9.5 %collective-permute-start.25 = (bf16[96,960]{1,0:T(8,128)(2,1)S(1)}, bf16[96,960]{1,0:T(8,128)(2,1)S(1)}, u32[]{:S(2)}, u32[]{:S(2)}) collective-permute-start(bf16[96,960]{1,0:T(8,128)(2,1)S(1)} %get-tuple-element.118), channel_id=1, source_target_pairs={{0,24},{1,25},{2,26},{3,27},{4,28},{5,29},{6,30},{7,31},{8,0},{9,1... | collective-permute-start | bytes 552968 | tf_op jit(solution)/shard_map/ppermute | solution.py:659
  (24 other events, 72.7 us)
Sparse Core Ops, SparseCore 0:
  9.6 31.2 all-gather.1

commit v2 on v1

--- a/solution.py
+++ b/solution.py
@@ -143,11 +143,10 @@
     )(tab, tok_all, mod, gain, cos, sin, w0, w1)
 
 
-def attend_kernel(lens, q, k, vt, mixed, probs):
+def attend_kernel(lens, q, k, vt, mixed, probs, *, group):
     heads, seq = k.shape[1], k.shape[2]
     block = q.shape[2]
-    live = lax.broadcasted_iota(jnp.int32, (seq, block), 0) < lens[pl.program_id(0)]
-    parts = []
+    live = lax.broadcasted_iota(jnp.int32, (seq, block), 0) < lens[group]
     for h in range(heads):
         scores = lax.dot_general(k[0, h], q[0, h], NT, preferred_element_type=F32)
         scores = jnp.where(live, scores, MASKED)
@@ -155,44 +154,37 @@
         weights = jnp.exp(scores - largest)
         total = jnp.sum(weights, axis=0, keepdims=True)
         low = (weights * (1.0 / total)).astype(BF)
-        probs[0, h] = low
-        parts.append(
-            jnp.dot(vt[0, h * HEAD : (h + 1) * HEAD, :], low, preferred_element_type=F32)
-        )
-    pad = (-heads * HEAD) % 128
-    if pad:
-        parts.append(jnp.zeros((pad, block), F32))
-    mixed[0, 0] = jnp.concatenate(parts, axis=0).T[:, : heads * HEAD].astype(BF)
-
-
-def attend_call(lens, q, k, vt):
-    groups, heads, seq, _ = q.shape
+        probs[h] = low
+        here = slice(h * HEAD, (h + 1) * HEAD)
+        mixed[0, here, :] = jnp.dot(vt[0, here, :], low, preferred_element_type=F32).astype(BF)
+
+
+def attend_call(group, lens, q, k, vt):
+    _, heads, seq, _ = q.shape
     block = seq // 4
     feats = heads * HEAD
     grid_spec = pltpu.PrefetchScalarGridSpec(
         num_scalar_prefetch=1,
-        grid=(groups, 4),
+        grid=(4,),
         in_specs=[
-            spec((1, heads, block, HEAD), lambda g, j, _: (g, 0, j, 0)),
-            spec((1, heads, seq, HEAD), lambda g, j, _: (g, 0, 0, 0)),
-            spec((1, feats, seq), lambda g, j, _: (g, 0, 0)),
+            spec((1, heads, block, HEAD), lambda j, _: (group, 0, j, 0)),
+            spec((1, heads, seq, HEAD), lambda j, _: (group, 0, 0, 0)),
+            spec((1, feats, seq), lambda j, _: (group, 0, 0)),
         ],
         out_specs=[
-            spec((1, 1, block, feats), lambda g, j, _: (j, g, 0, 0)),
-            spec((1, heads, seq, block), lambda g, j, _: (g, 0, 0, j)),
+            spec((1, feats, block), lambda j, _: (j, 0, 0)),
+            spec((heads, seq, block), lambda j, _: (0, 0, j)),
         ],
     )
     return pl.pallas_call(
-        attend_kernel,
+        functools.partial(attend_kernel, group=group),
         grid_spec=grid_spec,
         out_shape=[
-            jax.ShapeDtypeStruct((4, groups, block, feats), BF),
-            jax.ShapeDtypeStruct((groups, heads, seq, seq), BF),
+            jax.ShapeDtypeStruct((4, feats, block), BF),
+            jax.ShapeDtypeStruct((heads, seq, seq), BF),
         ],
         compiler_params=params(),
-        cost_estimate=cost(
-            16 * groups * heads * seq * seq * HEAD, 20 * 2**20, groups * heads * seq * seq
-        ),
+        cost_estimate=cost(16 * heads * seq * seq * HEAD, 10 * 2**20, heads * seq * seq),
         name="attend",
     )(lens, q, k, vt)
 
@@ -200,7 +192,7 @@
 def attend_back_kernel(q, kt, v, probs, gm, cos, sin, out, dk, dv):
     heads, block = q.shape[1], q.shape[2]
     half = HEAD // 2
-    j = pl.program_id(1)
+    j = pl.program_id(0)
 
     @pl.when(j == 0)
     def _():
@@ -213,66 +205,62 @@
     def store_turned(plane, h, vec, c, s, where):
         low, high = vec[:half], vec[half:]
         base = h * HEAD
-        out[0, plane, base : base + half, where] = (low * c + high * s).astype(BF)
-        out[0, plane, base + half : base + HEAD, where] = (high * c - low * s).astype(BF)
+        out[plane, base : base + half, where] = (low * c + high * s).astype(BF)
+        out[plane, base + half : base + HEAD, where] = (high * c - low * s).astype(BF)
 
     for h in range(heads):
-        tile = h // 2 * 128
-        stop = min(tile + 128, heads * HEAD)
-        part = gm[0, 0, :, tile:stop].astype(F32)
-        if h % 2:
-            part = pltpu.roll(part, HEAD, 1)
-        grad = part[:, :HEAD].astype(BF)
-        low = probs[0, h]
-        dp = lax.dot_general(v[0, h], grad, NT, preferred_element_type=F32)
+        here = slice(h * HEAD, (h + 1) * HEAD)
+        grad = gm[0, here, :]
+        low = probs[h]
+        dp = jnp.dot(v[0, h], grad, preferred_element_type=F32)
         soft = low.astype(F32)
         prod = soft * dp
         inner = jnp.sum(prod, axis=0, keepdims=True)
         ds = (prod - soft * inner).astype(BF)
-        dv[h] += jnp.dot(low, grad, preferred_element_type=F32)
+        dv[h] += lax.dot_general(low, grad, NT, preferred_element_type=F32)
         dk[h] += jnp.dot(ds, q[0, h], preferred_element_type=F32)
-        dq = jnp.dot(kt[0, h * HEAD : (h + 1) * HEAD, :], ds, preferred_element_type=F32)
+        dq = jnp.dot(kt[0, here, :], ds, preferred_element_type=F32)
         store_turned(0, h, dq * (HEAD**-0.5), cos_here, sin_here, columns)
 
-    @pl.when(j == pl.num_programs(1) - 1)
+    @pl.when(j == pl.num_programs(0) - 1)
     def _():
         for h in range(heads):
             store_turned(1, h, dk[h].T, cos[...], sin[...], slice(None))
-            out[0, 2, h * HEAD : (h + 1) * HEAD, :] = dv[h].T.astype(BF)
-
-
-def attend_back_call(q, kt, v, probs, gm, cos, sin):
-    groups, heads, seq, _ = q.shape
+            out[2, h * HEAD : (h + 1) * HEAD, :] = dv[h].T.astype(BF)
+
+
+def attend_back_call(group, q, kt, v, probs, gm, cos, sin):
+    _, heads, seq, _ = q.shape
     block = seq // 4
     feats = heads * HEAD
     half = HEAD // 2
     return pl.pallas_call(
         attend_back_kernel,
-        grid=(groups, 4),
+        grid=(4,),
         in_specs=[
-            spec((1, heads, block, HEAD), lambda g, j: (g, 0, j, 0)),
-            spec((1, feats, seq), lambda g, j: (g, 0, 0)),
-            spec((1, heads, seq, HEAD), lambda g, j: (g, 0, 0, 0)),
-            spec((1, heads, seq, block), lambda g, j: (g, 0, 0, j)),
-            spec((1, 1, block, feats), lambda g, j: (j, g, 0, 0)),
+            spec((1, heads, block, HEAD), lambda j: (group, 0, j, 0)),
+            spec((1, feats, seq), lambda j: (group, 0, 0)),
+            spec((1, heads, seq, HEAD), lambda j: (group, 0, 0, 0)),
+            spec((heads, seq, block), lambda j: (0, 0, j)),
+            spec((1, feats, block), lambda j: (j, 0, 0)),
             whole((half, seq)),
             whole((half, seq)),
         ],
-        out_specs=spec((1, 3, feats, seq), lambda g, j: (g, 0, 0, 0)),
-        out_shape=jax.ShapeDtypeStruct((groups, 3, feats, seq), BF),
+        out_specs=whole((3, feats, seq)),
+        out_shape=jax.ShapeDtypeStruct((3, feats, seq), BF),
         scratch_shapes=[
             pltpu.VMEM((heads, seq, HEAD), F32),
             pltpu.VMEM((heads, seq, HEAD), F32),
         ],
         compiler_params=params(),
-        cost_estimate=cost(32 * groups * heads * seq * seq * HEAD, 20 * 2**20),
+        cost_estimate=cost(32 * heads * seq * seq * HEAD, 10 * 2**20),
         name="attend_back",
     )(q, kt, v, probs, gm, cos, sin)
 
 
-def qkv_back_kernel(tab, gt, first, tok, w, fts, ftk, sums, dw, acc):
+def qkv_back_kernel(tab, gt0, gt1, first, tok, w, fts, ftk, sums, dw, acc):
     i = pl.program_id(0)
-    feats, block = gt.shape[2], gt.shape[3]
+    feats, block = gt0.shape[1], gt0.shape[2]
     wide, width = w.shape[2], w.shape[1]
     rows = dw.shape[2]
     g = lax.rem(i, 2)
@@ -284,7 +272,7 @@
 
     total = None
     for j in range(3):
-        part = gt[0, j]
+        part = jnp.where(g == 0, gt0[j], gt1[j])
         tall = part.astype(F32)
         if wide > feats:
             tall = jnp.concatenate([tall, jnp.zeros((wide - feats, block), F32)], axis=0)
@@ -312,8 +300,9 @@
                 dw[tab[b], j] = flat[b * rows : (b + 1) * rows]
 
 
-def qkv_back_call(tab, gt, first, tok_all, w):
-    groups, _, feats, seq = gt.shape
+def qkv_back_call(tab, gt0, gt1, first, tok_all, w):
+    _, feats, seq = gt0.shape
+    groups = first.shape[0]
     block = seq // 4
     width = first.shape[2]
     wide = w.shape[2]
@@ -326,7 +315,8 @@
         num_scalar_prefetch=1,
         grid=(8,),
         in_specs=[
-            spec((1, 3, feats, block), lambda i, tab: (lax.rem(i, 2), 0, 0, piece(i, tab))),
+            spec((3, feats, block), lambda i, tab: (0, 0, piece(i, tab))),
+            spec((3, feats, block), lambda i, tab: (0, 0, piece(i, tab))),
             spec((1, block, width), lambda i, tab: (lax.rem(i, 2), piece(i, tab), 0)),
             spec((1, block, width), lambda i, tab: (lax.rem(i, 2), piece(i, tab), 0)),
             whole((3, width, wide)),
@@ -363,32 +353,24 @@
         compiler_params=params(),
         cost_estimate=cost(4 * groups * seq * width * wide * 3, 16 * 2**20),
         name="qkv_back",
-    )(tab, gt, first, tok_all, w)
-
-
-def mlp_kernel(
-    tab,
-    tok,
-    cot,
-    mixed,
-    mod,
-    gain,
-    upb,
-    downb,
-    *rest,
-):
-    pieces = rest[:8]
+    )(tab, gt0, gt1, first, tok_all, w)
+
+
+def mlp_kernel(tab, tok, cot, mixed0, mixed1, mod, gain, upb, downb, *rest):
+    up_pieces, down_pieces = rest[:8], rest[8:16]
     (
         out,
         gafter,
-        gmixed,
+        gmixed0,
+        gmixed1,
         sums,
         upsum,
         gu_s,
         gu_k,
         gd_s,
         gd_k,
-        w,
+        wu,
+        wd,
         gu,
         gd,
         after,
@@ -403,45 +385,47 @@
         gsec,
         act,
         gh,
+        sem_u,
         sem_w,
         sem_g,
         sem_d,
-    ) = rest[8:]
+    ) = rest[16:]
+    mixed, gmixed = (mixed0, mixed1), (gmixed0, gmixed1)
     groups, block, width = tok.shape
-    feats = mixed.shape[3]
-    rows = pieces[0].shape[1]
+    feats = mixed0.shape[1]
+    rows = up_pieces[0].shape[1]
     fh = upb.shape[1]
     total_rows = groups * block
     t_part, t_row, t_slot, t_dst = 3, 7, 39, 47
 
-    loads = []
-    for p in range(8):
-        for j in range(4):
-            row = pl.multiple_of(tab[t_row + p * 4 + j] * rows, 16)
-            loads.append(
-                pltpu.make_async_copy(
-                    pieces[p].at[j],
-                    w.at[tab[t_slot + p], pl.ds(row, rows), :],
-                    sem_w.at[p * 4 + j],
+    def loads(sources, target, sem):
+        copies = []
+        for p in range(8):
+            for j in range(4):
+                row = pl.multiple_of(tab[t_row + p * 4 + j] * rows, 16)
+                copies.append(
+                    pltpu.make_async_copy(
+                        sources[p].at[j],
+                        target.at[tab[t_slot + p], pl.ds(row, rows), :],
+                        sem.at[p * 4 + j],
+                    )
                 )
-            )
-    for load in loads:
+        return copies
+
+    down_loads = loads(down_pieces, wd, sem_w)
+    up_loads = loads(up_pieces, wu, sem_u)
+    for load in down_loads + up_loads:
         load.start()
-    for load in loads:
+    for load in down_loads:
         load.wait()
 
-    def span(g):
-        return pl.ds(pl.multiple_of(g * block, block), block)
-
-    def prepare(g, _):
-        here = span(g)
+    for g in range(groups):
+        here = slice(g * block, (g + 1) * block)
         total = jnp.zeros((block, width), F32)
         for k in range(4):
+            rows_mixed = mixed[g][tab[t_part + k]].T
             total += lax.dot_general(
-                mixed[tab[t_part + k], g],
-                w[k, :, 2 * fh : 2 * fh + feats],
-                NT,
-                preferred_element_type=F32,
+                rows_mixed, wd[k, :, fh : fh + feats], NT, preferred_element_type=F32
             )
         att[here, :] = total
         rows_after = tok[g].astype(F32) + mod[g, 2:3, :] * total
@@ -458,71 +442,53 @@
         sums[g, 4:5, :] = jnp.sum(gb.astype(F32), axis=0, keepdims=True)
         branch[here, :] = jnp.broadcast_to(downb[...], (block, width))
         gsec[here, :] = jnp.zeros((block, width), F32)
-        return 0
-
-    lax.fori_loop(0, groups, prepare, 0)
     second_t[...] = second[...].T
     gbr_t[...] = gbr[...].T
+    for load in up_loads:
+        load.wait()
 
     c1, c3 = math.sqrt(2.0 / math.pi), 0.044715
 
-    def store_grads(k, src, send, keep, sem):
+    def store_grads(k, src, sent, kept, sem):
         for b in range(NBLK):
             there = tab[t_dst + k * NBLK + b]
             piece = src.at[k, pl.ds(b * rows, rows), :]
 
             @pl.when(k < 2)
             def _():
-                pltpu.make_async_copy(piece, keep.at[there], sem.at[k, b]).start()
+                pltpu.make_async_copy(piece, kept.at[there], sem.at[k, b]).start()
 
             @pl.when(k >= 2)
             def _():
-                pltpu.make_async_copy(piece, send.at[there], sem.at[k, b]).start()
+                pltpu.make_async_copy(piece, sent.at[there], sem.at[k, b]).start()
 
     def slot(k, _):
         part = tab[t_part + k]
         bias = upb[pl.ds(part, 1), :]
 
-        def half(g, total):
-            here = span(g)
-            hidden = jnp.dot(second[here, :], w[k, :, :fh], preferred_element_type=F32) + bias
-            square = hidden * hidden
-            th = jnp.tanh(c1 * hidden * (1.0 + c3 * square))
-            up = 0.5 * (1.0 + th)
-            active = (hidden * up).astype(BF)
-            act[here, :] = active
-            slope = up + (0.5 * c1) * hidden * (1.0 - th * th) * (1.0 + (3.0 * c3) * square)
-            branch[here, :] += lax.dot_general(
-                active, w[k, :, fh : 2 * fh], NT, preferred_element_type=F32
-            )
-            ga = jnp.dot(gbr[here, :], w[k, :, fh : 2 * fh], preferred_element_type=F32)
-            grad = (ga * slope).astype(BF)
-            gh[here, :] = grad
-            gsec[here, :] += lax.dot_general(
-                grad, w[k, :, :fh], NT, preferred_element_type=F32
-            )
-            return total + jnp.sum(grad.astype(F32), axis=0, keepdims=True)
-
-        upsum[pl.ds(part, 1), :] = lax.fori_loop(0, groups, half, jnp.zeros((1, fh), F32))
-
-        def grads(r, _):
-            these = pl.ds(pl.multiple_of(r * 256, 256), 256)
-            gu[k, these, :] = jnp.dot(
-                second_t[these, :], gh[...], preferred_element_type=F32
-            ).astype(BF)
-            gd[k, these, :fh] = jnp.dot(
-                gbr_t[these, :], act[...], preferred_element_type=F32
-            ).astype(BF)
-            return 0
-
-        lax.fori_loop(0, width // 256, grads, 0)
+        hidden = jnp.dot(second[...], wu[k], preferred_element_type=F32) + bias
+        square = hidden * hidden
+        th = jnp.tanh(c1 * hidden * (1.0 + c3 * square))
+        up = 0.5 * (1.0 + th)
+        act[...] = (hidden * up).astype(BF)
+        slope = up + (0.5 * c1) * hidden * (1.0 - th * th) * (1.0 + (3.0 * c3) * square)
+        ga = jnp.dot(gbr[...], wd[k, :, :fh], preferred_element_type=F32)
+        grad = (ga * slope).astype(BF)
+        gh[...] = grad
+        upsum[pl.ds(part, 1), :] = jnp.sum(grad.astype(F32), axis=0, keepdims=True)
+        branch[...] += lax.dot_general(
+            act[...], wd[k, :, :fh], NT, preferred_element_type=F32
+        )
+        gsec[...] += lax.dot_general(gh[...], wu[k], NT, preferred_element_type=F32)
+        gu[k] = jnp.dot(second_t[...], gh[...], preferred_element_type=F32).astype(BF)
+        gd[k, :, :fh] = jnp.dot(gbr_t[...], act[...], preferred_element_type=F32).astype(BF)
         store_grads(k, gu, gu_s, gu_k, sem_g)
         return 0
 
     lax.fori_loop(0, 4, slot, 0)
 
-    def finish(g, _):
-        here = span(g)
+    for g in range(groups):
+        here = slice(g * block, (g + 1) * block)
         position = tab[2] + lax.broadcasted_iota(jnp.int32, (block, width), 0)
         grad_y = jnp.where(position < tab[g], cot[g].astype(F32), 0.0)
         out[g] = (after[here, :] + mod[g, 5:6, :] * branch[here, :]).astype(BF)
@@ -540,19 +506,24 @@
         low = (mod[g, 2:3, :] * grad).astype(BF)
         gbr[here, :] = low
         for k in range(4):
-            gmixed[tab[t_part + k], g] = jnp.dot(
-                low, w[k, :, 2 * fh : 2 * fh + feats], preferred_element_type=F32
-            ).astype(BF)
-        return 0
-
-    lax.fori_loop(0, groups, finish, 0)
+            gmixed[g][tab[t_part + k]] = (
+                jnp.dot(low, wd[k, :, fh : fh + feats], preferred_element_type=F32)
+                .astype(BF)
+                .T
+            )
     gbr_t[...] = gbr[...].T
 
     def last(k, _):
-        part = mixed[tab[t_part + k]].reshape(total_rows, feats)
-        gd[k, :, fh : fh + feats] = jnp.dot(
-            gbr_t[...], part, preferred_element_type=F32
-        ).astype(BF)
+        part = tab[t_part + k]
+        total = jnp.zeros((width, feats), F32)
+        for g in range(groups):
+            total += lax.dot_general(
+                gbr_t[:, g * block : (g + 1) * block],
+                mixed[g][part],
+                NT,
+                preferred_element_type=F32,
+            )
+        gd[k, :, fh : fh + feats] = total.astype(BF)
         store_grads(k, gd, gd_s, gd_k, sem_d)
         return 0
 
@@ -567,25 +538,26 @@
             ).wait()
 
 
-def mlp_call(tab, tok, cot, mixed, mod, gain, upb, downb, pieces):
+def mlp_call(tab, tok, cot, mixed0, mixed1, mod, gain, upb, downb, up_pieces, down_pieces):
     groups, block, width = tok.shape
-    feats = mixed.shape[3]
+    feats = mixed0.shape[1]
     fh = upb.shape[1]
-    lanes = pieces[0].shape[2]
     rows = width // NBLK
     total = groups * block
     vm = pl.BlockSpec(memory_space=pltpu.VMEM)
     sm = pl.BlockSpec(memory_space=pltpu.SMEM)
     up = jax.ShapeDtypeStruct((16, rows, fh), BF)
     down = jax.ShapeDtypeStruct((16, rows, fh + feats), BF)
+    turned = jax.ShapeDtypeStruct((4, feats, block), BF)
     return pl.pallas_call(
         mlp_kernel,
-        in_specs=[sm] + [vm] * 7 + [ANY] * 8,
-        out_specs=[vm] * 5 + [ANY] * 4,
+        in_specs=[sm] + [vm] * 8 + [ANY] * 16,
+        out_specs=[vm] * 6 + [ANY] * 4,
         out_shape=[
             jax.ShapeDtypeStruct((groups, block, width), BF),
             jax.ShapeDtypeStruct((groups, block, width), F32),
-            jax.ShapeDtypeStruct((4, groups, block, feats), BF),
+            turned,
+            turned,
             jax.ShapeDtypeStruct((groups, 8, width), F32),
             jax.ShapeDtypeStruct((4, fh), F32),
             up,
@@ -594,7 +566,8 @@
             down,
         ],
         scratch_shapes=[
-            pltpu.VMEM((4, width, lanes), BF),
+            pltpu.VMEM((4, width, fh), BF),
+            pltpu.VMEM((4, width, fh + feats), BF),
             pltpu.VMEM((4, width, fh), BF),
             pltpu.VMEM((4, width, fh + feats), BF),
             pltpu.VMEM((total, width), F32),
@@ -610,13 +583,72 @@
             pltpu.VMEM((total, fh), BF),
             pltpu.VMEM((total, fh), BF),
             pltpu.SemaphoreType.DMA((32,)),
+            pltpu.SemaphoreType.DMA((32,)),
             pltpu.SemaphoreType.DMA((4, NBLK)),
             pltpu.SemaphoreType.DMA((4, NBLK)),
         ],
         compiler_params=params(),
         cost_estimate=cost(12 * total * width * fh * 4, 28 * 2**20, total * fh * 4),
         name="mlp",
-    )(tab, tok, cot, mixed, mod, gain, upb, downb, *pieces)
+    )(tab, tok, cot, mixed0, mixed1, mod, gain, upb, downb, *up_pieces, *down_pieces)
+
+
+def norm_back_kernel(t0, t1, t2, tok, after, mod, gain, out):
+    normed, inverse = norm_rows(tok[0].astype(F32))
+    grad = t0[0, 0].astype(F32) + t1[0, 0].astype(F32) + t2[0].astype(F32)
+    scaled = grad * (gain[...] * (1.0 + mod[0, 1:2, :]))
+    mean = jnp.mean(scaled, axis=1, keepdims=True)
+    along = jnp.mean(scaled * normed, axis=1, keepdims=True)
+    out[0] = (after[0] + inverse * (scaled - mean - normed * along)).astype(BF)
+
+
+def norm_back_call(t0, t1, t2, tok, after, mod, gain):
+    groups, block, width = tok.shape
+    row = spec((1, block, width), lambda g: (g, 0, 0))
+    near = spec((1, 1, block, width), lambda g: (0, g, 0, 0))
+    return pl.pallas_call(
+        norm_back_kernel,
+        grid=(groups,),
+        in_specs=[near, near, row, row, row, spec((1, 6, width), lambda g: (g, 0, 0)), whole((1, width))],
+        out_specs=row,
+        out_shape=jax.ShapeDtypeStruct((groups, block, width), BF),
+        compiler_params=params(),
+        cost_estimate=cost(40 * groups * block * width, 12 * groups * block * width),
+        name="norm_back",
+    )(t0, t1, t2, tok, after, mod, gain)
+
+
+AT = 640
+
+
+def small_kernel(got, cond_t, adaw, adab, upb, downb, gain_one, gain_two):
+    dp = got.shape[0]
+    cols = adaw.shape[1]
+    total = jnp.sum(got[...], axis=1)
+    mods = jnp.concatenate([total[:, 0, :], total[:, 1, :]], axis=0)
+    product = jnp.dot(
+        cond_t[...], mods, precision=lax.Precision.HIGHEST, preferred_element_type=F32
+    )
+    adaw[...] = product[:, :cols]
+    flat = jnp.sum(total, axis=0)
+    adab[...] = flat[0:1, :cols] + flat[1:2, :cols]
+    upb[...] = flat[2:3, : upb.shape[1]]
+    for row, ref in enumerate((downb, gain_one, gain_two)):
+        ref[...] = flat[row : row + 1, AT : AT + ref.shape[1]]
+
+
+def small_call(got, cond_t, cols, up_count, count):
+    shapes = [(cond_t.shape[0], cols), (1, cols), (1, up_count)] + [(1, count)] * 3
+    vm = pl.BlockSpec(memory_space=pltpu.VMEM)
+    return pl.pallas_call(
+        small_kernel,
+        in_specs=[vm, vm],
+        out_specs=[vm] * 6,
+        out_shape=[jax.ShapeDtypeStruct(shape, F32) for shape in shapes],
+        compiler_params=params(),
+        cost_estimate=cost(2**20, 2**20),
+        name="small",
+    )(got, cond_t)
 
 
 def time_embedding(time_steps, width_total):
@@ -659,31 +691,52 @@
     return lax.ppermute(array, ("dp", "tensor"), pairs)
 
 
+def start_z(shard):
+    return [shard] + [send(shard, ALONG_Z[s]) for s in (1, 2, 3)]
+
+
 def gather_z(shard):
-    parts = [shard] + [send(shard, ALONG_Z[s]) for s in (1, 2, 3)]
-    return jnp.stack(parts)
-
-
-def reduce_chunk(sent, kept):
-    shape = (2, 2, 4) + sent.shape[1:]
-    kept = kept.reshape(shape)
-    got = send(sent, CORE).reshape(shape)
-    first_half = (kept[1].astype(F32) + got[1].astype(F32)).astype(BF)
-    got_two = send(first_half, SECOND)
-    second_half = (
-        kept[0, 1].astype(F32) + got[0, 1].astype(F32) + got_two[1].astype(F32)
-    ).astype(BF)
-    got_three = send(second_half, FIRST)
-    summed = (
-        kept[0, 0].astype(F32)
-        + got[0, 0].astype(F32)
-        + got_two[0].astype(F32)
-        + got_three.astype(F32)
-    )
-    result = summed[0]
-    for s in (1, 2, 3):
-        result = result + send(summed[s].astype(BF), ALONG_Z[s]).astype(F32)
-    return result
+    return jnp.stack(start_z(shard))
+
+
+def after_all(value, *others):
+    flat, tree = jax.tree.flatten(value)
+    tied = lax.optimization_barrier((tuple(flat), others))[0]
+    return jax.tree.unflatten(tree, tied)
+
+
+def add_low(*terms):
+    return functools.reduce(jnp.add, [term.astype(F32) for term in terms]).astype(BF)
+
+
+class Reduce:
+    def __init__(self, sent, kept):
+        shape = (2, 2, 4) + sent.shape[1:]
+        self.kept = kept.reshape(shape)
+        self.got = send(sent, CORE).reshape(shape)
+
+    def one(self):
+        self.half = add_low(self.kept[1], self.got[1])
+        return self.half
+
+    def two(self):
+        self.got_two = send(self.half, SECOND)
+        self.quarter = add_low(self.kept[0, 1], self.got[0, 1], self.got_two[1])
+        return self.quarter
+
+    def three(self):
+        got_three = send(self.quarter, FIRST)
+        self.parts = [
+            add_low(self.kept[0, 0, s], self.got[0, 0, s], self.got_two[0, s], got_three[s])
+            for s in range(4)
+        ]
+        return self.parts
+
+    def last(self, *others):
+        got = [send(self.parts[s], ALONG_Z[s]) for s in (1, 2, 3)]
+        if others:
+            got = after_all(got, *others)
+        return functools.reduce(jnp.add, [g.astype(F32) for g in [self.parts[0]] + got])
 
 
 def tables(z, y, x, c):
@@ -743,52 +796,35 @@
     here = t if fast else zero
     parts, weight_rows, slots, targets, qkv_rows, qkv_targets = tables(z, y, x, c)
 
+    all_times = lax.all_to_all(
+        jnp.broadcast_to(times[None, :], (dp, groups)), "dp", 0, 0, tiled=True
+    ).reshape(-1)
     pad = (-feats) % 128
     qkv_shard = jnp.pad(w_qkv, ((0, 0), (0, 0), (0, pad)))
-    mlp_shard = jnp.concatenate([w_up, w_down.T, w_out.T], axis=1)
     if fast:
         near = gather_z(qkv_shard)
         qkv_pieces = (near, send(near, FLIP_Y))
-        base = gather_z(mlp_shard)
-        one = send(base, FIRST)
-        two = send(base, SECOND)
-        both = send(one, SECOND)
-        own = (base, one, two, both)
-        pieces = own + tuple(send(piece, CORE) for piece in own)
     else:
         full = lax.all_gather(qkv_shard, "dp", axis=1, tiled=True)
         full = full.reshape(3, NBLK, rows, feats + pad).transpose(1, 0, 2, 3)
         order = [[(-j) % 4 * 2 + p for j in range(4)] for p in range(2)]
         qkv_pieces = tuple(jnp.stack([full[b] for b in order[p]]) for p in range(2))
-        full = lax.all_gather(mlp_shard, "dp", axis=0, tiled=True)
-        full = lax.all_gather(full, "tensor", axis=0, tiled=False)
-        full = full.reshape(tp, NBLK, rows, full.shape[2])
-        pieces = []
-        for far in range(2):
-            for rel_x, rel_y in ((0, 0), (far, 1 - far), (1 - far, far), (1, 1)):
-                pieces.append(
-                    jnp.stack([full[rel_x * 2 + far, b] for b in order[rel_y]])
-                )
-        pieces = tuple(pieces)
     tok_all = lax.all_gather(tokens, "tensor", axis=1, tiled=True)
 
-    all_times = lax.all_to_all(
-        jnp.broadcast_to(times[None, :], (dp, groups)), "dp", 0, 0, tiled=True
-    ).reshape(-1)
     condition = time_embedding(all_times, ada_weight.shape[0])
     part = jnp.dot(
         condition, ada_weight.astype(F32), precision=lax.Precision.HIGHEST
     ) + ada_bias.astype(F32)
     cols = part.shape[1]
     vectors = jnp.concatenate([up_bias, down_bias, norm1_gain, norm2_gain]).astype(F32)
-    payload = jnp.concatenate(
+    sent_mod = jnp.concatenate(
         [
             part.reshape(dp, groups * cols),
             jnp.broadcast_to(vectors[None, :], (dp, vectors.shape[0])),
         ],
         axis=1,
     )
-    payload = lax.all_to_all(payload, "dp", 0, 0, tiled=True)
+    payload = lax.all_to_all(sent_mod, "dp", 0, 0, tiled=True)
     mod = (
         payload[:, : groups * cols]
         .reshape(dp, groups, cols)
@@ -803,6 +839,24 @@
     upb_all = small[0].reshape(tp, fh)
     downb_all, gain_one, gain_two = (v.reshape(1, width) for v in small[1:])
 
+    up_shard = w_up
+    down_shard = jnp.concatenate([w_down.T, w_out.T], axis=1)
+    if fast:
+        up_shard, down_shard = after_all((up_shard, down_shard), qkv_pieces[1], payload)
+        up_parts = start_z(up_shard)
+        down_parts = start_z(down_shard)
+    else:
+
+        def gather_pieces(shard):
+            full = lax.all_gather(shard, "dp", axis=0, tiled=True)
+            full = lax.all_gather(full, "tensor", axis=0, tiled=False)
+            full = full.reshape(tp, NBLK, rows, full.shape[2])
+            return [
+                jnp.stack([full[rel_x * 2 + far, b] for b in order[rel_y]])
+                for far in range(2)
+                for rel_x, rel_y in ((0, 0), (far, 1 - far), (1 - far, far), (1, 1))
+            ]
+
     cos, sin = rotary_halves(seq)
     heads_wide = (feats + pad) // HEAD
     cos_wide = jnp.tile(jnp.concatenate([cos, cos], axis=1), (1, heads_wide))
@@ -810,8 +864,31 @@
     first_all, q, k, v, kt, vt, w_all = qkv_call(
         qkv_rows.astype(jnp.int32), tok_all, mod, gain_one, cos_wide, sin_wide, *qkv_pieces
     )
-    mixed, probs = attend_call(lengths, q, k, vt)
-    mixed = lax.all_to_all(mixed, "tensor", 0, 0, tiled=True)
+    vt_later = vt
+    if fast:
+        up_near = jnp.stack(after_all(up_parts, vt))
+        vt = after_all(vt, up_near)
+        up_one, up_two = send(up_near, FIRST), send(up_near, SECOND)
+    mixed0, probs0 = attend_call(0, lengths, q, k, vt)
+    mixed0_all = lax.all_to_all(mixed0, "tensor", 0, 0, tiled=True)
+    if fast:
+        down_near = jnp.stack(after_all(down_parts, mixed0))
+        up_near, up_one, up_two = after_all((up_near, up_one, up_two), mixed0)
+        vt_later = after_all(vt, down_near, up_one, up_two)
+        up_both = send(up_one, SECOND)
+        own = (up_near, up_one, up_two, up_both)
+        down_one, down_two = send(down_near, FIRST), send(down_near, SECOND)
+    mixed1, probs1 = attend_call(1, lengths, q, k, vt_later)
+    if fast:
+        down_near, down_one, down_two = after_all((down_near, down_one, down_two), mixed1)
+    mixed1_all = lax.all_to_all(after_all(mixed1, mixed0_all), "tensor", 0, 0, tiled=True)
+    if fast:
+        down_both = send(down_one, SECOND)
+        up_pieces = own + tuple(send(piece, CORE) for piece in own)
+        own = (down_near, down_one, down_two, down_both)
+        down_pieces = own + tuple(send(piece, CORE) for piece in own)
+    else:
+        up_pieces, down_pieces = gather_pieces(up_shard), gather_pieces(down_shard)
 
     tab = jnp.concatenate(
         [
@@ -823,30 +900,56 @@
             targets,
         ]
     ).astype(jnp.int32)
-    out, grad_after, grad_mixed, sums, upsum, gu_s, gu_k, gd_s, gd_k = mlp_call(
-        tab, tokens, cotangent, mixed, mod, gain_two, upb_all, downb_all, pieces
-    )
-    grad_mixed = lax.all_to_all(grad_mixed, "tensor", 0, 0, tiled=True)
-    grad_t = attend_back_call(q, kt, v, probs, grad_mixed, cos.T, sin.T)
+    out, grad_after, gm0, gm1, sums, upsum, gu_s, gu_k, gd_s, gd_k = mlp_call(
+        tab,
+        tokens,
+        cotangent,
+        mixed0_all,
+        mixed1_all,
+        mod,
+        gain_two,
+        upb_all,
+        downb_all,
+        up_pieces,
+        down_pieces,
+    )
+    gm0 = lax.all_to_all(gm0, "tensor", 0, 0, tiled=True)
+    gm1 = lax.all_to_all(after_all(gm1, gm0), "tensor", 0, 0, tiled=True)
+    if fast:
+        up_sum = Reduce(gu_s, gu_k)
+        down_sum = Reduce(after_all(gd_s, up_sum.got), gd_k)
+        up_sum.got = after_all(up_sum.got, gm0)
+        gm0 = after_all(gm0, up_sum.one())
+    grad_t0 = attend_back_call(0, q, kt, v, probs0, gm0, cos.T, sin.T)
+    if fast:
+        gm1 = after_all(gm1, grad_t0, up_sum.two(), down_sum.one())
+    grad_t1 = attend_back_call(1, q, kt, v, probs1, gm1, cos.T, sin.T)
+    if fast:
+        grad_t1 = after_all(grad_t1, down_sum.two(), *up_sum.three())
     fts, ftk, sums_one, dw = qkv_back_call(
         jnp.concatenate([qkv_targets, here.reshape(1)]).astype(jnp.int32),
-        grad_t,
+        grad_t0,
+        grad_t1,
         first_all,
         tok_all,
         w_all,
     )
 
     if fast:
-        sum_up = reduce_chunk(gu_s, gu_k)
-        sum_down = reduce_chunk(gd_s, gd_k)
-        near, far = dw[:4], dw[4:]
-        near = near.astype(F32) + send(far, FLIP_Y).astype(F32)
-        sum_qkv = near[0]
-        for s in (1, 2, 3):
-            sum_qkv = sum_qkv + send(near[s].astype(BF), ALONG_Z[s]).astype(F32)
+        sum_up = up_sum.last()
         got = send(fts, CORE)
-        far = (ftk[1].astype(F32) + got[1].astype(F32)).astype(BF)
-        grad_first = ftk[0].astype(F32) + got[0].astype(F32) + send(far, FLIP_X).astype(F32)
+        far = send(add_low(ftk[1], got[1]), FLIP_X)
+        grad_in = norm_back_call(ftk, got, far, tokens, grad_after, mod, gain_one)
+        got_dw = send(dw[4:], FLIP_Y)
+        dw_parts = [add_low(dw[s], got_dw[s]) for s in range(4)]
+        last_parts = down_sum.three()
+        sum_down = down_sum.last(grad_in)
+        sum_qkv = functools.reduce(
+            jnp.add,
+            [dw_parts[0].astype(F32)]
+            + [send(dw_parts[s], ALONG_Z[s]).astype(F32) for s in (1, 2, 3)],
+        )
+        ready = last_parts[0][:8, :128].astype(F32)
     else:
 
         def absolute(sent, kept):
@@ -869,58 +972,57 @@
         sum_qkv = lax.psum_scatter(terms, "dp", scatter_dimension=1, tiled=True)
         terms = jnp.stack([ftk, fts], axis=1).reshape(tp, groups, block, width).astype(F32)
         grad_first = lax.psum_scatter(terms, "tensor", scatter_dimension=0, tiled=True)[0]
-
-    p_one, q_one = sums_one[:, 0], sums_one[:, 1]
-    p_two, q_two = sums[:, 0], sums[:, 1]
+        nought = jnp.zeros_like(grad_first)
+        grad_in = norm_back_call(
+            grad_first[None], nought[None], nought, tokens, grad_after, mod, gain_one
+        )
+        ready = sum_up
+
+    q_one, q_two = sums_one[:, 1], sums[:, 1]
     grad_mod = jnp.stack(
-        [p_one, gain_one * q_one, sums[:, 3], p_two, gain_two * q_two, sums[:, 2]], axis=1
-    )
-    grad_mod = grad_mod.reshape(groups, dp, cols).transpose(1, 0, 2).reshape(dp, groups * cols)
-    payload = jnp.concatenate(
+        [sums_one[:, 0], gain_one * q_one, sums[:, 3], sums[:, 0], gain_two * q_two, sums[:, 2]],
+        axis=1,
+    )
+    grad_mod = grad_mod.reshape(groups, dp, cols).transpose(1, 0, 2)
+    up_count, count = up_bias.shape[0], down_bias.shape[0]
+    firsts = jnp.concatenate(
         [
-            grad_mod,
-            upsum.reshape(dp, -1),
-            jnp.sum(sums[:, 4], axis=0).reshape(dp, -1),
-            jnp.sum((1.0 + mod[:, 1]) * q_one, axis=0).reshape(dp, -1),
-            jnp.sum((1.0 + mod[:, 4]) * q_two, axis=0).reshape(dp, -1),
+            jnp.pad(grad_mod, ((0, 0), (0, 0), (0, AT - cols))),
+            jnp.pad(upsum.reshape(dp, 1, up_count), ((0, 0), (0, 0), (0, AT - up_count))),
         ],
         axis=1,
     )
-    lanes = payload.shape[1]
-    payload = jnp.broadcast_to(payload[:, None, :], (dp, tp, lanes)).reshape(dp * tp, lanes)
+    seconds = jnp.stack(
+        [
+            jnp.sum(sums[:, 4], axis=0),
+            jnp.sum((1.0 + mod[:, 1]) * q_one, axis=0),
+            jnp.sum((1.0 + mod[:, 4]) * q_two, axis=0),
+        ]
+    )
+    seconds = seconds.reshape(3, dp, count).transpose(1, 0, 2)
+    seconds = jnp.pad(seconds, ((0, 0), (0, 0), (0, width - AT - count)))
+    payload = jnp.concatenate([firsts, seconds], axis=2)
+    payload = jnp.broadcast_to(payload[:, None], (dp, tp, 3, width)).reshape(dp * tp, 3, width)
+    payload = after_all(payload, ready)
     payload = lax.all_to_all(payload, ("dp", "tensor"), 0, 0, tiled=True)
-    payload = jnp.sum(payload.reshape(dp, tp, lanes), axis=1)
-    mods = payload[:, : groups * cols].reshape(dp * groups, cols)
-    grad_adaw = jnp.dot(condition.T, mods, precision=lax.Precision.HIGHEST)
-    grad_adab = jnp.sum(mods, axis=0)
-    vectors = jnp.sum(payload[:, groups * cols :], axis=0)
-    at, small = 0, []
-    for count in (up_bias.shape[0], down_bias.shape[0], norm1_gain.shape[0], norm2_gain.shape[0]):
-        small.append(vectors[at : at + count])
-        at += count
-
-    normed, inverse = (
-        a.reshape(groups, block, -1)
-        for a in norm_rows(tokens.astype(F32).reshape(groups * block, width))
-    )
-    scaled = grad_first * (gain_one * (1.0 + mod[:, 1]))[:, None, :]
-    mean = jnp.mean(scaled, axis=-1, keepdims=True)
-    along = jnp.mean(scaled * normed, axis=-1, keepdims=True)
-    grad_input = grad_after + inverse * (scaled - mean - normed * along)
+    cond_t = condition.reshape(dp, groups, -1).transpose(2, 1, 0).reshape(-1, dp * groups)
+    grad_adaw, grad_adab, g_up, g_down, g_one, g_two = small_call(
+        payload.reshape(dp, tp, 3, width), cond_t, cols, up_count, count
+    )
 
     return (
         out,
-        grad_input.astype(BF),
+        grad_in,
         sum_qkv[:, :, :feats],
         sum_down[:, fh:].T,
         sum_up,
-        small[0],
+        g_up[0],
         sum_down[:, :fh].T,
-        small[1],
-        small[2],
-        small[3],
+        g_down[0],
+        g_one[0],
+        g_two[0],
         grad_adaw,
-        grad_adab,
+        grad_adab[0],
     )
 
 

time: 404 us -> 342 us (0.85)
  waiting for transfers between devices: 113 us -> 77.8 us
  starting transfers between devices: 97.8 us -> 78.7 us
  local copies, waits for them, and re-layouts: 30.1 us -> 20.9 us
  Pallas kernels: 112 us -> 119 us
    ppermute x32 -> x42, waiting for transfers between devices: 74.8 us -> 46.6 us  [send(): return lax.ppermute(array, ('dp', 'tensor'), pairs)]
    all_to_all x3 -> x5, starting transfers between devices: 35.6 us -> 18.5 us  [the longest x1 4.12 us: shards(): gm1 = lax.all_to_all(after_all(gm1, gm0), 'tensor', 0, 0, tiled=True)]
    ppermute x32 -> x42, starting transfers between devices: 39.8 us -> 53.5 us  [send(): return lax.ppermute(array, ('dp', 'tensor'), pairs)]
    all_to_all x1, starting transfers between devices: 16.8 us -> 3.31 us  [shards(): payload = lax.all_to_all(payload, ('dp', 'tensor'), 0, 0, tiled=True)]
    convert_element_type x6 -> x8, other arithmetic: 8.67 us -> 16.4 us  [add_low(): functools.reduce(jnp.add, [term.astype(F32) for term in terms]).astype(BF)]
    another operation x6 -> x3, other arithmetic: 7.8 us -> 0.26 us  [the longest x1 0.11 us: shards(): down_near = jnp.stack(after_all(down_parts, mixed0))]
    all_to_all x1, waiting for transfers between devices: 10.1 us -> 3.32 us  [shards(): lax.all_to_all(jnp.broadcast_to(times[None, :], (dp, groups)), 'dp', 0, 0...]
    reduce_sum x7 -> x1, other arithmetic: 7.3 us -> 1.02 us  [shards(): jnp.sum(sums[:, 4], axis=0)]
  transfers between devices with their start and end apart: 38 -> 50, of which waited for: 14 -> 14; matrix products, arithmetic and copies ran while one was open for 14% -> 12% of each run, Pallas kernels for 19% -> 21%
where the time goes in v2:
time: 342 us; the launch traced here: 340 us
  Pallas kernels  119 us (35%)
  starting transfers between devices  78.7 us (23%)
  waiting for transfers between devices  77.8 us (23%)
  other arithmetic  28.9 us (8%)
  local copies, waits for them, and re-layouts  20.9 us (6%)
  between operations  14.8 us (4%)
    ppermute x42, starting transfers between devices, send(): return lax.ppermute(array, ('dp', 'tensor'), pairs)  53.5 us
    ppermute x42, waiting for transfers between devices, send(): return lax.ppermute(array, ('dp', 'tensor'), pairs)  46.6 us
    pallas_call x1, Pallas kernels, mlp_call(): pl.pallas_call(mlp_kernel, in_specs=[sm] + [vm] * 8 + [ANY] * 16, out_spe...  32.8 us
    pallas_call x2, Pallas kernels, attend_call(): pl.pallas_call(functools.partial(attend_kernel, group=group), grid_spec=g...  27.5 us
    pallas_call x2, Pallas kernels, attend_back_call(): pl.pallas_call(attend_back_kernel, grid=(4,), in_specs=[spec((1, heads, b...  24.8 us
    convert_element_type x8, other arithmetic, add_low(): functools.reduce(jnp.add, [term.astype(F32) for term in terms]).astype(BF)  16.4 us
    pallas_call x1, Pallas kernels, qkv_call(): pl.pallas_call(qkv_kernel, grid_spec=grid_spec, out_shape=[jax.ShapeDtype...  14.3 us
    pallas_call x1, Pallas kernels, qkv_back_call(): pl.pallas_call(qkv_back_kernel, grid_spec=grid_spec, out_shape=[terms, te...  13.2 us
  transfers between devices with their start and end apart: 50, of which 14 were waited for; matrix products, arithmetic and copies ran while one was open for 12% of the time, Pallas kernels for 21%

profile of v2, /device:TPU:0, one launch (start us, length us, event | category | flops | bytes accessed | tf_op | source)
XLA Modules:
  0.0 340.1 jit_solution(1548630028451234972)
XLA Ops:
  8.9 3.1 collective-permute-start
  11.9 2.6 collective-permute-start.1
  17.1 3.3 all-to-all-start
  25.0 3.3 all-to-all-done
  30.3 3.8 %all-to-all-start.1 = ((f32[8,1,1824]{2,1,0:T(1,128)}), f32[8,1,1824]{2,1,0:T(1,128)S(1)}, u32[]{:S(2)}, u32[]{:S(2)}) async-start(f32[8,1,1824]{2,1,0:T(1,128)} %all_to_all.28), calls=%async_computation.1 | async-start | bytes 122880 | tf_op jit(solution)/shard_map/all_to_all | solution.py:827
  34.7 10.0 %all-to-all-done.1 = f32[8,1,1824]{2,1,0:T(1,128)S(1)} async-done(((f32[8,1,1824]{2,1,0:T(1,128)}), f32[8,1,1824]{2,1,0:T(1,128)S(1)}, u32[]{:S(2)}, u32[]{:S(2)}) %all-to-all-start.1) | async-done | bytes 58400 | tf_op jit(solution)/shard_map/all_to_all | solution.py:827
  47.4 2.7 collective-permute-start.6
  52.2 14.3 %qkv.1 = (bf16[2,1024,768]{2,1,0:T(8,128)(2,1)}, bf16[2,3,1024,64]{3,2,1,0:T(8,128)(2,1)}, bf16[2,3,1024,64]{3,2,1,0:T(8,128)(2,1)}, bf16[2,3,1024,64]{3,2,1,0:T...) custom-call(s32[8]{0:T(128)} %pad_add_fusion.tab, ...), custom_call_target="tpu_custom_call" | custom-call | flops 2415919104 | bytes 16777216 | tf_op jit(solution)/shard_map/qkv/pallas_call | solution.py:128
  66.4 3.0 collective-permute-start.9
  71.7 13.8 %attend.2 = (bf16[4,192,256]{2,1,0:T(8,128)(2,1)}, bf16[3,1024,1024]{2,1,0:T(8,128)(2,1)}) custom-call(s32[2]{0:T(128)} %lens.3, bf16[2,3,1024,64]{3,2,1,0:T(8,128)(2,1)} %get-tuple-element.71.q, bf16[2,3,1024,64]{3,2,1,0:T(8,128)(2,1)} %get-tuple-element.72.k, bf16[2,192,1024]{2,1,0:T(8,128)(2,1)} %get-tuple-element.88.vt), custom_call_target="tpu_custom_call" | custom-call | flops 3221225472 | bytes 10485760 | tf_op jit(solution)/shard_map/attend/pallas_call | solution.py:179
  87.7 13.8 %attend.3 = (bf16[4,192,256]{2,1,0:T(8,128)(2,1)}, bf16[3,1024,1024]{2,1,0:T(8,128)(2,1)}) custom-call(s32[2]{0:T(128)} %lens.3, bf16[2,3,1024,64]{3,2,1,0:T(8,128)(2,1)} %get-tuple-element.71.q, bf16[2,3,1024,64]{3,2,1,0:T(8,128)(2,1)} %get-tuple-element.72.k, bf16[2,192,1024]{2,1,0:T(8,128)(2,1)} %get-tuple-element.88.vt), custom_call_target="tpu_custom_call" | custom-call | flops 3221225472 | bytes 10485760 | tf_op jit(solution)/shard_map/attend/pallas_call | solution.py:179
  101.5 1.9 collective-permute-done.17.rest_9_
  106.0 3.5 %all-to-all-start.2 = ((bf16[4,192,256]{2,1,0:T(8,128)(2,1)}), bf16[4,192,256]{2,1,0:T(8,128)(2,1)S(1)}, u32[]{:S(2)}, u32[]{:S(2)}) async-start(bf16[4,192,256]{2,1,0:T(8,128)(2,1)} %get-tuple-element.80), calls=%async_computation.2 | async-start | bytes 786432 | tf_op jit(solution)/shard_map/all_to_all | solution.py:873
  109.5 14.4 %collective-permute-done.12.rest_3_ = bf16[4,96,768]{2,1,0:T(8,128)(2,1)} collective-permute-done((bf16[4,96,768]{2,1,0:T(8,128)(2,1)}, bf16[4,96,768]{2,1,0:T(8,128)(2,1)}, u32[]{:S(2)}, u32[]{:S(2)}) %collective-permute-start.12) | collective-permute-done | bytes 589856 | tf_op jit(solution)/shard_map/ppermute | solution.py:691
  125.9 3.6 %all-to-all-start.3 = ((bf16[4,192,256]{2,1,0:T(8,128)(2,1)}), bf16[4,192,256]{2,1,0:T(8,128)(2,1)S(1)}, u32[]{:S(2)}, u32[]{:S(2)}) async-start(bf16[4,192,256]{2,1,0:T(8,128)(2,1)} %get-tuple-element.90), calls=%async_computation.3 | async-start | bytes 786432 | tf_op jit(solution)/shard_map/all_to_all | solution.py:884
  132.4 4.4 %all-to-all-done.3.mixed1 = bf16[4,192,256]{2,1,0:T(8,128)(2,1)S(1)} async-done(((bf16[4,192,256]{2,1,0:T(8,128)(2,1)}), bf16[4,192,256]{2,1,0:T(8,128)(2,1)S(1)}, u32[]{:S(2)}, u32[]{:S(2)}) %all-to-all-start.3) | async-done | bytes 393248 | tf_op jit(solution)/shard_map/all_to_all | solution.py:884
  137.6 32.8 %mlp.1 = (bf16[2,256,768]{2,1,0:T(8,128)(2,1)}, f32[2,256,768]{2,1,0:T(8,128)}, bf16[4,192,256]{2,1,0:T(8,128)(2,1)}, bf16[4,192,256]{2,1,0:T(8,128)(2,1)}, f32[...) custom-call(s32[79]{0:T(128)} %concatenate.41.tab, ...), custom_call_target="tpu_custom_call" | custom-call | flops 14495514624 | bytes 29360128 | tf_op jit(solution)/shard_map/mlp/pallas_call | solution.py:552
  170.4 4.9 %collective-permute-done.24 = bf16[16,96,768]{2,1,0:T(8,128)(2,1)} collective-permute-done((bf16[16,96,768]{2,1,0:T(8,128)(2,1)}, bf16[16,96,768]{2,1,0:T(8,128)(2,1)}, u32[]{:S(2)}, u32[]{:S(2)}) %collective-permute-start.24) | collective-permute-done | bytes 2359328 | tf_op jit(solution)/shard_map/ppermute | solution.py:691
  175.4 3.5 %all-to-all-start.4 = ((bf16[4,192,256]{2,1,0:T(8,128)(2,1)}), bf16[4,192,256]{2,1,0:T(8,128)(2,1)S(1)}, u32[]{:S(2)}, u32[]{:S(2)}) async-start(bf16[4,192,256]{2,1,0:T(8,128)(2,1)} %get-tuple-element.99), calls=%async_computation.4 | async-start | bytes 786432 | tf_op jit(solution)/shard_map/all_to_all | solution.py:916
  180.2 6.1 %all-to-all-done.4.gm = bf16[4,192,256]{2,1,0:T(8,128)(2,1)S(1)} async-done(((bf16[4,192,256]{2,1,0:T(8,128)(2,1)}), bf16[4,192,256]{2,1,0:T(8,128)(2,1)S(1)}, u32[]{:S(2)}, u32[]{:S(2)}) %all-to-all-start.4) | async-done | bytes 393248 | tf_op jit(solution)/shard_map/all_to_all | solution.py:916
  186.3 1.7 fusion
  188.4 15.8 %collective-permute-done.25 = bf16[2,4,96,768]{3,2,1,0:T(8,128)(2,1)S(1)} collective-permute-done((bf16[2,4,96,768]{3,2,1,0:T(8,128)(2,1)S(1)}, bf16[2,4,96,768]{3,2,1,0:T(8,128)(2,1)S(1)}, u32[]{:S(2)}, u32[]{:S(2)}) %collective-permute-start.25) | collective-permute-done | bytes 1179680 | tf_op jit(solution)/shard_map/ppermute | solution.py:691
  205.3 2.4 fusion.2
  211.0 4.1 %all-to-all-start.5 = ((bf16[4,192,256]{2,1,0:T(8,128)(2,1)}), bf16[4,192,256]{2,1,0:T(8,128)(2,1)}, u32[]{:S(2)}, u32[]{:S(2)}) async-start(bf16[4,192,256]{2,1,0:T(8,128)(2,1)} %get-tuple-element.106), calls=%async_computation.5 | async-start | bytes 786432 | tf_op jit(solution)/shard_map/all_to_all | solution.py:917
  215.1 3.3 add_convert_fusion
  218.4 2.0 collective-permute-start.27
  220.4 1.7 fusion.12
  222.1 2.5 collective-permute-start.39
  224.6 2.4 collective-permute-start.41
  227.1 12.4 %attend_back.2.gt0 = bf16[3,192,1024]{2,1,0:T(8,128)(2,1)} custom-call(bf16[2,3,1024,64]{3,2,1,0:T(8,128)(2,1)} %get-tuple-element.71.q, bf16[2,192,1024]{2,1,0:T(8,128)(2,1)} %get-tuple-element.96.kt, bf16[2,3,1024,64]{3,2,1,0:T(8,128)(2,1)} %get-tuple-element.97.v, bf16[3,1024,1024]{2,1,0:T(8,128)(2,1)} %get-tuple-element.98.probs, ...), custom_call_target="tpu_custom_call" | custom-call | flops 6442450944 | bytes 10485760 | tf_op jit(solution)/shard_map/attend_back/pallas_call | solution.py:237
  239.5 2.0 convert_add_fusion.21
  241.5 12.4 %attend_back.3.gt1 = bf16[3,192,1024]{2,1,0:T(8,128)(2,1)} custom-call(bf16[2,3,1024,64]{3,2,1,0:T(8,128)(2,1)} %get-tuple-element.71.q, bf16[2,192,1024]{2,1,0:T(8,128)(2,1)} %get-tuple-element.96.kt, bf16[2,3,1024,64]{3,2,1,0:T(8,128)(2,1)} %get-tuple-element.97.v, bf16[3,1024,1024]{2,1,0:T(8,128)(2,1)} %get-tuple-element.104.probs, ...), custom_call_target="tpu_custom_call" | custom-call | flops 6442450944 | bytes 10485760 | tf_op jit(solution)/shard_map/attend_back/pallas_call | solution.py:237
  254.0 2.7 fusion.1
  256.6 13.2 %qkv_back.1 = (bf16[2,2,256,768]{3,2,1,0:T(8,128)(2,1)}, bf16[2,2,256,768]{3,2,1,0:T(8,128)(2,1)}, f32[2,2,768]{2,1,0:T(2,128)}, bf16[8,3,96,256]{3,2,1,0:T(8,128)(2,1)}) custom-call(s32[9]{0:T(128)} %pad_add_fusion.1.tab, bf16[3,192,1024]{2,1,0:T(8,128)(2,1)} %attend_back.2.gt0, bf16[3,192,1024]{2,1,0:T(8,128)(2,1)} %attend_back.3.gt1, ...), custom_call_target="tpu_custom_call" | custom-call | flops 4831838208 | bytes 16777216 | tf_op jit(solution)/shard_map/qkv_back/pallas_call | solution.py:344
  270.2 1.8 collective-permute-start.35
  274.2 3.3 all-to-all-start.6
  277.5 1.9 slice.248
  284.8 6.0 %all-to-all-done.6 = f32[32,3,768]{2,1,0:T(4,128)} async-done(((f32[32,3,768]{2,1,0:T(4,128)}), f32[32,3,768]{2,1,0:T(4,128)}, u32[]{:S(2)}, u32[]{:S(2)}) %all-to-all-start.6) | async-done | bytes 294944 | tf_op jit(solution)/shard_map/all_to_all | solution.py:1007
  290.7 2.2 small.1
  292.9 1.8 copy.72
  297.3 2.1 collective-permute-done.31
  300.9 2.4 collective-permute-start.33
  304.9 2.1 fusion.4
  307.5 1.9 collective-permute-done.32
  309.4 5.6 %collective-permute-start.37 = (bf16[96,960]{1,0:T(8,128)(2,1)S(1)}, bf16[96,960]{1,0:T(8,128)(2,1)S(1)}, u32[]{:S(2)}, u32[]{:S(2)}) collective-permute-start(bf16[96,960]{1,0:T(8,128)(2,1)S(1)} %get-tuple-element.186), channel_id=1, source_target_pairs={{0,16},{1,17},{2,18},{3,19},{4,20},{5,21},{6,22},{7,23},{8,24},{9,... | collective-permute-start | bytes 552968 | tf_op jit(solution)/shard_map/ppermute | solution.py:691
  315.0 5.4 %collective-permute-done.33 = bf16[3,96,256]{2,1,0:T(8,128)(2,1)S(1)} collective-permute-done((bf16[3,96,256]{2,1,0:T(8,128)(2,1)S(1)}, bf16[3,96,256]{2,1,0:T(8,128)(2,1)S(1)}, u32[]{:S(2)}, u32[]{:S(2)}) %collective-permute-start.33) | collective-permute-done | bytes 147488 | tf_op jit(solution)/shard_map/ppermute | solution.py:691
  320.4 5.0 %collective-permute-start.38 = (bf16[96,960]{1,0:T(8,128)(2,1)S(1)}, bf16[96,960]{1,0:T(8,128)(2,1)S(1)}, u32[]{:S(2)}, u32[]{:S(2)}) collective-permute-start(bf16[96,960]{1,0:T(8,128)(2,1)S(1)} %get-tuple-element.185), channel_id=1, source_target_pairs={{0,24},{1,25},{2,26},{3,27},{4,28},{5,29},{6,30},{7,31},{8,0},{9,1... | collective-permute-start | bytes 552968 | tf_op jit(solution)/shard_map/ppermute | solution.py:691
  326.2 3.9 %norm_back.1 = bf16[2,256,768]{2,1,0:T(8,128)(2,1)} custom-call(bf16[2,2,256,768]{3,2,1,0:T(8,128)(2,1)} %get-tuple-element.114.t0, bf16[2,2,256,768]{3,2,1,0:T(8,128)(2,1)} %copy-done.3, bf16[2,256,768]{2,1,0:T(8,128)(2,1)} %collective-permute-done.30.t2, bf16[2,256,768]{2,1,0:T(8,128)(2,1)} %tok.3, f32[2,256,768]{2,1,0:T(8,128)} %get-tuple-element.116.after, ...), custom_call_target="tpu_custom_call" | custom-call | flops 15728640 | bytes 4718592 | tf_op jit(solution)/shard_map/norm_back/pallas_call | solution.py:609
  (216 shorter events, 52.6 us)
Async XLA Ops:
  7.2 45.0 %all-gather.2.cloned.1.call-start = ((), (), s32[]{:S(2)}) async-start(), calls=%async_computation.7 | async-start | bytes 3932160 | tf_op jit(solution)/shard_map/all_gather | solution.py:812
  8.9 20.0 %collective-permute-start = (bf16[3,96,256]{2,1,0:T(8,128)(2,1)S(1)}, bf16[3,96,256]{2,1,0:T(8,128)(2,1)S(1)}, u32[]{:S(2)}, u32[]{:S(2)}) collective-permute-start(bf16[3,96,256]{2,1,0:T(8,128)(2,1)S(1)} %get-tuple-element.196), channel_id=1, source_target_pairs={{0,8},{1,9},{2,10},{3,11},{4,12},{5,13},{6,14},{7,15},{8,16},{9,17... | collective-permute-start | bytes 442376 | tf_op jit(solution)/shard_map/ppermute | solution.py:691
  11.9 17.0 %collective-permute-start.1 = (bf16[3,96,256]{2,1,0:T(8,128)(2,1)S(1)}, bf16[3,96,256]{2,1,0:T(8,128)(2,1)S(1)}, u32[]{:S(2)}, u32[]{:S(2)}) collective-permute-start(bf16[3,96,256]{2,1,0:T(8,128)(2,1)S(1)} %get-tuple-element.196), channel_id=1, source_target_pairs={{0,16},{1,17},{2,18},{3,19},{4,20},{5,21},{6,22},{7,23},{8,24},{9,... | collective-permute-start | bytes 442376 | tf_op jit(solution)/shard_map/ppermute | solution.py:691
  14.5 14.4 %collective-permute-start.2 = (bf16[3,96,256]{2,1,0:T(8,128)(2,1)S(1)}, bf16[3,96,256]{2,1,0:T(8,128)(2,1)S(1)}, u32[]{:S(2)}, u32[]{:S(2)}) collective-permute-start(bf16[3,96,256]{2,1,0:T(8,128)(2,1)S(1)} %get-tuple-element.196), channel_id=1, source_target_pairs={{0,24},{1,25},{2,26},{3,27},{4,28},{5,29},{6,30},{7,31},{8,0},{9,1... | collective-permute-start | bytes 442376 | tf_op jit(solution)/shard_map/ppermute | solution.py:691
  17.1 11.2 %all-to-all-start = ((s32[8,1,2]{2,1,0:T(1,128)}), s32[8,1,2]{2,1,0:T(1,128)S(1)}, u32[]{:S(2)}, u32[]{:S(2)}) async-start(s32[8,1,2]{2,1,0:T(1,128)} %broadcast_in_dim.88), calls=%async_computation | async-start | bytes 8192 | tf_op jit(solution)/shard_map/all_to_all | solution.py:799
  29.0 17.2 %collective-permute-start.3 = (bf16[4,3,96,256]{3,2,1,0:T(8,128)(2,1)S(1)}, bf16[4,3,96,256]{3,2,1,0:T(8,128)(2,1)S(1)}, u32[]{:S(2)}, u32[]{:S(2)}) collective-permute-start(bf16[4,3,96,256]{3,2,1,0:T(8,128)(2,1)S(1)} %pad_maximum_fusion.1.w0), channel_id=1, source_target_pairs={{0,4},{1,5},{2,6},{3,7},{4,0},{5,1},{6,2},{7,3},{8,12},{9,13},{10,... | collective-permute-start | bytes 1769480 | tf_op jit(solution)/shard_map/ppermute | solution.py:691
  30.3 14.3 %all-to-all-start.1 = ((f32[8,1,1824]{2,1,0:T(1,128)}), f32[8,1,1824]{2,1,0:T(1,128)S(1)}, u32[]{:S(2)}, u32[]{:S(2)}) async-start(f32[8,1,1824]{2,1,0:T(1,128)} %all_to_all.28), calls=%async_computation.1 | async-start | bytes 122880 | tf_op jit(solution)/shard_map/all_to_all | solution.py:827
  46.3 20.2 %collective-permute-start.4 = (bf16[96,768]{1,0:T(8,128)(2,1)S(1)}, bf16[96,768]{1,0:T(8,128)(2,1)S(1)}, u32[]{:S(2)}, u32[]{:S(2)}) collective-permute-start(bf16[96,768]{1,0:T(8,128)(2,1)S(1)} %copy-done.13), channel_id=1, source_target_pairs={{0,8},{1,9},{2,10},{3,11},{4,12},{5,13},{6,14},{7,15},{8,16},{9,17... | collective-permute-start | bytes 442376 | tf_op jit(solution)/shard_map/ppermute | solution.py:691
  46.9 22.5 %collective-permute-start.5 = (bf16[96,768]{1,0:T(8,128)(2,1)S(1)}, bf16[96,768]{1,0:T(8,128)(2,1)S(1)}, u32[]{:S(2)}, u32[]{:S(2)}) collective-permute-start(bf16[96,768]{1,0:T(8,128)(2,1)S(1)} %copy-done.13), channel_id=1, source_target_pairs={{0,16},{1,17},{2,18},{3,19},{4,20},{5,21},{6,22},{7,23},{8,24},{9,... | collective-permute-start | bytes 442376 | tf_op jit(solution)/shard_map/ppermute | solution.py:691
  47.4 22.0 %collective-permute-start.6 = (bf16[96,768]{1,0:T(8,128)(2,1)S(1)}, bf16[96,768]{1,0:T(8,128)(2,1)S(1)}, u32[]{:S(2)}, u32[]{:S(2)}) collective-permute-start(bf16[96,768]{1,0:T(8,128)(2,1)S(1)} %copy-done.13), channel_id=1, source_target_pairs={{0,24},{1,25},{2,26},{3,27},{4,28},{5,29},{6,30},{7,31},{8,0},{9,1... | collective-permute-start | bytes 442376 | tf_op jit(solution)/shard_map/ppermute | solution.py:691
  50.1 35.3 %collective-permute-start.7 = (bf16[96,960]{1,0:T(8,128)(2,1)S(1)}, bf16[96,960]{1,0:T(8,128)(2,1)S(1)}, u32[]{:S(2)}, u32[]{:S(2)}) collective-permute-start(bf16[96,960]{1,0:T(8,128)(2,1)S(1)} %pad_maximum_fusion.5), channel_id=1, source_target_pairs={{0,8},{1,9},{2,10},{3,11},{4,12},{5,13},{6,14},{7,15},{8,16},{9,17... | collective-permute-start | bytes 552968 | tf_op jit(solution)/shard_map/ppermute | solution.py:691
  50.7 34.8 %collective-permute-start.8 = (bf16[96,960]{1,0:T(8,128)(2,1)S(1)}, bf16[96,960]{1,0:T(8,128)(2,1)S(1)}, u32[]{:S(2)}, u32[]{:S(2)}) collective-permute-start(bf16[96,960]{1,0:T(8,128)(2,1)S(1)} %pad_maximum_fusion.5), channel_id=1, source_target_pairs={{0,16},{1,17},{2,18},{3,19},{4,20},{5,21},{6,22},{7,23},{8,24},{9,... | collective-permute-start | bytes 552968 | tf_op jit(solution)/shard_map/ppermute | solution.py:691
  66.4 19.0 %collective-permute-start.9 = (bf16[96,960]{1,0:T(8,128)(2,1)S(1)}, bf16[96,960]{1,0:T(8,128)(2,1)S(1)}, u32[]{:S(2)}, u32[]{:S(2)}) collective-permute-start(bf16[96,960]{1,0:T(8,128)(2,1)S(1)} %pad_maximum_fusion.5), channel_id=1, source_target_pairs={{0,24},{1,25},{2,26},{3,27},{4,28},{5,29},{6,30},{7,31},{8,0},{9,1... | collective-permute-start | bytes 552968 | tf_op jit(solution)/shard_map/ppermute | solution.py:691
  69.5 18.2 %collective-permute-start.10 = (bf16[4,96,768]{2,1,0:T(8,128)(2,1)S(1)}, bf16[4,96,768]{2,1,0:T(8,128)(2,1)}, u32[]{:S(2)}, u32[]{:S(2)}) collective-permute-start(bf16[4,96,768]{2,1,0:T(8,128)(2,1)S(1)} %pad_maximum_fusion.2.rest_0_), channel_id=1, source_target_pairs={{0,4},{1,3},{2,6},{3,1},{4,0},{5,7},{6,2},{7,5},{8,12},{9,11},{10,... | collective-permute-start | bytes 1769480 | tf_op jit(solution)/shard_map/ppermute | solution.py:691
  70.2 17.5 %collective-permute-start.11 = (bf16[4,96,768]{2,1,0:T(8,128)(2,1)S(1)}, bf16[4,96,768]{2,1,0:T(8,128)(2,1)}, u32[]{:S(2)}, u32[]{:S(2)}) collective-permute-start(bf16[4,96,768]{2,1,0:T(8,128)(2,1)S(1)} %pad_maximum_fusion.2.rest_0_), channel_id=1, source_target_pairs={{0,2},{1,5},{2,0},{3,7},{4,6},{5,1},{6,4},{7,3},{8,10},{9,13},{10,... | collective-permute-start | bytes 1769480 | tf_op jit(solution)/shard_map/ppermute | solution.py:691
  85.7 17.7 %collective-permute-start.17 = (bf16[4,96,960]{2,1,0:T(8,128)(2,1)S(1)}, bf16[4,96,960]{2,1,0:T(8,128)(2,1)S(1)}, u32[]{:S(2)}, u32[]{:S(2)}) collective-permute-start(bf16[4,96,960]{2,1,0:T(8,128)(2,1)S(1)} %pad_maximum_fusion.rest_8_), channel_id=1, source_target_pairs={{0,4},{1,3},{2,6},{3,1},{4,0},{5,7},{6,2},{7,5},{8,12},{9,11},{10,... | collective-permute-start | bytes 2211848 | tf_op jit(solution)/shard_map/ppermute | solution.py:691
  87.2 16.2 %collective-permute-start.18 = (bf16[4,96,960]{2,1,0:T(8,128)(2,1)S(1)}, bf16[4,96,960]{2,1,0:T(8,128)(2,1)}, u32[]{:S(2)}, u32[]{:S(2)}) collective-permute-start(bf16[4,96,960]{2,1,0:T(8,128)(2,1)S(1)} %pad_maximum_fusion.rest_8_), channel_id=1, source_target_pairs={{0,2},{1,5},{2,0},{3,7},{4,6},{5,1},{6,4},{7,3},{8,10},{9,13},{10,... | collective-permute-start | bytes 2211848 | tf_op jit(solution)/shard_map/ppermute | solution.py:691
  103.4 21.1 %collective-permute-start.19 = (bf16[4,96,960]{2,1,0:T(8,128)(2,1)S(1)}, bf16[4,96,960]{2,1,0:T(8,128)(2,1)}, u32[]{:S(2)}, u32[]{:S(2)}) collective-permute-start(bf16[4,96,960]{2,1,0:T(8,128)(2,1)S(1)} %collective-permute-done.17.rest_9_), channel_id=1, source_target_pairs={{0,2},{1,5},{2,0},{3,7},{4,6},{5,1},{6,4},{7,3},{8,10},{9,13},{10,... | collective-permute-start | bytes 2211848 | tf_op jit(solution)/shard_map/ppermute | solution.py:691
  103.9 20.0 %collective-permute-start.12 = (bf16[4,96,768]{2,1,0:T(8,128)(2,1)}, bf16[4,96,768]{2,1,0:T(8,128)(2,1)}, u32[]{:S(2)}, u32[]{:S(2)}) collective-permute-start(bf16[4,96,768]{2,1,0:T(8,128)(2,1)} %collective-permute-done.10.rest_1_), channel_id=1, source_target_pairs={{0,2},{1,5},{2,0},{3,7},{4,6},{5,1},{6,4},{7,3},{8,10},{9,13},{10,... | collective-permute-start | bytes 1769480 | tf_op jit(solution)/shard_map/ppermute | solution.py:691
  105.4 18.5 %collective-permute-start.13 = (bf16[4,96,768]{2,1,0:T(8,128)(2,1)S(1)}, bf16[4,96,768]{2,1,0:T(8,128)(2,1)}, u32[]{:S(2)}, u32[]{:S(2)}) collective-permute-start(bf16[4,96,768]{2,1,0:T(8,128)(2,1)S(1)} %pad_maximum_fusion.2.rest_0_), channel_id=1, source_target_pairs={{0,1},{1,0},{2,3},{3,2},{4,5},{5,4},{6,7},{7,6},{8,9},{9,8},{10,11... | collective-permute-start | bytes 1769480 | tf_op jit(solution)/shard_map/ppermute | solution.py:691
  105.4 19.0 %collective-permute-start.14 = (bf16[4,96,768]{2,1,0:T(8,128)(2,1)}, bf16[4,96,768]{2,1,0:T(8,128)(2,1)}, u32[]{:S(2)}, u32[]{:S(2)}) collective-permute-start(bf16[4,96,768]{2,1,0:T(8,128)(2,1)} %collective-permute-done.10.rest_1_), channel_id=1, source_target_pairs={{0,1},{1,0},{2,3},{3,2},{4,5},{5,4},{6,7},{7,6},{8,9},{9,8},{10,11... | collective-permute-start | bytes 1769480 | tf_op jit(solution)/shard_map/ppermute | solution.py:691
  105.9 19.1 %collective-permute-start.15 = (bf16[4,96,768]{2,1,0:T(8,128)(2,1)}, bf16[4,96,768]{2,1,0:T(8,128)(2,1)}, u32[]{:S(2)}, u32[]{:S(2)}) collective-permute-start(bf16[4,96,768]{2,1,0:T(8,128)(2,1)} %collective-permute-done.11.rest_2_), channel_id=1, source_target_pairs={{0,1},{1,0},{2,3},{3,2},{4,5},{5,4},{6,7},{7,6},{8,9},{9,8},{10,11... | collective-permute-start | bytes 1769480 | tf_op jit(solution)/shard_map/ppermute | solution.py:691
  106.0 19.9 %all-to-all-start.2 = ((bf16[4,192,256]{2,1,0:T(8,128)(2,1)}), bf16[4,192,256]{2,1,0:T(8,128)(2,1)S(1)}, u32[]{:S(2)}, u32[]{:S(2)}) async-start(bf16[4,192,256]{2,1,0:T(8,128)(2,1)} %get-tuple-element.80), calls=%async_computation.2 | async-start | bytes 786432 | tf_op jit(solution)/shard_map/all_to_all | solution.py:873
  123.9 12.9 %collective-permute-start.21 = (bf16[4,96,960]{2,1,0:T(8,128)(2,1)S(1)}, bf16[4,96,960]{2,1,0:T(8,128)(2,1)}, u32[]{:S(2)}, u32[]{:S(2)}) collective-permute-start(bf16[4,96,960]{2,1,0:T(8,128)(2,1)S(1)} %collective-permute-done.17.rest_9_), channel_id=1, source_target_pairs={{0,1},{1,0},{2,3},{3,2},{4,5},{5,4},{6,7},{7,6},{8,9},{9,8},{10,11... | collective-permute-start | bytes 2211848 | tf_op jit(solution)/shard_map/ppermute | solution.py:691
  123.9 12.9 %collective-permute-start.20 = (bf16[4,96,960]{2,1,0:T(8,128)(2,1)S(1)}, bf16[4,96,960]{2,1,0:T(8,128)(2,1)}, u32[]{:S(2)}, u32[]{:S(2)}) collective-permute-start(bf16[4,96,960]{2,1,0:T(8,128)(2,1)S(1)} %pad_maximum_fusion.rest_8_), channel_id=1, source_target_pairs={{0,1},{1,0},{2,3},{3,2},{4,5},{5,4},{6,7},{7,6},{8,9},{9,8},{10,11... | collective-permute-start | bytes 2211848 | tf_op jit(solution)/shard_map/ppermute | solution.py:691
  124.4 12.4 %collective-permute-start.22 = (bf16[4,96,960]{2,1,0:T(8,128)(2,1)}, bf16[4,96,960]{2,1,0:T(8,128)(2,1)}, u32[]{:S(2)}, u32[]{:S(2)}) collective-permute-start(bf16[4,96,960]{2,1,0:T(8,128)(2,1)} %collective-permute-done.18.rest_10_), channel_id=1, source_target_pairs={{0,1},{1,0},{2,3},{3,2},{4,5},{5,4},{6,7},{7,6},{8,9},{9,8},{10,11... | collective-permute-start | bytes 2211848 | tf_op jit(solution)/shard_map/ppermute | solution.py:691
  124.5 12.3 %collective-permute-start.23 = (bf16[4,96,960]{2,1,0:T(8,128)(2,1)}, bf16[4,96,960]{2,1,0:T(8,128)(2,1)}, u32[]{:S(2)}, u32[]{:S(2)}) collective-permute-start(bf16[4,96,960]{2,1,0:T(8,128)(2,1)} %collective-permute-done.19.rest_11_), channel_id=1, source_target_pairs={{0,1},{1,0},{2,3},{3,2},{4,5},{5,4},{6,7},{7,6},{8,9},{9,8},{10,11... | collective-permute-start | bytes 2211848 | tf_op jit(solution)/shard_map/ppermute | solution.py:691
  125.0 11.8 %collective-permute-start.16 = (bf16[4,96,768]{2,1,0:T(8,128)(2,1)}, bf16[4,96,768]{2,1,0:T(8,128)(2,1)}, u32[]{:S(2)}, u32[]{:S(2)}) collective-permute-start(bf16[4,96,768]{2,1,0:T(8,128)(2,1)} %collective-permute-done.12.rest_3_), channel_id=1, source_target_pairs={{0,1},{1,0},{2,3},{3,2},{4,5},{5,4},{6,7},{7,6},{8,9},{9,8},{10,11... | collective-permute-start | bytes 1769480 | tf_op jit(solution)/shard_map/ppermute | solution.py:691
  125.9 10.9 %all-to-all-start.3 = ((bf16[4,192,256]{2,1,0:T(8,128)(2,1)}), bf16[4,192,256]{2,1,0:T(8,128)(2,1)S(1)}, u32[]{:S(2)}, u32[]{:S(2)}) async-start(bf16[4,192,256]{2,1,0:T(8,128)(2,1)} %get-tuple-element.90), calls=%async_computation.3 | async-start | bytes 786432 | tf_op jit(solution)/shard_map/all_to_all | solution.py:884
  175.3 39.8 %collective-permute-start.26 = (bf16[16,96,960]{2,1,0:T(8,128)(2,1)}, bf16[16,96,960]{2,1,0:T(8,128)(2,1)}, u32[]{:S(2)}, u32[]{:S(2)}) collective-permute-start(bf16[16,96,960]{2,1,0:T(8,128)(2,1)} %get-tuple-element.109), channel_id=1, source_target_pairs={{0,1},{1,0},{2,3},{3,2},{4,5},{5,4},{6,7},{7,6},{8,9},{9,8},{10,11... | collective-permute-start | bytes 8847368 | tf_op jit(solution)/shard_map/ppermute | solution.py:691
  175.4 10.9 %all-to-all-start.4 = ((bf16[4,192,256]{2,1,0:T(8,128)(2,1)}), bf16[4,192,256]{2,1,0:T(8,128)(2,1)S(1)}, u32[]{:S(2)}, u32[]{:S(2)}) async-start(bf16[4,192,256]{2,1,0:T(8,128)(2,1)} %get-tuple-element.99), calls=%async_computation.4 | async-start | bytes 786432 | tf_op jit(solution)/shard_map/all_to_all | solution.py:916
  188.0 16.3 %collective-permute-start.25 = (bf16[2,4,96,768]{3,2,1,0:T(8,128)(2,1)S(1)}, bf16[2,4,96,768]{3,2,1,0:T(8,128)(2,1)S(1)}, u32[]{:S(2)}, u32[]{:S(2)}) collective-permute-start(bf16[2,4,96,768]{3,2,1,0:T(8,128)(2,1)S(1)} %fusion), channel_id=1, source_target_pairs={{0,2},{1,5},{2,0},{3,7},{4,6},{5,1},{6,4},{7,3},{8,10},{9,13},{10,... | collective-permute-start | bytes 3538952 | tf_op jit(solution)/shard_map/ppermute | solution.py:691
  207.7 12.6 %collective-permute-start.28 = (bf16[4,96,768]{2,1,0:T(8,128)(2,1)}, bf16[4,96,768]{2,1,0:T(8,128)(2,1)}, u32[]{:S(2)}, u32[]{:S(2)}) collective-permute-start(bf16[4,96,768]{2,1,0:T(8,128)(2,1)} %fusion.2), channel_id=1, source_target_pairs={{0,4},{1,3},{2,6},{3,1},{4,0},{5,7},{6,2},{7,5},{8,12},{9,11},{10,... | collective-permute-start | bytes 1769480 | tf_op jit(solution)/shard_map/ppermute | solution.py:691
  211.0 30.5 %all-to-all-start.5 = ((bf16[4,192,256]{2,1,0:T(8,128)(2,1)}), bf16[4,192,256]{2,1,0:T(8,128)(2,1)}, u32[]{:S(2)}, u32[]{:S(2)}) async-start(bf16[4,192,256]{2,1,0:T(8,128)(2,1)} %get-tuple-element.106), calls=%async_computation.5 | async-start | bytes 786432 | tf_op jit(solution)/shard_map/all_to_all | solution.py:917
  218.4 35.5 %collective-permute-start.27 = (bf16[2,4,96,960]{3,2,1,0:T(8,128)(2,1)}, bf16[2,4,96,960]{3,2,1,0:T(8,128)(2,1)}, u32[]{:S(2)}, u32[]{:S(2)}) collective-permute-start(bf16[2,4,96,960]{3,2,1,0:T(8,128)(2,1)} %bitcast.25), channel_id=1, source_target_pairs={{0,2},{1,5},{2,0},{3,7},{4,6},{5,1},{6,4},{7,3},{8,10},{9,13},{10,... | collective-permute-start | bytes 4423688 | tf_op jit(solution)/shard_map/ppermute | solution.py:691
  222.1 17.4 %collective-permute-start.39 = (bf16[96,768]{1,0:T(8,128)(2,1)S(1)}, bf16[96,768]{1,0:T(8,128)(2,1)S(1)}, u32[]{:S(2)}, u32[]{:S(2)}) collective-permute-start(bf16[96,768]{1,0:T(8,128)(2,1)S(1)} %get-tuple-element.188), channel_id=1, source_target_pairs={{0,8},{1,9},{2,10},{3,11},{4,12},{5,13},{6,14},{7,15},{8,16},{9,17... | collective-permute-start | bytes 442376 | tf_op jit(solution)/shard_map/ppermute | solution.py:691
  224.6 14.9 %collective-permute-start.40 = (bf16[96,768]{1,0:T(8,128)(2,1)S(1)}, bf16[96,768]{1,0:T(8,128)(2,1)S(1)}, u32[]{:S(2)}, u32[]{:S(2)}) collective-permute-start(bf16[96,768]{1,0:T(8,128)(2,1)S(1)} %get-tuple-element.190), channel_id=1, source_target_pairs={{0,16},{1,17},{2,18},{3,19},{4,20},{5,21},{6,22},{7,23},{8,24},{9,... | collective-permute-start | bytes 442376 | tf_op jit(solution)/shard_map/ppermute | solution.py:691
  224.6 14.9 %collective-permute-start.41 = (bf16[96,768]{1,0:T(8,128)(2,1)S(1)}, bf16[96,768]{1,0:T(8,128)(2,1)}, u32[]{:S(2)}, u32[]{:S(2)}) collective-permute-start(bf16[96,768]{1,0:T(8,128)(2,1)S(1)} %get-tuple-element.189), channel_id=1, source_target_pairs={{0,24},{1,25},{2,26},{3,27},{4,28},{5,29},{6,30},{7,31},{8,0},{9,1... | collective-permute-start | bytes 442376 | tf_op jit(solution)/shard_map/ppermute | solution.py:691
  269.8 11.4 %collective-permute-start.29 = (bf16[2,2,256,768]{3,2,1,0:T(8,128)(2,1)}, bf16[2,2,256,768]{3,2,1,0:T(8,128)(2,1)S(1)}, u32[]{:S(2)}, u32[]{:S(2)}) collective-permute-start(bf16[2,2,256,768]{3,2,1,0:T(8,128)(2,1)} %get-tuple-element.115), channel_id=1, source_target_pairs={{0,1},{1,0},{2,3},{3,2},{4,5},{5,4},{6,7},{7,6},{8,9},{9,8},{10,11... | collective-permute-start | bytes 4718600 | tf_op jit(solution)/shard_map/ppermute | solution.py:691
  270.2 34.7 %collective-permute-start.35 = (bf16[4,96,960]{2,1,0:T(8,128)(2,1)}, bf16[4,96,960]{2,1,0:T(8,128)(2,1)}, u32[]{:S(2)}, u32[]{:S(2)}) collective-permute-start(bf16[4,96,960]{2,1,0:T(8,128)(2,1)} %fusion.1), channel_id=1, source_target_pairs={{0,4},{1,3},{2,6},{3,1},{4,0},{5,7},{6,2},{7,5},{8,12},{9,11},{10,... | collective-permute-start | bytes 2211848 | tf_op jit(solution)/shard_map/ppermute | solution.py:691
  274.2 16.5 %all-to-all-start.6 = ((f32[32,3,768]{2,1,0:T(4,128)}), f32[32,3,768]{2,1,0:T(4,128)}, u32[]{:S(2)}, u32[]{:S(2)}) async-start(f32[32,3,768]{2,1,0:T(4,128)} %bitcast.186), calls=%async_computation.6 | async-start | bytes 786432 | tf_op jit(solution)/shard_map/all_to_all | solution.py:1007
  279.5 19.9 %collective-permute-start.31 = (bf16[4,3,96,256]{3,2,1,0:T(8,128)(2,1)}, bf16[4,3,96,256]{3,2,1,0:T(8,128)(2,1)}, u32[]{:S(2)}, u32[]{:S(2)}) collective-permute-start(bf16[4,3,96,256]{3,2,1,0:T(8,128)(2,1)} %slice.248), channel_id=1, source_target_pairs={{0,4},{1,5},{2,6},{3,7},{4,0},{5,1},{6,2},{7,3},{8,12},{9,13},{10,... | collective-permute-start | bytes 1769480 | tf_op jit(solution)/shard_map/ppermute | solution.py:691
  282.5 43.7 %collective-permute-start.30 = (bf16[2,256,768]{2,1,0:T(8,128)(2,1)}, bf16[2,256,768]{2,1,0:T(8,128)(2,1)}, u32[]{:S(2)}, u32[]{:S(2)}) collective-permute-start(bf16[2,256,768]{2,1,0:T(8,128)(2,1)} %fusion.3), channel_id=1, source_target_pairs={{0,2},{1,3},{2,0},{3,1},{4,6},{5,7},{6,4},{7,5},{8,10},{9,11},{10,... | collective-permute-start | bytes 2359304 | tf_op jit(solution)/shard_map/ppermute | solution.py:691
  300.9 19.5 %collective-permute-start.33 = (bf16[3,96,256]{2,1,0:T(8,128)(2,1)S(1)}, bf16[3,96,256]{2,1,0:T(8,128)(2,1)S(1)}, u32[]{:S(2)}, u32[]{:S(2)}) collective-permute-start(bf16[3,96,256]{2,1,0:T(8,128)(2,1)S(1)} %get-tuple-element.193), channel_id=1, source_target_pairs={{0,16},{1,17},{2,18},{3,19},{4,20},{5,21},{6,22},{7,23},{8,24},{9,... | collective-permute-start | bytes 442376 | tf_op jit(solution)/shard_map/ppermute | solution.py:691
  303.3 22.1 %collective-permute-start.34 = (bf16[3,96,256]{2,1,0:T(8,128)(2,1)S(1)}, bf16[3,96,256]{2,1,0:T(8,128)(2,1)S(1)}, u32[]{:S(2)}, u32[]{:S(2)}) collective-permute-start(bf16[3,96,256]{2,1,0:T(8,128)(2,1)S(1)} %get-tuple-element.192), channel_id=1, source_target_pairs={{0,24},{1,25},{2,26},{3,27},{4,28},{5,29},{6,30},{7,31},{8,0},{9,1... | collective-permute-start | bytes 442376 | tf_op jit(solution)/shard_map/ppermute | solution.py:691
  307.0 23.1 %collective-permute-start.36 = (bf16[96,960]{1,0:T(8,128)(2,1)S(1)}, bf16[96,960]{1,0:T(8,128)(2,1)S(1)}, u32[]{:S(2)}, u32[]{:S(2)}) collective-permute-start(bf16[96,960]{1,0:T(8,128)(2,1)S(1)} %get-tuple-element.187), channel_id=1, source_target_pairs={{0,8},{1,9},{2,10},{3,11},{4,12},{5,13},{6,14},{7,15},{8,16},{9,17... | collective-permute-start | bytes 552968 | tf_op jit(solution)/shard_map/ppermute | solution.py:691
  309.4 20.8 %collective-permute-start.37 = (bf16[96,960]{1,0:T(8,128)(2,1)S(1)}, bf16[96,960]{1,0:T(8,128)(2,1)S(1)}, u32[]{:S(2)}, u32[]{:S(2)}) collective-permute-start(bf16[96,960]{1,0:T(8,128)(2,1)S(1)} %get-tuple-element.186), channel_id=1, source_target_pairs={{0,16},{1,17},{2,18},{3,19},{4,20},{5,21},{6,22},{7,23},{8,24},{9,... | collective-permute-start | bytes 552968 | tf_op jit(solution)/shard_map/ppermute | solution.py:691
  320.4 9.9 %collective-permute-start.38 = (bf16[96,960]{1,0:T(8,128)(2,1)S(1)}, bf16[96,960]{1,0:T(8,128)(2,1)S(1)}, u32[]{:S(2)}, u32[]{:S(2)}) collective-permute-start(bf16[96,960]{1,0:T(8,128)(2,1)S(1)} %get-tuple-element.185), channel_id=1, source_target_pairs={{0,24},{1,25},{2,26},{3,27},{4,28},{5,29},{6,30},{7,31},{8,0},{9,1... | collective-permute-start | bytes 552968 | tf_op jit(solution)/shard_map/ppermute | solution.py:691
  (36 other events, 540.9 us)
Sparse Core Ops, SparseCore 0:
  9.6 31.2 all-gather.1

commit v3 on v2

v3 whole, which is shorter than its diff:
```python
import functools
import math

import jax
import jax.numpy as jnp
import numpy as np
from jax import lax
from jax.experimental import pallas as pl
from jax.experimental.pallas import tpu as pltpu
from jax.sharding import PartitionSpec as P

HEAD = 64
EPS = 1e-05
MASKED = -1e30
BF = jnp.bfloat16
F32 = jnp.float32
VMEM_MAX = 60 * 1024 * 1024
NBLK = 8
NT = (((1,), (1,)), ((), ()))


def spec(block, index_map):
    return pl.BlockSpec(block, index_map)


def whole(shape):
    return pl.BlockSpec(shape, lambda *_: (0,) * len(shape))


ANY = pl.BlockSpec(memory_space=pl.ANY)


def params():
    return pltpu.CompilerParams(vmem_limit_bytes=VMEM_MAX)


def cost(flops, moved, trans=0):
    return pl.CostEstimate(flops=flops, bytes_accessed=moved, transcendentals=trans)


def norm_rows(rows):
    centered = rows - jnp.mean(rows, axis=1, keepdims=True)
    variance = jnp.mean(centered * centered, axis=1, keepdims=True)
    inverse = lax.rsqrt(variance + EPS)
    return centered * inverse, inverse


def qkv_kernel(tab, tok, mod, gain, cos, sin, w0, w1, first, q, k, v, kt, vt, w, sem):
    heads, block = q.shape[1], q.shape[2]
    step = pl.program_id(0) * pl.num_programs(1) + pl.program_id(1)
    rows = w0.shape[2]

    @pl.when(step == 0)
    def _():
        copies = []
        for p, ref in enumerate((w0, w1)):
            for j in range(4):
                row = pl.multiple_of(tab[p * 4 + j] * rows, 16)
                copies.append(
                    pltpu.make_async_copy(
                        ref.at[j], w.at[:, pl.ds(row, rows), :], sem.at[p * 4 + j]
                    )
                )
        for copy in copies:
            copy.start()
        for copy in copies:
            copy.wait()

    normed, _ = norm_rows(tok[0].astype(F32))
    factor = gain[...] * (1.0 + mod[0, 1:2, :])
    x = (normed * factor + mod[0, 0:1, :]).astype(BF)
    first[0] = x
    wide = w.shape[2]
    low = lax.rem(lax.broadcasted_iota(jnp.int32, (block, wide), 1), HEAD) < HEAD // 2

    def rotate(vec):
        turned = jnp.where(
            low, pltpu.roll(vec, wide - HEAD // 2, 1), pltpu.roll(vec, HEAD // 2, 1)
        )
        return vec * cos[...] + turned * sin[...]

    def store_heads(ref, vec):
        for h in range(heads):
            shifted = vec if h == 0 else pltpu.roll(vec, wide - h * HEAD, 1)
            ref[0, h] = shifted[:, :HEAD].astype(BF)

    query = rotate(jnp.dot(x, w[0], preferred_element_type=F32))
    store_heads(q, query * (HEAD**-0.5))
    key = rotate(jnp.dot(x, w[1], preferred_element_type=F32))
    store_heads(k, key)
    kt[0] = key.T[: heads * HEAD].astype(BF)
    value = jnp.dot(x, w[2], preferred_element_type=F32)
    store_heads(v, value)
    vt[0] = value.T[: heads * HEAD].astype(BF)


def qkv_call(tab, tok_all, mod, gain, cos, sin, w0, w1):
    groups, seq, width = tok_all.shape
    block = seq // 4
    wide = w0.shape[3]
    heads = (wide // HEAD) * 3 // 4
    feats = heads * HEAD
    grid_spec = pltpu.PrefetchScalarGridSpec(
        num_scalar_prefetch=1,
        grid=(groups, 4),
        in_specs=[
            spec((1, block, width), lambda g, j, _: (g, j, 0)),
            spec((1, 6, width), lambda g, j, _: (g, 0, 0)),
            whole((1, width)),
            spec((block, wide), lambda g, j, _: (j, 0)),
            spec((block, wide), lambda g, j, _: (j, 0)),
            ANY,
            ANY,
        ],
        out_specs=[
            spec((1, block, width), lambda g, j, _: (g, j, 0)),
            spec((1, heads, block, HEAD), lambda g, j, _: (g, 0, j, 0)),
            spec((1, heads, block, HEAD), lambda g, j, _: (g, 0, j, 0)),
            spec((1, heads, block, HEAD), lambda g, j, _: (g, 0, j, 0)),
            spec((1, feats, block), lambda g, j, _: (g, 0, j)),
            spec((1, feats, block), lambda g, j, _: (g, 0, j)),
            whole((3, width, wide)),
        ],
        scratch_shapes=[pltpu.SemaphoreType.DMA((8,))],
    )
    head_shape = jax.ShapeDtypeStruct((groups, heads, seq, HEAD), BF)
    turned = jax.ShapeDtypeStruct((groups, feats, seq), BF)
    return pl.pallas_call(
        qkv_kernel,
        grid_spec=grid_spec,
        out_shape=[
            jax.ShapeDtypeStruct((groups, seq, width), BF),
            head_shape,
            head_shape,
            head_shape,
            turned,
            turned,
            jax.ShapeDtypeStruct((3, width, wide), BF),
        ],
        compiler_params=params(),
        cost_estimate=cost(2 * groups * seq * width * wide * 3, 16 * 2**20),
        name="qkv",
    )(tab, tok_all, mod, gain, cos, sin, w0, w1)


def attend_kernel(tab, q, k, vt, mix0, mix1, mix2, mix3, probs, *, group):
    heads, seq = k.shape[1], k.shape[2]
    block = q.shape[2]
    live = lax.broadcasted_iota(jnp.int32, (seq, block), 0) < tab[group]
    parts = []
    for h in range(heads):
        scores = lax.dot_general(k[0, h], q[0, h], NT, preferred_element_type=F32)
        scores = jnp.where(live, scores, MASKED)
        largest = jnp.max(scores, axis=0, keepdims=True)
        weights = jnp.exp(scores - largest)
        total = jnp.sum(weights, axis=0, keepdims=True)
        low = (weights * (1.0 / total)).astype(BF)
        probs[h] = low
        here = slice(h * HEAD, (h + 1) * HEAD)
        parts.append(jnp.dot(vt[0, here, :], low, preferred_element_type=F32).astype(BF))
    for r, ref in enumerate((mix0, mix1, mix2, mix3)):

        @pl.when(turn(pl.program_id(0)) == r)
        def _():
            for h in range(heads):
                ref[h * HEAD : (h + 1) * HEAD, :] = parts[h]


def turn(step):
    return lax.rem(step + 1, 4)


def attend_call(group, tab, q, k, vt):
    _, heads, seq, _ = q.shape
    block = seq // 4
    feats = heads * HEAD

    def piece(i, tab):
        return lax.bitwise_xor(tab[2], turn(i))

    grid_spec = pltpu.PrefetchScalarGridSpec(
        num_scalar_prefetch=1,
        grid=(4,),
        in_specs=[
            spec((1, heads, block, HEAD), lambda i, tab: (group, 0, piece(i, tab), 0)),
            spec((1, heads, seq, HEAD), lambda i, tab: (group, 0, 0, 0)),
            spec((1, feats, seq), lambda i, tab: (group, 0, 0)),
        ],
        out_specs=[
            *[whole((feats, block))] * 4,
            spec((heads, seq, block), lambda i, tab: (0, 0, piece(i, tab))),
        ],
    )
    return pl.pallas_call(
        functools.partial(attend_kernel, group=group),
        grid_spec=grid_spec,
        out_shape=[
            *[jax.ShapeDtypeStruct((feats, block), BF)] * 4,
            jax.ShapeDtypeStruct((heads, seq, seq), BF),
        ],
        compiler_params=params(),
        cost_estimate=cost(16 * heads * seq * seq * HEAD, 10 * 2**20, heads * seq * seq),
        name="attend",
    )(tab, q, k, vt)


def attend_back_kernel(tab, q, kt, v, probs, gm0, gm1, gm2, gm3, cos, sin, out, dk, dv, gm):
    heads, block = q.shape[1], q.shape[2]
    half = HEAD // 2
    step = pl.program_id(0)
    j = lax.bitwise_xor(tab[0], step)

    @pl.when(step == 0)
    def _():
        dk[...] = jnp.zeros_like(dk)
        dv[...] = jnp.zeros_like(dv)
        for r, ref in enumerate((gm0, gm1, gm2, gm3)):
            gm[r] = ref[...]

    columns = pl.ds(pl.multiple_of(j * block, 128), block)
    cos_here, sin_here = cos[:, columns], sin[:, columns]

    def store_turned(plane, h, vec, c, s, where):
        low, high = vec[:half], vec[half:]
        base = h * HEAD
        out[plane, base : base + half, where] = (low * c + high * s).astype(BF)
        out[plane, base + half : base + HEAD, where] = (high * c - low * s).astype(BF)

    for h in range(heads):
        here = slice(h * HEAD, (h + 1) * HEAD)
        grad = gm[step, here, :]
        low = probs[h]
        dp = jnp.dot(v[0, h], grad, preferred_element_type=F32)
        soft = low.astype(F32)
        prod = soft * dp
        inner = jnp.sum(prod, axis=0, keepdims=True)
        ds = (prod - soft * inner).astype(BF)
        dv[h] += lax.dot_general(low, grad, NT, preferred_element_type=F32)
        dk[h] += jnp.dot(ds, q[0, h], preferred_element_type=F32)
        dq = jnp.dot(kt[0, here, :], ds, preferred_element_type=F32)
        store_turned(0, h, dq * (HEAD**-0.5), cos_here, sin_here, columns)

    @pl.when(step == pl.num_programs(0) - 1)
    def _():
        for h in range(heads):
            store_turned(1, h, dk[h].T, cos[...], sin[...], slice(None))
            out[2, h * HEAD : (h + 1) * HEAD, :] = dv[h].T.astype(BF)


def attend_back_call(group, tab, q, kt, v, probs, gm, cos, sin):
    _, heads, seq, _ = q.shape
    block = seq // 4
    feats = heads * HEAD
    half = HEAD // 2

    def piece(i, tab):
        return lax.bitwise_xor(tab[0], i)

    grid_spec = pltpu.PrefetchScalarGridSpec(
        num_scalar_prefetch=1,
        grid=(4,),
        in_specs=[
            spec((1, heads, block, HEAD), lambda i, tab: (group, 0, piece(i, tab), 0)),
            spec((1, feats, seq), lambda i, tab: (group, 0, 0)),
            spec((1, heads, seq, HEAD), lambda i, tab: (group, 0, 0, 0)),
            spec((heads, seq, block), lambda i, tab: (0, 0, piece(i, tab))),
            *[spec((feats, block), lambda i, tab: (0, group))] * 4,
            whole((half, seq)),
            whole((half, seq)),
        ],
        out_specs=whole((3, feats, seq)),
        scratch_shapes=[
            pltpu.VMEM((heads, seq, HEAD), F32),
            pltpu.VMEM((heads, seq, HEAD), F32),
            pltpu.VMEM((4, feats, block), BF),
        ],
    )
    return pl.pallas_call(
        attend_back_kernel,
        grid_spec=grid_spec,
        out_shape=jax.ShapeDtypeStruct((3, feats, seq), BF),
        compiler_params=params(),
        cost_estimate=cost(32 * heads * seq * seq * HEAD, 10 * 2**20),
        name="attend_back",
    )(tab, q, kt, v, probs, *gm, cos, sin)


def qkv_back_kernel(tab, gt0, gt1, first, tok, w, fts, ftk, sums, dws, dwk, acc):
    i = pl.program_id(0)
    feats, block = gt0.shape[1], gt0.shape[2]
    wide, width = w.shape[2], w.shape[1]
    rows = dws.shape[2]
    g = lax.rem(i, 2)

    @pl.when(i == 0)
    def _():
        acc[...] = jnp.zeros_like(acc)
        sums[...] = jnp.zeros_like(sums)

    total = None
    for j in range(3):
        part = jnp.where(g == 0, gt0[j], gt1[j])
        tall = part.astype(F32)
        if wide > feats:
            tall = jnp.concatenate([tall, jnp.zeros((wide - feats, block), F32)], axis=0)
        term = lax.dot_general(tall.T.astype(BF), w[j], NT, preferred_element_type=F32)
        total = term if total is None else total + term
        acc[j, :feats] += jnp.dot(part, first[0], preferred_element_type=F32)
    normed, _ = norm_rows(tok[0].astype(F32))
    sums[g, 0:1, :] += jnp.sum(total, axis=0, keepdims=True)
    sums[g, 1:2, :] += jnp.sum(total * normed, axis=0, keepdims=True)
    low = total.astype(BF)

    @pl.when(i < 4)
    def _():
        fts[0, 0] = low

    @pl.when(i >= 4)
    def _():
        ftk[0, 0] = low

    @pl.when(i == pl.num_programs(0) - 1)
    def _():
        for j in range(3):
            flat = acc[j].T.astype(BF)
            for b in range(NBLK):
                part = flat[b * rows : (b + 1) * rows]
                there = tab[b]

                @pl.when(there < NBLK // 2)
                def _():
                    dwk[there, j] = part

                @pl.when(there >= NBLK // 2)
                def _():
                    dws[there - NBLK // 2, j] = part


def qkv_back_call(tab, gt0, gt1, first, tok_all, w):
    _, feats, seq = gt0.shape
    groups = first.shape[0]
    block = seq // 4
    width = first.shape[2]
    wide = w.shape[2]
    rows = width // NBLK

    def piece(i, tab):
        return lax.bitwise_xor(tab[NBLK], lax.rem(i, 4) // 2 * 2 + (1 - i // 4))

    grid_spec = pltpu.PrefetchScalarGridSpec(
        num_scalar_prefetch=1,
        grid=(8,),
        in_specs=[
            spec((3, feats, block), lambda i, tab: (0, 0, piece(i, tab))),
            spec((3, feats, block), lambda i, tab: (0, 0, piece(i, tab))),
            spec((1, block, width), lambda i, tab: (lax.rem(i, 2), piece(i, tab), 0)),
            spec((1, block, width), lambda i, tab: (lax.rem(i, 2), piece(i, tab), 0)),
            whole((3, width, wide)),
        ],
        out_specs=[
            spec(
                (1, 1, block, width),
                lambda i, tab: (jnp.minimum(i, 3) // 2, lax.rem(jnp.minimum(i, 3), 2), 0, 0),
            ),
            spec(
                (1, 1, block, width),
                lambda i, tab: (
                    jnp.maximum(i - 4, 0) // 2,
                    lax.rem(jnp.maximum(i - 4, 0), 2),
                    0,
                    0,
                ),
            ),
            whole((groups, 2, width)),
            whole((NBLK // 2, 3, rows, wide)),
            whole((NBLK // 2, 3, rows, wide)),
        ],
        scratch_shapes=[pltpu.VMEM((3, wide, width), F32)],
    )
    terms = jax.ShapeDtypeStruct((2, groups, block, width), BF)
    return pl.pallas_call(
        qkv_back_kernel,
        grid_spec=grid_spec,
        out_shape=[
            terms,
            terms,
            jax.ShapeDtypeStruct((groups, 2, width), F32),
            jax.ShapeDtypeStruct((NBLK // 2, 3, rows, wide), BF),
            jax.ShapeDtypeStruct((NBLK // 2, 3, rows, wide), BF),
        ],
        compiler_params=params(),
        cost_estimate=cost(4 * groups * seq * width * wide * 3, 16 * 2**20),
        name="qkv_back",
    )(tab, gt0, gt1, first, tok_all, w)


MIXED = (0, 2, 1, 3)
T_PART, T_ROW, T_SLOT = 3, 7, 39


def start_weights(tab, pieces, lanes, target, sem):
    rows = pieces[0].shape[1]
    for p in range(8):
        slot = tab[T_SLOT + p]
        for j in range(4):
            row = pl.multiple_of(tab[T_ROW + p * 4 + j] * rows, 16)
            pltpu.make_async_copy(
                pieces[p].at[j, :, lanes], target.at[slot, pl.ds(row, rows), :], sem.at[slot]
            ).start()


def wait_weights(target, k, sem):
    pltpu.make_async_copy(target.at[k], target.at[k], sem.at[k]).wait()


def live_cotangent(tab, cot, g):
    _, block, width = cot.shape
    position = tab[2] + lax.broadcasted_iota(jnp.int32, (block, width), 0)
    return jnp.where(position < tab[g], cot[g].astype(F32), 0.0)


def mlp_in_kernel(tab, tok, cot, mod, gain, upb, *rest):
    mixed, pieces, rest = (rest[:4], rest[4:8]), rest[8:16], rest[16:]
    after, att, second_t, gbr, gbr_t, sums, act, slope, w, wo, second, sem, sem_o = rest
    groups, block, width = tok.shape
    feats = mixed[0][0].shape[0]
    fh = upb.shape[1]
    k = pl.program_id(0)

    @pl.when(k == 0)
    def _():
        start_weights(tab, pieces, slice(fh, None), wo, sem_o)
        start_weights(tab, pieces, slice(0, fh), w, sem)
        for g in range(groups):
            here = slice(g * block, (g + 1) * block)
            gb = (mod[g, 5:6, :] * live_cotangent(tab, cot, g)).astype(BF)
            gbr[here, :] = gb
            sums[g : g + 1, :] = jnp.sum(gb.astype(F32), axis=0, keepdims=True)
        gbr_t[...] = gbr[...].T
        for r in range(4):
            wait_weights(wo, r, sem_o)
        for g in range(groups):
            here = slice(g * block, (g + 1) * block)
            total = jnp.zeros((block, width), F32)
            for r in range(4):
                total += lax.dot_general(
                    mixed[g][MIXED[r]][...].T,
                    wo[r, :, :feats],
                    NT,
                    preferred_element_type=F32,
                )
            att[g] = total
            rows_after = tok[g].astype(F32) + mod[g, 2:3, :] * total
            after[g] = rows_after
            n, _ = norm_rows(rows_after)
            x = n * (gain[...] * (1.0 + mod[g, 4:5, :])) + mod[g, 3:4, :]
            second[here, :] = x.astype(BF)
        second_t[...] = second[...].T

    c1, c3 = math.sqrt(2.0 / math.pi), 0.044715
    wait_weights(w, k, sem)
    bias = upb[pl.ds(tab[T_PART + k], 1), :]
    hidden = jnp.dot(second[...], w[k], preferred_element_type=F32) + bias
    square = hidden * hidden
    th = jnp.tanh(c1 * hidden * (1.0 + c3 * square))
    up = 0.5 * (1.0 + th)
    act[0] = (hidden * up).astype(BF)
    slope[0] = (
        up + (0.5 * c1) * hidden * (1.0 - th * th) * (1.0 + (3.0 * c3) * square)
    ).astype(BF)


def mlp_out_kernel(tab, mod, downb, gbr, act, slope, *rest):
    pieces, late, rest = rest[:8], rest[8:10], rest[10:]
    out, sums, upsum, gh, w, branch, cot, after, sem, sem_late = rest
    groups, block, width = cot.shape
    k = pl.program_id(0)

    @pl.when(k == 0)
    def _():
        start_weights(tab, pieces, slice(None), w, sem)
        start_late(late, (cot, after), sem_late)
        branch[...] = jnp.broadcast_to(downb[...], branch.shape)

    wait_weights(w, k, sem)
    ga = jnp.dot(gbr[...], w[k], preferred_element_type=F32)
    grad = (ga * slope[0].astype(F32)).astype(BF)
    gh[0] = grad
    upsum[pl.ds(tab[T_PART + k], 1), :] = jnp.sum(grad.astype(F32), axis=0, keepdims=True)
    branch[...] += lax.dot_general(act[0], w[k], NT, preferred_element_type=F32)

    @pl.when(k == 3)
    def _():
        wait_late(late, (cot, after), sem_late)
        for g in range(groups):
            here = slice(g * block, (g + 1) * block)
            out[g] = (after[g] + mod[g, 5:6, :] * branch[here, :]).astype(BF)
            sums[g : g + 1, :] = jnp.sum(
                live_cotangent(tab, cot, g) * branch[here, :], axis=0, keepdims=True
            )


def start_late(sources, targets, sem):
    for i, (source, target) in enumerate(zip(sources, targets)):
        pltpu.make_async_copy(source, target, sem.at[i]).start()


def wait_late(sources, targets, sem):
    for i, (source, target) in enumerate(zip(sources, targets)):
        pltpu.make_async_copy(source, target, sem.at[i]).wait()


def mlp_back_kernel(tab, mod, gain, gh, *rest):
    pieces, late, rest = rest[:8], rest[8:11], rest[11:]
    gmixed, rest = rest[:4], rest[4:]
    sums, gafter, gat_t, w, wo, gsec, gat, cot, after, att, sem, sem_o, sem_late = rest
    groups, block, width = cot.shape
    feats = gmixed[0].shape[0]
    fh = gh.shape[2]
    k = pl.program_id(0)

    @pl.when(k == 0)
    def _():
        start_weights(tab, pieces, slice(0, fh), w, sem)
        start_weights(tab, pieces, slice(fh, None), wo, sem_o)
        start_late(late, (cot, after, att), sem_late)
        gsec[...] = jnp.zeros_like(gsec)

    wait_weights(w, k, sem)
    gsec[...] += lax.dot_general(gh[0], w[k], NT, preferred_element_type=F32)

    @pl.when(k == 3)
    def _():
        wait_late(late, (cot, after, att), sem_late)
        for r in range(4):
            wait_weights(wo, r, sem_o)
        for g in range(groups):
            here = slice(g * block, (g + 1) * block)
            n, inverse = norm_rows(after[g])
            gs = gsec[here, :]
            sums[g, 0:1, :] = jnp.sum(gs, axis=0, keepdims=True)
            sums[g, 1:2, :] = jnp.sum(gs * n, axis=0, keepdims=True)
            scaled = gs * (gain[...] * (1.0 + mod[g, 4:5, :]))
            mean = jnp.mean(scaled, axis=1, keepdims=True)
            along = jnp.mean(scaled * n, axis=1, keepdims=True)
            grad = live_cotangent(tab, cot, g) + inverse * (scaled - mean - n * along)
            gafter[g] = grad
            sums[g, 2:3, :] = jnp.sum(grad * att[g], axis=0, keepdims=True)
            low = (mod[g, 2:3, :] * grad).astype(BF)
            gat[here, :] = low
            for r in range(4):
                gmixed[MIXED[r]][:, here] = (
                    jnp.dot(low, wo[r, :, :feats], preferred_element_type=F32)
                    .astype(BF)
                    .T
                )
        gat_t[...] = gat[...].T


def steps_call(
    kernel, name, tab, arrays, stepped, pieces, late, outs, stepped_outs, scratch, sems, flops
):
    sm = pl.BlockSpec(memory_space=pltpu.SMEM)

    def slot_spec(shape):
        return spec((1,) + shape[1:], lambda k: (k, 0, 0))

    return pl.pallas_call(
        kernel,
        grid=(4,),
        in_specs=[sm]
        + [whole(a.shape) for a in arrays]
        + [slot_spec(a.shape) for a in stepped]
        + [ANY] * (len(pieces) + len(late)),
        out_specs=[whole(a.shape) for a in outs] + [slot_spec(a.shape) for a in stepped_outs],
        out_shape=list(outs) + list(stepped_outs),
        scratch_shapes=scratch
        + [pltpu.VMEM(a.shape, a.dtype) for a in late]
        + [pltpu.SemaphoreType.DMA((4,))] * sems,
        compiler_params=params(),
        cost_estimate=cost(flops, 16 * 2**20),
        name=name,
    )(tab, *arrays, *stepped, *pieces, *late)


def struct(shape, dtype):
    return jax.ShapeDtypeStruct(shape, dtype)


def mlp_in_call(tab, tok, cot, mod, gain, upb, mixed, pieces):
    groups, block, width = tok.shape
    total, fh = groups * block, upb.shape[1]
    rows = struct((groups, block, width), F32)
    tall = struct((width, total), BF)
    wide = struct((4, total, fh), BF)

    return steps_call(
        mlp_in_kernel,
        "mlp_in",
        tab,
        [tok, cot, mod, gain, upb, *mixed[0], *mixed[1]],
        [],
        pieces,
        [],
        [rows, rows, tall, struct((total, width), BF), tall, struct((groups, width), F32)],
        [wide, wide],
        [
            pltpu.VMEM((4, width, fh), BF),
            pltpu.VMEM((4, width, pieces[0].shape[2] - fh), BF),
            pltpu.VMEM((total, width), BF),
        ],
        2,
        10 * total * width * fh,
    )


def mlp_out_call(tab, cot, mod, downb, after, gbr, act, slope, pieces):
    groups, block, width = cot.shape
    total, fh = groups * block, act.shape[2]
    return steps_call(
        mlp_out_kernel,
        "mlp_out",
        tab,
        [mod, downb, gbr],
        [act, slope],
        pieces,
        [cot, after],
        [
            struct((groups, block, width), BF),
            struct((groups, width), F32),
            struct((4, fh), F32),
        ],
        [struct((4, total, fh), BF)],
        [pltpu.VMEM((4, width, fh), BF), pltpu.VMEM((total, width), F32)],
        2,
        16 * total * width * fh,
    )


def mlp_back_call(tab, cot, mod, gain, after, att, gh, pieces, feats):
    groups, block, width = cot.shape
    total, fh = groups * block, gh.shape[2]
    return steps_call(
        mlp_back_kernel,
        "mlp_back",
        tab,
        [mod, gain],
        [gh],
        pieces,
        [cot, after, att],
        [
            *[struct((feats, groups * block), BF)] * 4,
            struct((groups, 3, width), F32),
            struct((groups, block, width), F32),
            struct((width, total), BF),
        ],
        [],
        [
            pltpu.VMEM((4, width, fh), BF),
            pltpu.VMEM((4, width, pieces[0].shape[2] - fh), BF),
            pltpu.VMEM((total, width), F32),
            pltpu.VMEM((total, width), BF),
        ],
        3,
        10 * total * width * fh,
    )


def store_grads(tab, k, src, sent, kept0, kept1, sem):
    rows = src.shape[1] // NBLK
    for b in range(NBLK):
        there = tab[k * NBLK + b]
        piece = src.at[k, pl.ds(b * rows, rows), :]

        @pl.when(k >= 2)
        def _():
            pltpu.make_async_copy(piece, sent.at[there], sem.at[k, b]).start()

        @pl.when((k < 2) & (there < 8))
        def _():
            pltpu.make_async_copy(piece, kept0.at[there], sem.at[k, b]).start()

        @pl.when((k < 2) & (there >= 8))
        def _():
            pltpu.make_async_copy(piece, kept1.at[there - 8], sem.at[k, b]).start()


def wait_grads(src, sent, sem):
    rows = src.shape[1] // NBLK
    for k in range(4):
        for b in range(NBLK):
            pltpu.make_async_copy(
                src.at[k, pl.ds(b * rows, rows), :], sent.at[0], sem.at[k, b]
            ).wait()


def down_grad_kernel(tab, gbr_t, act, sent, kept0, kept1, acc, sem):
    k = pl.program_id(0)
    acc[k] = jnp.dot(gbr_t[...], act[0], preferred_element_type=F32).astype(BF)
    store_grads(tab, k, acc, sent, kept0, kept1, sem)

    @pl.when(k == 3)
    def _():
        wait_grads(acc, sent, sem)


def up_grad_kernel(tab, second_t, gat_t, gh, *rest):
    mixed, (sent, kept0, kept1, acc, sem) = (rest[:4], rest[4:8]), rest[8:]
    k = pl.program_id(0)
    fh = gh.shape[2]
    feats, block = mixed[0][0].shape
    acc[k, :, :fh] = jnp.dot(second_t[...], gh[0], preferred_element_type=F32).astype(BF)
    if acc.shape[2] > fh + feats:
        acc[k, :, fh + feats :] = jnp.zeros((acc.shape[1], acc.shape[2] - fh - feats), BF)
    for r in range(4):

        @pl.when(k == r)
        def _():
            total = None
            for g in range(2):
                term = lax.dot_general(
                    gat_t[:, g * block : (g + 1) * block],
                    mixed[g][MIXED[r]][...],
                    NT,
                    preferred_element_type=F32,
                )
                total = term if total is None else total + term
            acc[k, :, fh : fh + feats] = total.astype(BF)

    store_grads(tab, k, acc, sent, kept0, kept1, sem)

    @pl.when(k == 3)
    def _():
        wait_grads(acc, sent, sem)


def grad_call(kernel, name, tab, fixed, moving, others, lanes):
    width, total = fixed[0].shape
    fh = moving.shape[2]
    rows = width // NBLK
    grid_spec = pltpu.PrefetchScalarGridSpec(
        num_scalar_prefetch=1,
        grid=(4,),
        in_specs=[whole(a.shape) for a in fixed]
        + [spec((1, total, fh), lambda k, _: (k, 0, 0))]
        + [whole(a.shape) for a in others],
        out_specs=[ANY, ANY, ANY],
        scratch_shapes=[
            pltpu.VMEM((4, width, lanes), BF),
            pltpu.SemaphoreType.DMA((4, NBLK)),
        ],
    )
    return pl.pallas_call(
        kernel,
        grid_spec=grid_spec,
        out_shape=[struct((16, rows, lanes), BF)] + [struct((8, rows, lanes), BF)] * 2,
        compiler_params=params(),
        cost_estimate=cost(8 * width * total * lanes, 14 * 2**20),
        name=name,
    )(tab, *fixed, moving, *others)


def norm_back_kernel(t0, t1, t2, tok, after, mod, gain, out):
    normed, inverse = norm_rows(tok[0].astype(F32))
    grad = t0[0, 0].astype(F32) + t1[0, 0].astype(F32) + t2[0].astype(F32)
    scaled = grad * (gain[...] * (1.0 + mod[0, 1:2, :]))
    mean = jnp.mean(scaled, axis=1, keepdims=True)
    along = jnp.mean(scaled * normed, axis=1, keepdims=True)
    out[0] = (after[0] + inverse * (scaled - mean - normed * along)).astype(BF)


def norm_back_call(t0, t1, t2, tok, after, mod, gain):
    groups, block, width = tok.shape
    row = spec((1, block, width), lambda g: (g, 0, 0))
    near = spec((1, 1, block, width), lambda g: (0, g, 0, 0))
    return pl.pallas_call(
        norm_back_kernel,
        grid=(groups,),
        in_specs=[near, near, row, row, row, spec((1, 6, width), lambda g: (g, 0, 0)), whole((1, width))],
        out_specs=row,
        out_shape=jax.ShapeDtypeStruct((groups, block, width), BF),
        compiler_params=params(),
        cost_estimate=cost(40 * groups * block * width, 12 * groups * block * width),
        name="norm_back",
    )(t0, t1, t2, tok, after, mod, gain)


AT = 640


def pack_kernel(one, two, gate_two, upsum, down_bias, mod, gain_one, gain_two, out):
    dp, tp, _, width = out.shape
    groups = one.shape[0]
    lane = lax.broadcasted_iota(jnp.int32, (1, width), 1)

    def window(rows, start, count, at=0):
        row, offset = divmod(start, width)
        first = min(count, width - offset)
        got = rows[row]
        shift = (at - offset) % width
        got = pltpu.roll(got, shift, 1) if shift else got
        if first < count:
            shift = (at + first) % width
            rest = rows[row + 1]
            rest = pltpu.roll(rest, shift, 1) if shift else rest
            got = jnp.where(lane < at + first, got, rest)
        return got

    mods, count_mod = [], 6 * width // dp
    for g in range(groups):
        mods.append(
            [
                one[g, 0:1, :],
                gain_one[...] * one[g, 1:2, :],
                two[g, 2:3, :],
                two[g, 0:1, :],
                gain_two[...] * two[g, 1:2, :],
                gate_two[g : g + 1, :],
            ]
        )
    zero = jnp.zeros((1, width), F32)
    vectors = [zero, zero, zero]
    for g in range(groups):
        vectors[0] += down_bias[g : g + 1, :]
        vectors[1] += (1.0 + mod[g, 1:2, :]) * one[g, 1:2, :]
        vectors[2] += (1.0 + mod[g, 4:5, :]) * two[g, 1:2, :]
    rows_up = [upsum[r : r + 1, :] for r in range(upsum.shape[0])]
    count_up, count = upsum.shape[0] * width // dp, width // dp
    for d in range(dp):
        firsts = [window(mods[g], d * count_mod, count_mod) for g in range(groups)]
        firsts.append(window(rows_up, d * count_up, count_up))
        for r in range(3):
            row = jnp.where(lane < AT, firsts[r], window([vectors[r]], d * count, count, AT))
            for t in range(tp):
                out[d, t, r : r + 1, :] = row


def pack_call(dp, tp, one, two, gate_two, upsum, down_bias, mod, gain_one, gain_two):
    vm = pl.BlockSpec(memory_space=pltpu.VMEM)
    return pl.pallas_call(
        pack_kernel,
        in_specs=[vm] * 8,
        out_specs=vm,
        out_shape=struct((dp, tp, 3, one.shape[2]), F32),
        compiler_params=params(),
        cost_estimate=cost(2**20, 2**20),
        name="pack",
    )(one, two, gate_two, upsum, down_bias, mod, gain_one, gain_two)


def small_kernel(got, cond_t, adaw, adab, upb, downb, gain_one, gain_two):
    dp = got.shape[0]
    cols = adaw.shape[0]
    total = jnp.sum(got[...], axis=1)
    mods = jnp.concatenate([total[:, 0, :], total[:, 1, :]], axis=0)
    product = lax.dot_general(
        mods,
        cond_t[...],
        (((0,), (1,)), ((), ())),
        precision=lax.Precision.HIGHEST,
        preferred_element_type=F32,
    )
    adaw[...] = product[:cols]
    flat = jnp.sum(total, axis=0)
    adab[...] = flat[0:1, :cols] + flat[1:2, :cols]
    upb[...] = flat[2:3, : upb.shape[1]]
    for row, ref in enumerate((downb, gain_one, gain_two)):
        ref[...] = flat[row : row + 1, AT : AT + ref.shape[1]]


def small_call(got, cond_t, cols, up_count, count):
    shapes = [(cols, cond_t.shape[0]), (1, cols), (1, up_count)] + [(1, count)] * 3
    vm = pl.BlockSpec(memory_space=pltpu.VMEM)
    return pl.pallas_call(
        small_kernel,
        in_specs=[vm, vm],
        out_specs=[vm] * 6,
        out_shape=[jax.ShapeDtypeStruct(shape, F32) for shape in shapes],
        compiler_params=params(),
        cost_estimate=cost(2**20, 2**20),
        name="small",
    )(got, cond_t)


def time_embedding(time_steps, width_total):
    half_width = width_total // 2
    frequency = jnp.exp(-math.log(10000.0) * jnp.arange(half_width, dtype=F32) / half_width)
    angles = time_steps.astype(F32)[:, None] * frequency[None, :]
    return jnp.concatenate([jnp.cos(angles), jnp.sin(angles)], axis=-1)


def rotary_halves(length_total):
    half = HEAD // 2
    inverse = jnp.exp(-math.log(10000.0) * 2.0 * jnp.arange(half, dtype=F32) / HEAD)
    angles = jnp.arange(length_total, dtype=F32)[:, None] * inverse[None, :]
    return jnp.cos(angles), jnp.sin(angles)


def device_index(z, y, x, c):
    return ((z * 2 + y) * 2 + x) * 2 + c


def permutation(move):
    pairs = []
    for z in range(4):
        for y in range(2):
            for x in range(2):
                for c in range(2):
                    pairs.append((device_index(z, y, x, c), device_index(*move(z, y, x, c))))
    return pairs


CORE = permutation(lambda z, y, x, c: (z, y, x, 1 - c))
FLIP_X = permutation(lambda z, y, x, c: (z, y, 1 - x, c))
FLIP_BOTH = permutation(lambda z, y, x, c: (z, y, 1 - x, 1 - c))
FLIP_Y = permutation(lambda z, y, x, c: (z, 1 - y, x, c))
FIRST = permutation(lambda z, y, x, c: (z, 1 - y, x, c) if c == 0 else (z, y, 1 - x, c))
SECOND = permutation(lambda z, y, x, c: (z, y, 1 - x, c) if c == 0 else (z, 1 - y, x, c))
ALONG_Z = [permutation(lambda z, y, x, c, s=s: ((z + s) % 4, y, x, c)) for s in range(4)]


def send(array, pairs):
    return lax.ppermute(array, ("dp", "tensor"), pairs)


def start_z(shard):
    return [shard] + [send(shard, ALONG_Z[s]) for s in (1, 2, 3)]


def gather_z(shard):
    return jnp.stack(start_z(shard))


def after_all(value, *others):
    flat, tree = jax.tree.flatten(value)
    tied = lax.optimization_barrier((tuple(flat), others))[0]
    return jax.tree.unflatten(tree, tied)


def add_low(*terms):
    return functools.reduce(jnp.add, [term.astype(F32) for term in terms]).astype(BF)


def exchange(arrays, fast):
    if fast:
        perms = (None, CORE, FLIP_X, FLIP_BOTH)
        return [arrays[0]] + [send(arrays[r], perms[r]) for r in (1, 2, 3)]
    return list(lax.all_to_all(jnp.stack(arrays), "tensor", 0, 0, tiled=True))


class Reduce:
    def __init__(self, sent, kept0, kept1):
        shape = (2, 4) + sent.shape[1:]
        self.kept = kept0.reshape(shape), kept1.reshape(shape)
        self.got = send(sent, CORE).reshape((2,) + shape)

    def one(self, *others):
        got = after_all(self.got, *others) if others else self.got
        self.got = got
        self.half = add_low(self.kept[1], got[1])
        return self.half

    def two(self, *others):
        self.got_two = after_all(send(self.half, SECOND), *others)
        self.quarter = add_low(self.kept[0][1], self.got[0, 1], self.got_two[1])
        return self.quarter

    def three(self, *others):
        self.got_three = after_all(send(self.quarter, FIRST), *others)
        self.parts = [
            add_low(self.kept[0][0, s], self.got[0, 0, s], self.got_two[0, s], self.got_three[s])
            for s in range(4)
        ]
        return self.parts

    def start_last(self):
        return [send(self.parts[s], ALONG_Z[s]) for s in (1, 2, 3)]

    def end_last(self, got):
        return functools.reduce(jnp.add, [g.astype(F32) for g in [self.parts[0]] + list(got)])


def tables(z, y, x, c):
    far_core = np.array([0, 0, 0, 0, 1, 1, 1, 1])
    kind = np.array([0, 1, 2, 3] * 2)
    core = jnp.bitwise_xor(c, far_core)
    rel_x = jnp.where(kind == 0, 0, jnp.where(kind == 3, 1, jnp.where(kind == 1, core, 1 - core)))
    rel_y = jnp.where(kind == 0, 0, jnp.where(kind == 3, 1, jnp.where(kind == 1, 1 - core, core)))
    slots = far_core * 2 + rel_x
    back = np.arange(4)
    from_z = jnp.remainder(z - back, 4)
    weight_rows = (from_z[None, :] * 2 + jnp.bitwise_xor(y, rel_y)[:, None]).reshape(32)
    slot = np.arange(4)
    parts = jnp.bitwise_xor(x, slot % 2) * 2 + jnp.bitwise_xor(c, slot // 2)
    block = np.arange(NBLK)
    to_z = jnp.remainder(block // 2 - z, 4)
    to_y = jnp.bitwise_xor(block % 2, y)
    slot_core = jnp.bitwise_xor(c, slot // 2)[:, None]
    to_x = (slot % 2)[:, None]
    major = jnp.where(slot_core == 0, to_x, to_y[None, :])
    minor = jnp.where(slot_core == 0, to_y[None, :], to_x)
    targets = (major * 8 + minor * 4 + to_z[None, :]).reshape(4 * NBLK)
    qkv_rows = jnp.concatenate(
        [from_z * 2 + y, from_z * 2 + (1 - y)]
    )
    qkv_targets = to_y * 4 + to_z
    return parts, weight_rows, slots, targets, qkv_rows, qkv_targets


def shards(
    tokens,
    lengths,
    times,
    cotangent,
    w_qkv,
    w_out,
    w_up,
    up_bias,
    w_down,
    down_bias,
    norm1_gain,
    norm2_gain,
    ada_weight,
    ada_bias,
):
    groups, block, width = tokens.shape
    dp, tp = lax.axis_size("dp"), lax.axis_size("tensor")
    seq = block * tp
    t = lax.axis_index("tensor")
    d = lax.axis_index("dp")
    fast = dp == 8 and tp == 4
    feats = w_qkv.shape[2]
    fh = w_up.shape[1]
    rows = width // NBLK
    zero = jnp.zeros((), jnp.int32)
    z, y, x, c = (d // 2, d % 2, t // 2, t % 2) if fast else (zero, zero, zero, zero)
    here = t if fast else zero
    parts, weight_rows, slots, targets, qkv_rows, qkv_targets = tables(z, y, x, c)

    all_times = lax.all_to_all(
        jnp.broadcast_to(times[None, :], (dp, groups)), "dp", 0, 0, tiled=True
    ).reshape(-1)
    pad = (-feats) % 128
    qkv_shard = jnp.pad(w_qkv, ((0, 0), (0, 0), (0, pad)))
    if fast:
        near = gather_z(qkv_shard)
        qkv_pieces = (near, send(near, FLIP_Y))
    else:
        full = lax.all_gather(qkv_shard, "dp", axis=1, tiled=True)
        full = full.reshape(3, NBLK, rows, feats + pad).transpose(1, 0, 2, 3)
        order = [[(-j) % 4 * 2 + p for j in range(4)] for p in range(2)]
        qkv_pieces = tuple(jnp.stack([full[b] for b in order[p]]) for p in range(2))
    tok_all = lax.all_gather(tokens, "tensor", axis=1, tiled=True)

    condition = time_embedding(all_times, ada_weight.shape[0])
    part = jnp.dot(
        condition, ada_weight.astype(F32), precision=lax.Precision.HIGHEST
    ) + ada_bias.astype(F32)
    cols = part.shape[1]
    vectors = jnp.concatenate([up_bias, down_bias, norm1_gain, norm2_gain]).astype(F32)
    sent_mod = jnp.concatenate(
        [
            part.reshape(dp, groups * cols),
            jnp.broadcast_to(vectors[None, :], (dp, vectors.shape[0])),
        ],
        axis=1,
    )
    payload = lax.all_to_all(sent_mod, "dp", 0, 0, tiled=True)
    mod = (
        payload[:, : groups * cols]
        .reshape(dp, groups, cols)
        .transpose(1, 0, 2)
        .reshape(groups, 6, width)
    )
    at = groups * cols
    small = []
    for count in (up_bias.shape[0], down_bias.shape[0], norm1_gain.shape[0], norm2_gain.shape[0]):
        small.append(payload[:, at : at + count].reshape(-1))
        at += count
    upb_all = small[0].reshape(tp, fh)
    downb_all, gain_one, gain_two = (v.reshape(1, width) for v in small[1:])

    up_shard = jnp.pad(
        jnp.concatenate([w_up, w_out.T], axis=1), ((0, 0), (0, (-fh - feats) % 128))
    )
    down_shard = w_down.T
    if fast:
        up_shard, down_shard = after_all((up_shard, down_shard), qkv_pieces[1], payload)
        up_parts = start_z(up_shard)
        down_parts = start_z(down_shard)
    else:

        def gather_pieces(shard):
            full = lax.all_gather(shard, "dp", axis=0, tiled=True)
            full = lax.all_gather(full, "tensor", axis=0, tiled=False)
            full = full.reshape(tp, NBLK, rows, full.shape[2])
            return [
                jnp.stack([full[rel_x * 2 + far, b] for b in order[rel_y]])
                for far in range(2)
                for rel_x, rel_y in ((0, 0), (far, 1 - far), (1 - far, far), (1, 1))
            ]

    cos, sin = rotary_halves(seq)
    heads_wide = (feats + pad) // HEAD
    cos_wide = jnp.tile(jnp.concatenate([cos, cos], axis=1), (1, heads_wide))
    sin_wide = jnp.tile(jnp.concatenate([-sin, sin], axis=1), (1, heads_wide))
    first_all, q, k, v, kt, vt, w_all = qkv_call(
        qkv_rows.astype(jnp.int32), tok_all, mod, gain_one, cos_wide, sin_wide, *qkv_pieces
    )
    vt_later = vt
    if fast:
        up_near = jnp.stack(after_all(up_parts, vt))
        vt = after_all(vt, up_near)
        up_one, up_two = send(up_near, FIRST), send(up_near, SECOND)
    small_tab = jnp.concatenate([lengths, here.reshape(1)]).astype(jnp.int32)
    *mixed0, probs0 = attend_call(0, small_tab, q, k, vt)
    if fast:
        mixed0, up_near, up_one, up_two, down_parts = after_all(
            (mixed0, up_near, up_one, up_two, down_parts), probs0
        )
        vt_later = after_all(vt, up_one, up_two)
        mixed0_all = exchange(mixed0, fast)
        up_both = send(up_one, SECOND)
        up_far = [send(piece, CORE) for piece in (up_near, up_one, up_two)]
    *mixed1, probs1 = attend_call(1, small_tab, q, k, vt_later)
    if fast:
        mixed1, up_both = after_all((mixed1, up_both), probs1, *mixed0_all)
        mixed1 = after_all(mixed1, up_both)
        up_far.append(send(up_both, CORE))
        up_pieces = [up_near, up_one, up_two, up_both] + up_far
    else:
        up_pieces, down_pieces = gather_pieces(up_shard), gather_pieces(down_shard)
        mixed0_all = exchange(mixed0, fast)
    mixed1_all = exchange(mixed1, fast)

    tab = jnp.concatenate([lengths, (t * block).reshape(1), parts, weight_rows, slots]).astype(
        jnp.int32
    )
    if fast:
        down_parts, up_pieces = after_all((down_parts, up_pieces), *mixed1_all)
        down_near = jnp.stack(down_parts)
        up_pieces = after_all(up_pieces, down_near)
        down_one, down_two = send(down_near, FIRST), send(down_near, SECOND)
    after, att, second_t, gbr, gbr_t, sum_down_bias, act, slope = mlp_in_call(
        tab, tokens, cotangent, mod, gain_two, upb_all, (mixed0_all, mixed1_all), up_pieces
    )
    targets = targets.astype(jnp.int32)
    if fast:
        down_one, down_two, act = after_all((down_one, down_two, act), after)
        act = after_all(act, down_one, down_two)
        down_both = send(down_one, SECOND)
        down_far = [send(piece, CORE) for piece in (down_near, down_one, down_two)]
    gd_s, *gd_k = grad_call(down_grad_kernel, "down_grad", targets, [gbr_t], act, [], fh)
    if fast:
        gd_s, down_both, down_far = after_all((gd_s, down_both, down_far), *gd_k)
        gd_s = after_all(gd_s, down_both, *down_far)
        down_sum = Reduce(gd_s, *gd_k)
        down_far.append(send(down_both, CORE))
        down_pieces = [down_near, down_one, down_two, down_both] + down_far
    out, sum_gate_two, upsum, gh = mlp_out_call(
        tab, cotangent, mod, downb_all, after, gbr, act, slope, down_pieces
    )
    if fast:
        gh = after_all(gh, down_sum.one(gh))
    *gms, sums_two, grad_after, gat_t = mlp_back_call(
        tab, cotangent, mod, gain_two, after, att, gh, up_pieces, feats
    )
    if fast:
        gms, gh, quarter = after_all((gms, gh, down_sum.two(grad_after)), down_sum.got_two)
    gm = exchange(gms, fast)
    if fast:
        gh = after_all(gh, quarter)
    gu_s, *gu_k = grad_call(
        up_grad_kernel,
        "up_grad",
        targets,
        [second_t, gat_t],
        gh,
        [*mixed0_all, *mixed1_all],
        up_pieces[0].shape[2],
    )
    here_tab = here.reshape(1).astype(jnp.int32)
    if fast:
        down_sum.three(*gu_k)
        gu_s = after_all(gu_s, down_sum.got_three, *gm)
        up_sum = Reduce(gu_s, *gu_k)
        down_got = down_sum.start_last()
        gm = after_all(gm, up_sum.one(*down_sum.parts))
    grad_t0 = attend_back_call(0, here_tab, q, kt, v, probs0, gm, cos.T, sin.T)
    if fast:
        down_got = after_all(down_got, grad_t0)
        gm = after_all(gm, up_sum.two(grad_t0, *down_got))
    grad_t1 = attend_back_call(1, here_tab, q, kt, v, probs1, gm, cos.T, sin.T)
    if fast:
        grad_t1 = after_all(grad_t1, *up_sum.three(grad_t1))
    fts, ftk, sums_one, dws, dwk = qkv_back_call(
        jnp.concatenate([qkv_targets, here.reshape(1)]).astype(jnp.int32),
        grad_t0,
        grad_t1,
        first_all,
        tok_all,
        w_all,
    )

    if fast:
        up_got = up_sum.start_last()
        fts, dws, sums_one, sums_two = after_all((fts, dws, sums_one, sums_two), *up_got)
        got, got_dw = send(fts, CORE), send(dws, FLIP_Y)
        far = send(add_low(ftk[1], got[1]), FLIP_X)
    else:

        def absolute(sent, kept):
            lanes = sent.shape[2]
            near = kept.reshape(2, 2, 4, rows, lanes)
            far = sent.reshape(2, 2, 4, rows, lanes).transpose(1, 0, 2, 3, 4)
            both = jnp.stack([near, far], axis=1)
            return both.transpose(0, 1, 3, 2, 4, 5).reshape(tp, width, lanes).astype(F32)

        def reduce_all(sent, kept):
            terms = lax.psum_scatter(
                absolute(sent, kept), "tensor", scatter_dimension=0, tiled=True
            )[0]
            return lax.psum_scatter(terms, "dp", scatter_dimension=0, tiled=True)

        sum_up = reduce_all(gu_s, jnp.concatenate(gu_k))
        sum_down = reduce_all(gd_s, jnp.concatenate(gd_k))
        terms = jnp.stack([dwk, dws]).transpose(2, 1, 0, 3, 4)
        terms = terms.reshape(3, width, feats + pad).astype(F32)
        sum_qkv = lax.psum_scatter(terms, "dp", scatter_dimension=1, tiled=True)
        terms = jnp.stack([ftk, fts], axis=1).reshape(tp, groups, block, width).astype(F32)
        grad_first = lax.psum_scatter(terms, "tensor", scatter_dimension=0, tiled=True)[0]
        nought = jnp.zeros_like(grad_first)
        grad_in = norm_back_call(
            grad_first[None], nought[None], nought, tokens, grad_after, mod, gain_one
        )

    up_count, count = up_bias.shape[0], down_bias.shape[0]
    payload = pack_call(
        dp,
        tp,
        sums_one,
        sums_two,
        sum_gate_two,
        upsum,
        sum_down_bias,
        mod,
        gain_one,
        gain_two,
    ).reshape(dp * tp, 3, width)
    payload = lax.all_to_all(payload, ("dp", "tensor"), 0, 0, tiled=True)
    cond_t = condition.reshape(dp, groups, -1).transpose(2, 1, 0).reshape(-1, dp * groups)
    grad_adaw, grad_adab, g_up, g_down, g_one, g_two = small_call(
        payload.reshape(dp, tp, 3, width), cond_t, cols, up_count, count
    )
    if fast:
        got_dw = after_all(got_dw, grad_adaw)
        dw_parts = [add_low(dwk[s], got_dw[s]) for s in range(4)]
        dw_got = [send(dw_parts[s], ALONG_Z[s]) for s in (1, 2, 3)]
        far, up_got = after_all((far, up_got), *dw_parts)
        grad_in = norm_back_call(ftk, got, far, tokens, grad_after, mod, gain_one)
        dw_got = after_all(dw_got, grad_in)
        sum_up = up_sum.end_last(up_got)
        sum_down = down_sum.end_last(down_got)
        sum_qkv = functools.reduce(jnp.add, [g.astype(F32) for g in [dw_parts[0]] + dw_got])

    return (
        out,
        grad_in,
        sum_qkv[:, :, :feats],
        sum_up[:, fh : fh + feats].T,
        sum_up[:, :fh],
        g_up[0],
        sum_down.T,
        g_down[0],
        g_one[0],
        g_two[0],
        grad_adaw.T,
        grad_adab[0],
    )


def solution(mesh):
    in_specs = (
        P("dp", "tensor", None),
        P("dp"),
        P("dp"),
        P("dp", "tensor", None),
        P(None, "dp", "tensor"),
        P("tensor", "dp"),
        P("dp", "tensor"),
        P("dp"),
        P("tensor", "dp"),
        P("dp"),
        P("dp"),
        P("dp"),
        P(None, "dp"),
        P("dp"),
    )
    out_specs = (
        P("dp", "tensor", None),
        P("dp", "tensor", None),
        P(None, "dp", "tensor"),
        P("tensor", "dp"),
        P("dp", "tensor"),
        P("dp"),
        P("tensor", "dp"),
        P("dp"),
        P("dp"),
        P("dp"),
        P(None, "dp"),
        P("dp"),
    )
    return jax.shard_map(shards, mesh=mesh, in_specs=in_specs, out_specs=out_specs, check_vma=False)
```

time: 342 us -> 323 us (0.944); the launches traced: 340 us -> 317 us
  waiting for transfers between devices: 77.8 us -> 45.4 us
  Pallas kernels: 119 us -> 143 us
  starting transfers between devices: 78.7 us -> 64.3 us
    pallas_call x3 -> x8, Pallas kernels: 57.6 us -> 80.8 us  [the longest x3 36.6 us: steps_call(): pl.pallas_call(kernel, grid=(4,), in_specs=[sm] + [whole(a.shape) for a i...]
    ppermute x42 -> x51, waiting for transfers between devices: 46.6 us -> 26.4 us  [send(): return lax.ppermute(array, ('dp', 'tensor'), pairs)]
    all_to_all x4 -> x0, starting transfers between devices: 14.7 us -> none  [the longest x1 4.12 us: shards(): gm1 = lax.all_to_all(after_all(gm1, gm0), 'tensor', 0, 0, tiled=True)]
    all_to_all x4 -> x0, waiting for transfers between devices: 11.3 us -> none  [the longest x1 6.06 us: shards(): gm0 = lax.all_to_all(gm0, 'tensor', 0, 0, tiled=True)]
    ppermute x42 -> x51, starting transfers between devices: 53.5 us -> 52.4 us  [send(): return lax.ppermute(array, ('dp', 'tensor'), pairs)]
  transfers between devices with their start and end apart: 50 -> 55, of which waited for: 14 -> 13; matrix products, arithmetic and copies ran while one was open for 12% -> 9% of each run, Pallas kernels for 21% -> 45%
where the time goes in v3:
time: 323 us; the launch traced here: 317 us
  Pallas kernels  143 us (44%)
  starting transfers between devices  64.3 us (20%)
  waiting for transfers between devices  45.4 us (14%)
  other arithmetic  29.8 us (9%)
  local copies, waits for them, and re-layouts  18.7 us (6%)
  between operations  15.4 us (5%)
    ppermute x51, starting transfers between devices, send(): return lax.ppermute(array, ('dp', 'tensor'), pairs)  52.4 us
    pallas_call x3, Pallas kernels, steps_call(): pl.pallas_call(kernel, grid=(4,), in_specs=[sm] + [whole(a.shape) for a i...  36.6 us
    pallas_call x2, Pallas kernels, attend_call(): pl.pallas_call(functools.partial(attend_kernel, group=group), grid_spec=g...  28.5 us
    ppermute x51, waiting for transfers between devices, send(): return lax.ppermute(array, ('dp', 'tensor'), pairs)  26.4 us
    pallas_call x2, Pallas kernels, attend_back_call(): pl.pallas_call(attend_back_kernel, grid_spec=grid_spec, out_shape=jax.Sha...  25.5 us
    convert_element_type x8, other arithmetic, add_low(): functools.reduce(jnp.add, [term.astype(F32) for term in terms]).astype(BF)  18.2 us
    pallas_call x2, Pallas kernels, grad_call(): pl.pallas_call(kernel, grid_spec=grid_spec, out_shape=[struct((16, rows,...  16.9 us
    pallas_call x1, Pallas kernels, qkv_call(): pl.pallas_call(qkv_kernel, grid_spec=grid_spec, out_shape=[jax.ShapeDtype...  14.2 us
  transfers between devices with their start and end apart: 55, of which 13 were waited for; matrix products, arithmetic and copies ran while one was open for 9% of the time, Pallas kernels for 45%

profile of v3, /device:TPU:0, one launch (start us, length us, event | category | flops | bytes accessed | tf_op | source)
XLA Modules:
  0.0 316.8 jit_solution(15075598428781171235)
XLA Ops:
  8.9 3.1 collective-permute-start
  11.9 2.6 collective-permute-start.1
  17.1 3.3 %all-to-all-start = ((s32[8,1,2]{2,1,0:T(1,128)}), s32[8,1,2]{2,1,0:T(1,128)S(1)}, u32[]{:S(2)}, u32[]{:S(2)}) async-start(s32[8,1,2]{2,1,0:T(1,128)} %broadcast_in_dim.78), calls=%async_computation | async-start | bytes 8192 | tf_op jit(solution)/shard_map/all_to_all | solution.py:1040
  25.1 3.2 %all-to-all-done = s32[8,1,2]{2,1,0:T(1,128)S(1)} async-done(((s32[8,1,2]{2,1,0:T(1,128)}), s32[8,1,2]{2,1,0:T(1,128)S(1)}, u32[]{:S(2)}, u32[]{:S(2)}) %all-to-all-start) | async-done | bytes 96 | tf_op jit(solution)/shard_map/all_to_all | solution.py:1040
  30.3 3.8 %all-to-all-start.1 = ((f32[8,1,1824]{2,1,0:T(1,128)}), f32[8,1,1824]{2,1,0:T(1,128)S(1)}, u32[]{:S(2)}, u32[]{:S(2)}) async-start(f32[8,1,1824]{2,1,0:T(1,128)} %all_to_all.16), calls=%async_computation.1 | async-start | bytes 122880 | tf_op jit(solution)/shard_map/all_to_all | solution.py:1068
  34.7 10.0 %all-to-all-done.1 = f32[8,1,1824]{2,1,0:T(1,128)S(1)} async-done(((f32[8,1,1824]{2,1,0:T(1,128)}), f32[8,1,1824]{2,1,0:T(1,128)S(1)}, u32[]{:S(2)}, u32[]{:S(2)}) %all-to-all-start.1) | async-done | bytes 58400 | tf_op jit(solution)/shard_map/all_to_all | solution.py:1068
  47.4 2.7 collective-permute-start.6
  50.1 14.2 %qkv.1 = (bf16[2,1024,768]{2,1,0:T(8,128)(2,1)}, bf16[2,3,1024,64]{3,2,1,0:T(8,128)(2,1)}, bf16[2,3,1024,64]{3,2,1,0:T(8,128)(2,1)}, bf16[2,3,1024,64]{3,2,1,0:T...) custom-call(s32[8]{0:T(128)} %pad_add_fusion.1.tab, ...), custom_call_target="tpu_custom_call" | custom-call | flops 2415919104 | bytes 16777216 | tf_op jit(solution)/shard_map/qkv/pallas_call | solution.py:128
  65.1 1.5 collective-permute-start.8
  67.2 2.0 collective-permute-start.10
  69.2 3.0 collective-permute-start.11
  72.4 14.2 %attend.2 = (bf16[192,256]{1,0:T(8,128)(2,1)}, bf16[192,256]{1,0:T(8,128)(2,1)}, bf16[192,256]{1,0:T(8,128)(2,1)}, bf16[192,256]{1,0:T(8,128)(2,1)}, bf16[3,1024,1024]{2,1,0:T(8,128)(2,1)}) custom-call(s32[3]{0:T(128)} %pad_add_fusion.tab, bf16[2,3,1024,64]{3,2,1,0:T(8,128)(2,1)} %get-tuple-element.160.q, bf16[2,3,1024,64]{3,2,1,0:T(8,128)(2,1)} %get-tuple-element.161.k, ...), custom_call_target="tpu_custom_call" | custom-call | flops 3221225472 | bytes 10485760 | tf_op jit(solution)/shard_map/attend/pallas_call | solution.py:194
  90.2 14.2 %attend.3 = (bf16[192,256]{1,0:T(8,128)(2,1)}, bf16[192,256]{1,0:T(8,128)(2,1)}, bf16[192,256]{1,0:T(8,128)(2,1)}, bf16[192,256]{1,0:T(8,128)(2,1)}, bf16[3,1024,1024]{2,1,0:T(8,128)(2,1)}) custom-call(s32[3]{0:T(128)} %pad_add_fusion.tab, bf16[2,3,1024,64]{3,2,1,0:T(8,128)(2,1)} %get-tuple-element.160.q, bf16[2,3,1024,64]{3,2,1,0:T(8,128)(2,1)} %get-tuple-element.161.k, ...), custom_call_target="tpu_custom_call" | custom-call | flops 3221225472 | bytes 10485760 | tf_op jit(solution)/shard_map/attend/pallas_call | solution.py:194
  105.4 1.5 collective-permute-start.17
  107.4 3.8 %collective-permute-done.17.rest_6_ = bf16[192,256]{1,0:T(8,128)(2,1)S(1)} collective-permute-done((bf16[192,256]{1,0:T(8,128)(2,1)}, bf16[192,256]{1,0:T(8,128)(2,1)S(1)}, u32[]{:S(2)}, u32[]{:S(2)}) %collective-permute-start.17) | collective-permute-done | bytes 98336 | tf_op jit(solution)/shard_map/ppermute | solution.py:923
  118.0 14.3 %mlp_in.1 = (f32[2,256,768]{2,1,0:T(8,128)}, f32[2,256,768]{2,1,0:T(8,128)}, bf16[768,512]{1,0:T(8,128)(2,1)}, bf16[512,768]{1,0:T(8,128)(2,1)}, bf16[768,512]{1...) custom-call(s32[47]{0:T(128)} %concatenate.37.tab, ...), custom_call_target="tpu_custom_call" | custom-call | flops 3019898880 | bytes 16777216 | tf_op jit(solution)/shard_map/mlp_in/pallas_call | solution.py:568
  134.5 7.4 %down_grad.1 = (bf16[16,96,768]{2,1,0:T(8,128)(2,1)}, bf16[8,96,768]{2,1,0:T(8,128)(2,1)}, bf16[8,96,768]{2,1,0:T(8,128)(2,1)}) custom-call(s32[32]{0:T(128)} %add.244.tab, bf16[768,512]{1,0:T(8,128)(2,1)} %get-tuple-element.229.gbr_t, bf16[4,512,768]{2,1,0:T(8,128)(2,1)} %get-tuple-element.227.act), custom_call_target="tpu_custom_call" | custom-call | flops 2415919104 | bytes 14680064 | tf_op jit(solution)/shard_map/down_grad/pallas_call | solution.py:753
  144.5 4.4 %collective-permute-done.29.rest_7_ = bf16[4,96,768]{2,1,0:T(8,128)(2,1)S(1)} collective-permute-done((bf16[4,96,768]{2,1,0:T(8,128)(2,1)}, bf16[4,96,768]{2,1,0:T(8,128)(2,1)S(1)}, u32[]{:S(2)}, u32[]{:S(2)}) %collective-permute-start.29) | collective-permute-done | bytes 589856 | tf_op jit(solution)/shard_map/ppermute | solution.py:923
  149.8 11.1 %mlp_out.1 = (bf16[2,256,768]{2,1,0:T(8,128)(2,1)}, f32[2,768]{1,0:T(2,128)}, f32[4,768]{1,0:T(4,128)}, bf16[4,512,768]{2,1,0:T(8,128)(2,1)}) custom-call(s32[47]{0:T(128)} %concatenate.37.tab, f32[2,6,768]{2,1,0:T(8,128)} %reshape.287.mod, f32[1,768]{1,0:T(1,128)} %reshape_reshape.12.downb, bf16[512,768]{1,0:T(8,128)(2,1)} %get-tuple-element.221.gbr, ...), custom_call_target="tpu_custom_call" | custom-call | flops 4831838208 | bytes 16777216 | tf_op jit(solution)/shard_map/mlp_out/pallas_call | solution.py:568
  160.9 3.4 %fusion.1 = bf16[2,4,96,768]{3,2,1,0:T(8,128)(2,1)} fusion(bf16[2,4,96,768]{3,2,1,0:T(8,128)(2,1)} %bitcast.199, bf16[2,2,4,96,768]{4,3,2,1,0:T(8,128)(2,1)S(1)} %bitcast.192), kind=kLoop, calls=%fused_computation.3 | loop fusion | flops 2359296 | bytes 3538944 | tf_op jit(solution)/shard_map/convert_element_type | solution.py:941
  165.1 11.2 %mlp_back.1 = (bf16[192,512]{1,0:T(8,128)(2,1)}, bf16[192,512]{1,0:T(8,128)(2,1)}, bf16[192,512]{1,0:T(8,128)(2,1)}, bf16[192,512]{1,0:T(8,128)(2,1)}, f32[2,3,7...) custom-call(s32[47]{0:T(128)} %concatenate.37.tab, f32[2,6,768]{2,1,0:T(8,128)} %reshape.287.mod, ...), custom_call_target="tpu_custom_call" | custom-call | flops 3019898880 | bytes 16777216 | tf_op jit(solution)/shard_map/mlp_back/pallas_call | solution.py:568
  176.3 4.5 %collective-permute-done.31 = bf16[2,4,96,768]{3,2,1,0:T(8,128)(2,1)} collective-permute-done((bf16[2,4,96,768]{3,2,1,0:T(8,128)(2,1)}, bf16[2,4,96,768]{3,2,1,0:T(8,128)(2,1)}, u32[]{:S(2)}, u32[]{:S(2)}) %collective-permute-start.31) | collective-permute-done | bytes 1179680 | tf_op jit(solution)/shard_map/ppermute | solution.py:923
  180.9 2.3 fusion.3
  186.2 9.5 %up_grad.1 = (bf16[16,96,1024]{2,1,0:T(8,128)(2,1)}, bf16[8,96,1024]{2,1,0:T(8,128)(2,1)}, bf16[8,96,1024]{2,1,0:T(8,128)(2,1)}) custom-call(s32[32]{0:T(128)} %add.244.tab, bf16[768,512]{1,0:T(8,128)(2,1)} %get-tuple-element.256.second_t, bf16[768,512]{1,0:T(8,128)(2,1)} %get-tuple-element.257.gat_t, bf16[4,512,768]{2,1,0:T(8,128)(2,1)} %get-tuple-element.258.gh, ...), custom_call_target="tpu_custom_call" | custom-call | flops 3221225472 | bytes 14680064 | tf_op jit(solution)/shard_map/up_grad/pallas_call | solution.py:753
  195.8 4.4 %collective-permute-done.34.gm3 = bf16[192,512]{1,0:T(8,128)(2,1)S(1)} collective-permute-done((bf16[192,512]{1,0:T(8,128)(2,1)S(1)}, bf16[192,512]{1,0:T(8,128)(2,1)S(1)}, u32[]{:S(2)}, u32[]{:S(2)}) %collective-permute-start.34) | collective-permute-done | bytes 196640 | tf_op jit(solution)/shard_map/ppermute | solution.py:923
  200.8 2.5 fusion.11
  203.3 3.4 %collective-permute-done.36 = bf16[16,96,1024]{2,1,0:T(8,128)(2,1)S(1)} collective-permute-done((bf16[16,96,1024]{2,1,0:T(8,128)(2,1)}, bf16[16,96,1024]{2,1,0:T(8,128)(2,1)S(1)}, u32[]{:S(2)}, u32[]{:S(2)}) %collective-permute-start.36) | collective-permute-done | bytes 3145760 | tf_op jit(solution)/shard_map/ppermute | solution.py:923
  206.7 1.9 fusion
  211.2 3.7 %collective-permute-start.39 = (bf16[96,768]{1,0:T(8,128)(2,1)}, bf16[96,768]{1,0:T(8,128)(2,1)S(1)}, u32[]{:S(2)}, u32[]{:S(2)}) collective-permute-start(bf16[96,768]{1,0:T(8,128)(2,1)} %get-tuple-element.363), channel_id=1, source_target_pairs={{0,16},{1,17},{2,18},{3,19},{4,20},{5,21},{6,22},{7,23},{8,24},{9,... | collective-permute-start | bytes 442376 | tf_op jit(solution)/shard_map/ppermute | solution.py:923
  214.9 12.9 %attend_back.2.gt0 = bf16[3,192,1024]{2,1,0:T(8,128)(2,1)} custom-call(s32[1]{0:T(128)} %bitcast.2.tab, bf16[2,3,1024,64]{3,2,1,0:T(8,128)(2,1)} %get-tuple-element.160.q, bf16[2,192,1024]{2,1,0:T(8,128)(2,1)} %get-tuple-element.238.kt, bf16[2,3,1024,64]{3,2,1,0:T(8,128)(2,1)} %get-tuple-element.239.v, bf16[3,1024,1024]{2,1,0:T(8,128)(2,1)} %get-tuple-element.174.probs, ...), custom_call_target="tpu_custom_call" | custom-call | flops 6442450944 | bytes 10485760 | tf_op jit(solution)/shard_map/attend_back/pallas_call | solution.py:278
  229.3 1.8 fusion.2
  232.9 12.6 %attend_back.3.gt1 = bf16[3,192,1024]{2,1,0:T(8,128)(2,1)} custom-call(s32[1]{0:T(128)} %bitcast.2.tab, bf16[2,3,1024,64]{3,2,1,0:T(8,128)(2,1)} %get-tuple-element.160.q, bf16[2,192,1024]{2,1,0:T(8,128)(2,1)} %get-tuple-element.238.kt, bf16[2,3,1024,64]{3,2,1,0:T(8,128)(2,1)} %get-tuple-element.239.v, bf16[3,1024,1024]{2,1,0:T(8,128)(2,1)} %get-tuple-element.186.probs, ...), custom_call_target="tpu_custom_call" | custom-call | flops 6442450944 | bytes 10485760 | tf_op jit(solution)/shard_map/attend_back/pallas_call | solution.py:278
  245.6 3.0 fusion.7
  248.6 2.0 collective-permute-start.42
  250.6 2.4 collective-permute-start.43
  253.0 13.5 %qkv_back.1 = (bf16[2,2,256,768]{3,2,1,0:T(8,128)(2,1)}, bf16[2,2,256,768]{3,2,1,0:T(8,128)(2,1)}, f32[2,2,768]{2,1,0:T(2,128)}, bf16[4,3,96,256]{3,2,1,0:T(8,128)(2,1)}, bf16[4,3,96,256]{3,2,1,0:T(8,128)(2,1)}) custom-call(s32[9]{0:T(128)} %pad_add_fusion.2.tab, bf16[3,192,1024]{2,1,0:T(8,128)(2,1)} %attend_back.2.gt0, ...), custom_call_target="tpu_custom_call" | custom-call | flops 4831838208 | bytes 16777216 | tf_op jit(solution)/shard_map/qkv_back/pallas_call | solution.py:381
  267.3 1.8 pack.1
  269.1 4.7 %all-to-all-start.2 = ((f32[32,3,768]{2,1,0:T(4,128)}), f32[32,3,768]{2,1,0:T(4,128)S(1)}, u32[]{:S(2)}, u32[]{:S(2)}) async-start(f32[32,3,768]{2,1,0:T(4,128)} %bitcast.196), calls=%async_computation.2 | async-start | bytes 786432 | tf_op jit(solution)/shard_map/all_to_all | solution.py:1250
  273.8 1.8 collective-permute-start.47
  275.6 1.9 fusion.4
  277.5 1.5 collective-permute-start.46
  279.9 1.8 add_bitcast_fusion
  281.8 5.2 %all-to-all-done.2 = f32[32,3,768]{2,1,0:T(4,128)S(1)} async-done(((f32[32,3,768]{2,1,0:T(4,128)}), f32[32,3,768]{2,1,0:T(4,128)S(1)}, u32[]{:S(2)}, u32[]{:S(2)}) %all-to-all-start.2) | async-done | bytes 294944 | tf_op jit(solution)/shard_map/all_to_all | solution.py:1250
  287.7 2.2 small.1
  295.1 1.7 collective-permute-start.48
  296.8 2.3 collective-permute-start.49
  302.1 3.8 %norm_back.1 = bf16[2,256,768]{2,1,0:T(8,128)(2,1)} custom-call(bf16[2,2,256,768]{3,2,1,0:T(8,128)(2,1)} %get-tuple-element.281.t0, bf16[2,2,256,768]{3,2,1,0:T(8,128)(2,1)} %copy-done.2, bf16[2,256,768]{2,1,0:T(8,128)(2,1)} %collective-permute-done.46.t2, bf16[2,256,768]{2,1,0:T(8,128)(2,1)} %tok.3, f32[2,256,768]{2,1,0:T(8,128)} %get-tuple-element.250.after, ...), custom_call_target="tpu_custom_call" | custom-call | flops 15728640 | bytes 4718592 | tf_op jit(solution)/shard_map/norm_back/pallas_call | solution.py:776
  305.9 2.9 collective-permute-done.49
  (250 shorter events, 54.5 us)
Async XLA Ops:
  7.2 42.9 %all-gather.2.cloned.1.call-start = ((), (), s32[]{:S(2)}) async-start(), calls=%async_computation.3 | async-start | bytes 3932160 | tf_op jit(solution)/shard_map/all_gather | solution.py:1053
  8.9 20.0 %collective-permute-start = (bf16[3,96,256]{2,1,0:T(8,128)(2,1)S(1)}, bf16[3,96,256]{2,1,0:T(8,128)(2,1)S(1)}, u32[]{:S(2)}, u32[]{:S(2)}) collective-permute-start(bf16[3,96,256]{2,1,0:T(8,128)(2,1)S(1)} %get-tuple-element.371), channel_id=1, source_target_pairs={{0,8},{1,9},{2,10},{3,11},{4,12},{5,13},{6,14},{7,15},{8,16},{9,17... | collective-permute-start | bytes 442376 | tf_op jit(solution)/shard_map/ppermute | solution.py:923
  11.9 17.0 %collective-permute-start.1 = (bf16[3,96,256]{2,1,0:T(8,128)(2,1)S(1)}, bf16[3,96,256]{2,1,0:T(8,128)(2,1)S(1)}, u32[]{:S(2)}, u32[]{:S(2)}) collective-permute-start(bf16[3,96,256]{2,1,0:T(8,128)(2,1)S(1)} %get-tuple-element.371), channel_id=1, source_target_pairs={{0,16},{1,17},{2,18},{3,19},{4,20},{5,21},{6,22},{7,23},{8,24},{9,... | collective-permute-start | bytes 442376 | tf_op jit(solution)/shard_map/ppermute | solution.py:923
  14.5 14.4 %collective-permute-start.2 = (bf16[3,96,256]{2,1,0:T(8,128)(2,1)S(1)}, bf16[3,96,256]{2,1,0:T(8,128)(2,1)S(1)}, u32[]{:S(2)}, u32[]{:S(2)}) collective-permute-start(bf16[3,96,256]{2,1,0:T(8,128)(2,1)S(1)} %get-tuple-element.371), channel_id=1, source_target_pairs={{0,24},{1,25},{2,26},{3,27},{4,28},{5,29},{6,30},{7,31},{8,0},{9,1... | collective-permute-start | bytes 442376 | tf_op jit(solution)/shard_map/ppermute | solution.py:923
  17.1 11.2 %all-to-all-start = ((s32[8,1,2]{2,1,0:T(1,128)}), s32[8,1,2]{2,1,0:T(1,128)S(1)}, u32[]{:S(2)}, u32[]{:S(2)}) async-start(s32[8,1,2]{2,1,0:T(1,128)} %broadcast_in_dim.78), calls=%async_computation | async-start | bytes 8192 | tf_op jit(solution)/shard_map/all_to_all | solution.py:1040
  29.0 17.2 %collective-permute-start.3 = (bf16[4,3,96,256]{3,2,1,0:T(8,128)(2,1)S(1)}, bf16[4,3,96,256]{3,2,1,0:T(8,128)(2,1)S(1)}, u32[]{:S(2)}, u32[]{:S(2)}) collective-permute-start(bf16[4,3,96,256]{3,2,1,0:T(8,128)(2,1)S(1)} %pad_maximum_fusion.1.w0), channel_id=1, source_target_pairs={{0,4},{1,5},{2,6},{3,7},{4,0},{5,1},{6,2},{7,3},{8,12},{9,13},{10,... | collective-permute-start | bytes 1769480 | tf_op jit(solution)/shard_map/ppermute | solution.py:923
  30.3 14.3 %all-to-all-start.1 = ((f32[8,1,1824]{2,1,0:T(1,128)}), f32[8,1,1824]{2,1,0:T(1,128)S(1)}, u32[]{:S(2)}, u32[]{:S(2)}) async-start(f32[8,1,1824]{2,1,0:T(1,128)} %all_to_all.16), calls=%async_computation.1 | async-start | bytes 122880 | tf_op jit(solution)/shard_map/all_to_all | solution.py:1068
  46.3 18.0 %collective-permute-start.4 = (bf16[96,1024]{1,0:T(8,128)(2,1)S(1)}, bf16[96,1024]{1,0:T(8,128)(2,1)S(1)}, u32[]{:S(2)}, u32[]{:S(2)}) collective-permute-start(bf16[96,1024]{1,0:T(8,128)(2,1)S(1)} %fusion.15), channel_id=1, source_target_pairs={{0,8},{1,9},{2,10},{3,11},{4,12},{5,13},{6,14},{7,15},{8,16},{9,17... | collective-permute-start | bytes 589832 | tf_op jit(solution)/shard_map/ppermute | solution.py:923
  46.9 17.4 %collective-permute-start.5 = (bf16[96,1024]{1,0:T(8,128)(2,1)S(1)}, bf16[96,1024]{1,0:T(8,128)(2,1)S(1)}, u32[]{:S(2)}, u32[]{:S(2)}) collective-permute-start(bf16[96,1024]{1,0:T(8,128)(2,1)S(1)} %fusion.15), channel_id=1, source_target_pairs={{0,16},{1,17},{2,18},{3,19},{4,20},{5,21},{6,22},{7,23},{8,24},{9,... | collective-permute-start | bytes 589832 | tf_op jit(solution)/shard_map/ppermute | solution.py:923
  47.4 16.9 %collective-permute-start.6 = (bf16[96,1024]{1,0:T(8,128)(2,1)S(1)}, bf16[96,1024]{1,0:T(8,128)(2,1)S(1)}, u32[]{:S(2)}, u32[]{:S(2)}) collective-permute-start(bf16[96,1024]{1,0:T(8,128)(2,1)S(1)} %fusion.15), channel_id=1, source_target_pairs={{0,24},{1,25},{2,26},{3,27},{4,28},{5,29},{6,30},{7,31},{8,0},{9,1... | collective-permute-start | bytes 589832 | tf_op jit(solution)/shard_map/ppermute | solution.py:923
  64.4 22.3 %collective-permute-start.7 = (bf16[4,96,1024]{2,1,0:T(8,128)(2,1)S(1)}, bf16[4,96,1024]{2,1,0:T(8,128)(2,1)S(1)}, u32[]{:S(2)}, u32[]{:S(2)}) collective-permute-start(bf16[4,96,1024]{2,1,0:T(8,128)(2,1)S(1)} %pad_maximum_fusion.rest_8_.rest_0_), channel_id=1, source_target_pairs={{0,4},{1,3},{2,6},{3,1},{4,0},{5,7},{6,2},{7,5},{8,12},{9,11},{10,... | collective-permute-start | bytes 2359304 | tf_op jit(solution)/shard_map/ppermute | solution.py:923
  65.1 21.6 %collective-permute-start.8 = (bf16[4,96,1024]{2,1,0:T(8,128)(2,1)S(1)}, bf16[4,96,1024]{2,1,0:T(8,128)(2,1)S(1)}, u32[]{:S(2)}, u32[]{:S(2)}) collective-permute-start(bf16[4,96,1024]{2,1,0:T(8,128)(2,1)S(1)} %pad_maximum_fusion.rest_8_.rest_0_), channel_id=1, source_target_pairs={{0,2},{1,5},{2,0},{3,7},{4,6},{5,1},{6,4},{7,3},{8,10},{9,13},{10,... | collective-permute-start | bytes 2359304 | tf_op jit(solution)/shard_map/ppermute | solution.py:923
  67.2 19.4 %collective-permute-start.10 = (bf16[96,768]{1,0:T(8,128)(2,1)S(1)}, bf16[96,768]{1,0:T(8,128)(2,1)S(1)}, u32[]{:S(2)}, u32[]{:S(2)}) collective-permute-start(bf16[96,768]{1,0:T(8,128)(2,1)S(1)} %bitcast.210), channel_id=1, source_target_pairs={{0,16},{1,17},{2,18},{3,19},{4,20},{5,21},{6,22},{7,23},{8,24},{9,... | collective-permute-start | bytes 442376 | tf_op jit(solution)/shard_map/ppermute | solution.py:923
  69.2 17.4 %collective-permute-start.11 = (bf16[96,768]{1,0:T(8,128)(2,1)S(1)}, bf16[96,768]{1,0:T(8,128)(2,1)S(1)}, u32[]{:S(2)}, u32[]{:S(2)}) collective-permute-start(bf16[96,768]{1,0:T(8,128)(2,1)S(1)} %bitcast.211), channel_id=1, source_target_pairs={{0,24},{1,25},{2,26},{3,27},{4,28},{5,29},{6,30},{7,31},{8,0},{9,1... | collective-permute-start | bytes 442376 | tf_op jit(solution)/shard_map/ppermute | solution.py:923
  72.2 14.4 %collective-permute-start.9 = (bf16[96,768]{1,0:T(8,128)(2,1)S(1)}, bf16[96,768]{1,0:T(8,128)(2,1)S(1)}, u32[]{:S(2)}, u32[]{:S(2)}) collective-permute-start(bf16[96,768]{1,0:T(8,128)(2,1)S(1)} %bitcast.212), channel_id=1, source_target_pairs={{0,8},{1,9},{2,10},{3,11},{4,12},{5,13},{6,14},{7,15},{8,16},{9,17... | collective-permute-start | bytes 442376 | tf_op jit(solution)/shard_map/ppermute | solution.py:923
  86.9 17.8 %collective-permute-start.15 = (bf16[4,96,1024]{2,1,0:T(8,128)(2,1)S(1)}, bf16[4,96,1024]{2,1,0:T(8,128)(2,1)S(1)}, u32[]{:S(2)}, u32[]{:S(2)}) collective-permute-start(bf16[4,96,1024]{2,1,0:T(8,128)(2,1)S(1)} %collective-permute-done.7.rest_9_.rest_1_), channel_id=1, source_target_pairs={{0,2},{1,5},{2,0},{3,7},{4,6},{5,1},{6,4},{7,3},{8,10},{9,13},{10,... | collective-permute-start | bytes 2359304 | tf_op jit(solution)/shard_map/ppermute | solution.py:923
  87.5 19.4 %collective-permute-start.20 = (bf16[4,96,1024]{2,1,0:T(8,128)(2,1)S(1)}, bf16[4,96,1024]{2,1,0:T(8,128)(2,1)}, u32[]{:S(2)}, u32[]{:S(2)}) collective-permute-start(bf16[4,96,1024]{2,1,0:T(8,128)(2,1)S(1)} %collective-permute-done.7.rest_9_.rest_1_), channel_id=1, source_target_pairs={{0,1},{1,0},{2,3},{3,2},{4,5},{5,4},{6,7},{7,6},{8,9},{9,8},{10,11... | collective-permute-start | bytes 2359304 | tf_op jit(solution)/shard_map/ppermute | solution.py:923
  88.0 16.5 %collective-permute-start.13 = (bf16[192,256]{1,0:T(8,128)(2,1)}, bf16[192,256]{1,0:T(8,128)(2,1)}, u32[]{:S(2)}, u32[]{:S(2)}) collective-permute-start(bf16[192,256]{1,0:T(8,128)(2,1)} %get-tuple-element.177), channel_id=1, source_target_pairs={{0,2},{1,3},{2,0},{3,1},{4,6},{5,7},{6,4},{7,5},{8,10},{9,11},{10,... | collective-permute-start | bytes 294920 | tf_op jit(solution)/shard_map/ppermute | solution.py:923
  89.5 15.2 %collective-permute-start.14 = (bf16[192,256]{1,0:T(8,128)(2,1)}, bf16[192,256]{1,0:T(8,128)(2,1)}, u32[]{:S(2)}, u32[]{:S(2)}) collective-permute-start(bf16[192,256]{1,0:T(8,128)(2,1)} %get-tuple-element.178), channel_id=1, source_target_pairs={{0,3},{1,2},{2,1},{3,0},{4,7},{5,6},{6,5},{7,4},{8,11},{9,10},{10,... | collective-permute-start | bytes 294920 | tf_op jit(solution)/shard_map/ppermute | solution.py:923
  89.5 15.9 %collective-permute-start.19 = (bf16[4,96,1024]{2,1,0:T(8,128)(2,1)S(1)}, bf16[4,96,1024]{2,1,0:T(8,128)(2,1)}, u32[]{:S(2)}, u32[]{:S(2)}) collective-permute-start(bf16[4,96,1024]{2,1,0:T(8,128)(2,1)S(1)} %pad_maximum_fusion.rest_8_.rest_0_), channel_id=1, source_target_pairs={{0,1},{1,0},{2,3},{3,2},{4,5},{5,4},{6,7},{7,6},{8,9},{9,8},{10,11... | collective-permute-start | bytes 2359304 | tf_op jit(solution)/shard_map/ppermute | solution.py:923
  104.6 7.8 %collective-permute-start.22 = (bf16[4,96,1024]{2,1,0:T(8,128)(2,1)S(1)}, bf16[4,96,1024]{2,1,0:T(8,128)(2,1)}, u32[]{:S(2)}, u32[]{:S(2)}) collective-permute-start(bf16[4,96,1024]{2,1,0:T(8,128)(2,1)S(1)} %collective-permute-done.15.rest_11_.rest_3_), channel_id=1, source_target_pairs={{0,1},{1,0},{2,3},{3,2},{4,5},{5,4},{6,7},{7,6},{8,9},{9,8},{10,11... | collective-permute-start | bytes 2359304 | tf_op jit(solution)/shard_map/ppermute | solution.py:923
  113.6 18.8 %collective-permute-start.23 = (bf16[4,96,768]{2,1,0:T(8,128)(2,1)S(1)}, bf16[4,96,768]{2,1,0:T(8,128)(2,1)S(1)}, u32[]{:S(2)}, u32[]{:S(2)}) collective-permute-start(bf16[4,96,768]{2,1,0:T(8,128)(2,1)S(1)} %pad_maximum_fusion.2.rest_0_), channel_id=1, source_target_pairs={{0,4},{1,3},{2,6},{3,1},{4,0},{5,7},{6,2},{7,5},{8,12},{9,11},{10,... | collective-permute-start | bytes 1769480 | tf_op jit(solution)/shard_map/ppermute | solution.py:923
  114.5 17.9 %collective-permute-start.24 = (bf16[4,96,768]{2,1,0:T(8,128)(2,1)S(1)}, bf16[4,96,768]{2,1,0:T(8,128)(2,1)S(1)}, u32[]{:S(2)}, u32[]{:S(2)}) collective-permute-start(bf16[4,96,768]{2,1,0:T(8,128)(2,1)S(1)} %pad_maximum_fusion.2.rest_0_), channel_id=1, source_target_pairs={{0,2},{1,5},{2,0},{3,7},{4,6},{5,1},{6,4},{7,3},{8,10},{9,13},{10,... | collective-permute-start | bytes 1769480 | tf_op jit(solution)/shard_map/ppermute | solution.py:923
  118.0 23.9 %collective-permute-start.26 = (bf16[4,96,768]{2,1,0:T(8,128)(2,1)S(1)}, bf16[4,96,768]{2,1,0:T(8,128)(2,1)}, u32[]{:S(2)}, u32[]{:S(2)}) collective-permute-start(bf16[4,96,768]{2,1,0:T(8,128)(2,1)S(1)} %pad_maximum_fusion.2.rest_0_), channel_id=1, source_target_pairs={{0,1},{1,0},{2,3},{3,2},{4,5},{5,4},{6,7},{7,6},{8,9},{9,8},{10,11... | collective-permute-start | bytes 1769480 | tf_op jit(solution)/shard_map/ppermute | solution.py:923
  132.4 9.9 %collective-permute-start.25 = (bf16[4,96,768]{2,1,0:T(8,128)(2,1)S(1)}, bf16[4,96,768]{2,1,0:T(8,128)(2,1)S(1)}, u32[]{:S(2)}, u32[]{:S(2)}) collective-permute-start(bf16[4,96,768]{2,1,0:T(8,128)(2,1)S(1)} %collective-permute-done.23.rest_1_), channel_id=1, source_target_pairs={{0,2},{1,5},{2,0},{3,7},{4,6},{5,1},{6,4},{7,3},{8,10},{9,13},{10,... | collective-permute-start | bytes 1769480 | tf_op jit(solution)/shard_map/ppermute | solution.py:923
  133.0 9.3 %collective-permute-start.27 = (bf16[4,96,768]{2,1,0:T(8,128)(2,1)S(1)}, bf16[4,96,768]{2,1,0:T(8,128)(2,1)S(1)}, u32[]{:S(2)}, u32[]{:S(2)}) collective-permute-start(bf16[4,96,768]{2,1,0:T(8,128)(2,1)S(1)} %collective-permute-done.23.rest_1_), channel_id=1, source_target_pairs={{0,1},{1,0},{2,3},{3,2},{4,5},{5,4},{6,7},{7,6},{8,9},{9,8},{10,11... | collective-permute-start | bytes 1769480 | tf_op jit(solution)/shard_map/ppermute | solution.py:923
  133.8 8.5 %collective-permute-start.28 = (bf16[4,96,768]{2,1,0:T(8,128)(2,1)S(1)}, bf16[4,96,768]{2,1,0:T(8,128)(2,1)}, u32[]{:S(2)}, u32[]{:S(2)}) collective-permute-start(bf16[4,96,768]{2,1,0:T(8,128)(2,1)S(1)} %collective-permute-done.24.rest_2_), channel_id=1, source_target_pairs={{0,1},{1,0},{2,3},{3,2},{4,5},{5,4},{6,7},{7,6},{8,9},{9,8},{10,11... | collective-permute-start | bytes 1769480 | tf_op jit(solution)/shard_map/ppermute | solution.py:923
  143.4 17.5 %collective-permute-start.30 = (bf16[16,96,768]{2,1,0:T(8,128)(2,1)}, bf16[16,96,768]{2,1,0:T(8,128)(2,1)S(1)}, u32[]{:S(2)}, u32[]{:S(2)}) collective-permute-start(bf16[16,96,768]{2,1,0:T(8,128)(2,1)} %get-tuple-element.242), channel_id=1, source_target_pairs={{0,1},{1,0},{2,3},{3,2},{4,5},{5,4},{6,7},{7,6},{8,9},{9,8},{10,11... | collective-permute-start | bytes 7077896 | tf_op jit(solution)/shard_map/ppermute | solution.py:923
  164.3 16.5 %collective-permute-start.31 = (bf16[2,4,96,768]{3,2,1,0:T(8,128)(2,1)}, bf16[2,4,96,768]{3,2,1,0:T(8,128)(2,1)}, u32[]{:S(2)}, u32[]{:S(2)}) collective-permute-start(bf16[2,4,96,768]{3,2,1,0:T(8,128)(2,1)} %fusion.1), channel_id=1, source_target_pairs={{0,2},{1,5},{2,0},{3,7},{4,6},{5,1},{6,4},{7,3},{8,10},{9,13},{10,... | collective-permute-start | bytes 3538952 | tf_op jit(solution)/shard_map/ppermute | solution.py:923
  183.1 12.6 %collective-permute-start.35 = (bf16[4,96,768]{2,1,0:T(8,128)(2,1)}, bf16[4,96,768]{2,1,0:T(8,128)(2,1)S(1)}, u32[]{:S(2)}, u32[]{:S(2)}) collective-permute-start(bf16[4,96,768]{2,1,0:T(8,128)(2,1)} %fusion.3), channel_id=1, source_target_pairs={{0,4},{1,3},{2,6},{3,1},{4,0},{5,7},{6,2},{7,5},{8,12},{9,11},{10,... | collective-permute-start | bytes 1769480 | tf_op jit(solution)/shard_map/ppermute | solution.py:923
  184.3 11.4 %collective-permute-start.32 = (bf16[192,512]{1,0:T(8,128)(2,1)}, bf16[192,512]{1,0:T(8,128)(2,1)S(1)}, u32[]{:S(2)}, u32[]{:S(2)}) collective-permute-start(bf16[192,512]{1,0:T(8,128)(2,1)} %get-tuple-element.253), channel_id=1, source_target_pairs={{0,1},{1,0},{2,3},{3,2},{4,5},{5,4},{6,7},{7,6},{8,9},{9,8},{10,11... | collective-permute-start | bytes 589832 | tf_op jit(solution)/shard_map/ppermute | solution.py:923
  184.3 11.4 %collective-permute-start.33 = (bf16[192,512]{1,0:T(8,128)(2,1)}, bf16[192,512]{1,0:T(8,128)(2,1)S(1)}, u32[]{:S(2)}, u32[]{:S(2)}) collective-permute-start(bf16[192,512]{1,0:T(8,128)(2,1)} %get-tuple-element.254), channel_id=1, source_target_pairs={{0,2},{1,3},{2,0},{3,1},{4,6},{5,7},{6,4},{7,5},{8,10},{9,11},{10,... | collective-permute-start | bytes 589832 | tf_op jit(solution)/shard_map/ppermute | solution.py:923
  185.1 15.0 %collective-permute-start.34 = (bf16[192,512]{1,0:T(8,128)(2,1)S(1)}, bf16[192,512]{1,0:T(8,128)(2,1)S(1)}, u32[]{:S(2)}, u32[]{:S(2)}) collective-permute-start(bf16[192,512]{1,0:T(8,128)(2,1)S(1)} %copy-done.46), channel_id=1, source_target_pairs={{0,3},{1,2},{2,1},{3,0},{4,7},{5,6},{6,5},{7,4},{8,11},{9,10},{10,... | collective-permute-start | bytes 589832 | tf_op jit(solution)/shard_map/ppermute | solution.py:923
  208.6 20.7 %collective-permute-start.37 = (bf16[2,4,96,1024]{3,2,1,0:T(8,128)(2,1)}, bf16[2,4,96,1024]{3,2,1,0:T(8,128)(2,1)}, u32[]{:S(2)}, u32[]{:S(2)}) collective-permute-start(bf16[2,4,96,1024]{3,2,1,0:T(8,128)(2,1)} %fusion), channel_id=1, source_target_pairs={{0,2},{1,5},{2,0},{3,7},{4,6},{5,1},{6,4},{7,3},{8,10},{9,13},{10,... | collective-permute-start | bytes 4718600 | tf_op jit(solution)/shard_map/ppermute | solution.py:923
  210.6 17.2 %collective-permute-start.38 = (bf16[96,768]{1,0:T(8,128)(2,1)}, bf16[96,768]{1,0:T(8,128)(2,1)S(1)}, u32[]{:S(2)}, u32[]{:S(2)}) collective-permute-start(bf16[96,768]{1,0:T(8,128)(2,1)} %get-tuple-element.364), channel_id=1, source_target_pairs={{0,8},{1,9},{2,10},{3,11},{4,12},{5,13},{6,14},{7,15},{8,16},{9,17... | collective-permute-start | bytes 442376 | tf_op jit(solution)/shard_map/ppermute | solution.py:923
  211.2 16.6 %collective-permute-start.39 = (bf16[96,768]{1,0:T(8,128)(2,1)}, bf16[96,768]{1,0:T(8,128)(2,1)S(1)}, u32[]{:S(2)}, u32[]{:S(2)}) collective-permute-start(bf16[96,768]{1,0:T(8,128)(2,1)} %get-tuple-element.363), channel_id=1, source_target_pairs={{0,16},{1,17},{2,18},{3,19},{4,20},{5,21},{6,22},{7,23},{8,24},{9,... | collective-permute-start | bytes 442376 | tf_op jit(solution)/shard_map/ppermute | solution.py:923
  214.9 12.9 %collective-permute-start.40 = (bf16[96,768]{1,0:T(8,128)(2,1)S(1)}, bf16[96,768]{1,0:T(8,128)(2,1)S(1)}, u32[]{:S(2)}, u32[]{:S(2)}) collective-permute-start(bf16[96,768]{1,0:T(8,128)(2,1)S(1)} %get-tuple-element.362), channel_id=1, source_target_pairs={{0,24},{1,25},{2,26},{3,27},{4,28},{5,29},{6,30},{7,31},{8,0},{9,1... | collective-permute-start | bytes 442376 | tf_op jit(solution)/shard_map/ppermute | solution.py:923
  231.1 14.5 %collective-permute-start.41 = (bf16[4,96,1024]{2,1,0:T(8,128)(2,1)S(1)}, bf16[4,96,1024]{2,1,0:T(8,128)(2,1)}, u32[]{:S(2)}, u32[]{:S(2)}) collective-permute-start(bf16[4,96,1024]{2,1,0:T(8,128)(2,1)S(1)} %fusion.2), channel_id=1, source_target_pairs={{0,4},{1,3},{2,6},{3,1},{4,0},{5,7},{6,2},{7,5},{8,12},{9,11},{10,... | collective-permute-start | bytes 2359304 | tf_op jit(solution)/shard_map/ppermute | solution.py:923
  248.6 17.9 %collective-permute-start.42 = (bf16[96,1024]{1,0:T(8,128)(2,1)}, bf16[96,1024]{1,0:T(8,128)(2,1)S(1)}, u32[]{:S(2)}, u32[]{:S(2)}) collective-permute-start(bf16[96,1024]{1,0:T(8,128)(2,1)} %get-tuple-element.360), channel_id=1, source_target_pairs={{0,8},{1,9},{2,10},{3,11},{4,12},{5,13},{6,14},{7,15},{8,16},{9,17... | collective-permute-start | bytes 589832 | tf_op jit(solution)/shard_map/ppermute | solution.py:923
  250.6 16.0 %collective-permute-start.43 = (bf16[96,1024]{1,0:T(8,128)(2,1)}, bf16[96,1024]{1,0:T(8,128)(2,1)S(1)}, u32[]{:S(2)}, u32[]{:S(2)}) collective-permute-start(bf16[96,1024]{1,0:T(8,128)(2,1)} %get-tuple-element.359), channel_id=1, source_target_pairs={{0,16},{1,17},{2,18},{3,19},{4,20},{5,21},{6,22},{7,23},{8,24},{9,... | collective-permute-start | bytes 589832 | tf_op jit(solution)/shard_map/ppermute | solution.py:923
  252.9 13.6 %collective-permute-start.44 = (bf16[96,1024]{1,0:T(8,128)(2,1)}, bf16[96,1024]{1,0:T(8,128)(2,1)S(1)}, u32[]{:S(2)}, u32[]{:S(2)}) collective-permute-start(bf16[96,1024]{1,0:T(8,128)(2,1)} %get-tuple-element.358), channel_id=1, source_target_pairs={{0,24},{1,25},{2,26},{3,27},{4,28},{5,29},{6,30},{7,31},{8,0},{9,1... | collective-permute-start | bytes 589832 | tf_op jit(solution)/shard_map/ppermute | solution.py:923
  267.2 8.4 %collective-permute-start.45 = (bf16[2,2,256,768]{3,2,1,0:T(8,128)(2,1)}, bf16[2,2,256,768]{3,2,1,0:T(8,128)(2,1)S(1)}, u32[]{:S(2)}, u32[]{:S(2)}) collective-permute-start(bf16[2,2,256,768]{3,2,1,0:T(8,128)(2,1)} %get-tuple-element.286), channel_id=1, source_target_pairs={{0,1},{1,0},{2,3},{3,2},{4,5},{5,4},{6,7},{7,6},{8,9},{9,8},{10,11... | collective-permute-start | bytes 4718600 | tf_op jit(solution)/shard_map/ppermute | solution.py:923
  269.1 17.9 %all-to-all-start.2 = ((f32[32,3,768]{2,1,0:T(4,128)}), f32[32,3,768]{2,1,0:T(4,128)S(1)}, u32[]{:S(2)}, u32[]{:S(2)}) async-start(f32[32,3,768]{2,1,0:T(4,128)} %bitcast.196), calls=%async_computation.2 | async-start | bytes 786432 | tf_op jit(solution)/shard_map/all_to_all | solution.py:1250
  273.8 19.8 %collective-permute-start.47 = (bf16[4,3,96,256]{3,2,1,0:T(8,128)(2,1)}, bf16[4,3,96,256]{3,2,1,0:T(8,128)(2,1)}, u32[]{:S(2)}, u32[]{:S(2)}) collective-permute-start(bf16[4,3,96,256]{3,2,1,0:T(8,128)(2,1)} %get-tuple-element.288), channel_id=1, source_target_pairs={{0,4},{1,5},{2,6},{3,7},{4,0},{5,1},{6,2},{7,3},{8,12},{9,13},{10,... | collective-permute-start | bytes 1769480 | tf_op jit(solution)/shard_map/ppermute | solution.py:923
  277.5 23.0 %collective-permute-start.46 = (bf16[2,256,768]{2,1,0:T(8,128)(2,1)S(1)}, bf16[2,256,768]{2,1,0:T(8,128)(2,1)}, u32[]{:S(2)}, u32[]{:S(2)}) collective-permute-start(bf16[2,256,768]{2,1,0:T(8,128)(2,1)S(1)} %fusion.4), channel_id=1, source_target_pairs={{0,2},{1,3},{2,0},{3,1},{4,6},{5,7},{6,4},{7,5},{8,10},{9,11},{10,... | collective-permute-start | bytes 2359304 | tf_op jit(solution)/shard_map/ppermute | solution.py:923
  295.1 10.8 %collective-permute-start.48 = (bf16[3,96,256]{2,1,0:T(8,128)(2,1)S(1)}, bf16[3,96,256]{2,1,0:T(8,128)(2,1)S(1)}, u32[]{:S(2)}, u32[]{:S(2)}) collective-permute-start(bf16[3,96,256]{2,1,0:T(8,128)(2,1)S(1)} %get-tuple-element.368), channel_id=1, source_target_pairs={{0,8},{1,9},{2,10},{3,11},{4,12},{5,13},{6,14},{7,15},{8,16},{9,17... | collective-permute-start | bytes 442376 | tf_op jit(solution)/shard_map/ppermute | solution.py:923
  296.8 12.0 %collective-permute-start.49 = (bf16[3,96,256]{2,1,0:T(8,128)(2,1)S(1)}, bf16[3,96,256]{2,1,0:T(8,128)(2,1)S(1)}, u32[]{:S(2)}, u32[]{:S(2)}) collective-permute-start(bf16[3,96,256]{2,1,0:T(8,128)(2,1)S(1)} %get-tuple-element.367), channel_id=1, source_target_pairs={{0,16},{1,17},{2,18},{3,19},{4,20},{5,21},{6,22},{7,23},{8,24},{9,... | collective-permute-start | bytes 442376 | tf_op jit(solution)/shard_map/ppermute | solution.py:923
  299.0 9.7 %collective-permute-start.50 = (bf16[3,96,256]{2,1,0:T(8,128)(2,1)S(1)}, bf16[3,96,256]{2,1,0:T(8,128)(2,1)S(1)}, u32[]{:S(2)}, u32[]{:S(2)}) collective-permute-start(bf16[3,96,256]{2,1,0:T(8,128)(2,1)S(1)} %get-tuple-element.366), channel_id=1, source_target_pairs={{0,24},{1,25},{2,26},{3,27},{4,28},{5,29},{6,30},{7,31},{8,0},{9,1... | collective-permute-start | bytes 442376 | tf_op jit(solution)/shard_map/ppermute | solution.py:923
  (58 other events, 553.0 us)
Sparse Core Ops, SparseCore 0:
  9.6 31.2 all-gather.1
